TPU v7x, 32 devices: a whole 2x2x4 slice. The times are simulated.
32 devices in a mesh: dp: 8 (over z, x), tensor: 4 (over y, core).
Axes of the slice: x: 2, y: 2, z: 4, core: 2. Of those that a mesh axis runs over, the one named last changes fastest.
Arguments:
- tokens: bfloat16 [16384, 768], P(('dp', 'tensor')), may hold values from -6 to 6
- seq_lengths: int32 [8, 3], P('dp'), may hold values from 0 to 2048, as said below
- norm1_gain: float32 [768], replicated, may hold values from 0.1 to 1.9
- norm1_shift: float32 [768], replicated, may hold values from -2 to 2
- qkv_weight: bfloat16 [768, 3, 768], P('dp', None, 'tensor'), may hold values from -0.21875 to 0.21875
- qv_bias: float32 [2, 768], replicated, may hold values from -3 to 3
- out_weight: bfloat16 [768, 768], P('tensor', 'dp'), may hold values from -0.875 to 0.875
- out_bias: float32 [768], replicated, may hold values from -2 to 2
- norm2_gain: float32 [768], replicated, may hold values from 0.1 to 1.9
- norm2_shift: float32 [768], replicated, may hold values from -2 to 2
- fc_weight: bfloat16 [768, 3072], P('dp', 'tensor'), may hold values from -0.21875 to 0.21875
- fc_bias: float32 [3072], replicated, may hold values from -3 to 3
- proj_weight: bfloat16 [3072, 768], P('tensor', 'dp'), may hold values from -0.109375 to 0.109375
- proj_bias: float32 [768], replicated, may hold values from -2 to 2
- out_grad: bfloat16 [16384, 768], P(('dp', 'tensor')), may hold values from -6 to 6
Outputs:
- block_out: bfloat16 [16384, 768], P(('dp', 'tensor'))
- grad_tokens: bfloat16 [16384, 768], P(('dp', 'tensor'))
- grad_norm1_gain: float32 [768], replicated
- grad_norm1_shift: float32 [768], replicated
- grad_qkv_weight: float32 [768, 3, 768], P('dp', None, 'tensor')
- grad_qv_bias: float32 [2, 768], replicated
- grad_out_weight: float32 [768, 768], P('tensor', 'dp')
- grad_out_bias: float32 [768], replicated
- grad_norm2_gain: float32 [768], replicated
- grad_norm2_shift: float32 [768], replicated
- grad_fc_weight: float32 [768, 3072], P('dp', 'tensor')
- grad_fc_bias: float32 [3072], replicated
- grad_proj_weight: float32 [3072, 768], P('tensor', 'dp')
- grad_proj_bias: float32 [768], replicated
Inputs may be any that keep to these rules, and one draw needn't show every extreme that they name: `seq_lengths`: A group holds one to three sequences; its nonzero lengths fill the first slots; each is at least 512; rounded up to multiples of 128 they sum to at most 2048; some group holds a single sequence of exactly 2048.
All inputs are finite; a program needn't handle non-finite values.
Results may differ from a plain program's by a relative error of at most 0.015.
Values may be sent and summed in bfloat16 or wider, within the bound.
No kernel may reach another device: no remote copies, remote signals or barrier semaphores. Data moves between devices by JAX's collectives and lax.ppermute only.
A program may use at most 192 MiB of HBM per device.

v0:
```python
import jax
import jax.numpy as jnp
from jax import lax
from jax.sharding import PartitionSpec as P

HS = 64
BLK = 128
QB = 512


EPSILON = 1e-05
MASKED = -1e30
GELU_SCALE = 0.7978845608028654


def layer_norm(values, norm_gain, norm_shift):
    centre = values - jnp.mean(values, axis=-1, keepdims=True)
    spread = jnp.mean(centre * centre, axis=-1, keepdims=True)
    return centre * lax.rsqrt(spread + EPSILON) * norm_gain + norm_shift


def gelu_tanh(values):
    return (
        0.5 * values * (1.0 + jnp.tanh(GELU_SCALE * (values + 0.044715 * values * values * values)))
    )


def segment_ids(lengths, capacity):
    padded = (lengths + BLK - 1) // BLK * BLK
    starts = jnp.cumsum(padded, axis=1) - padded
    places = jnp.arange(capacity, dtype=jnp.int32)
    inside = (places[None, None, :] >= starts[:, :, None]) & (
        places[None, None, :] < (starts + lengths)[:, :, None]
    )
    labels = jnp.arange(lengths.shape[1], dtype=jnp.int32)[None, :, None] + 1
    return jnp.sum(jnp.where(inside, labels, 0), axis=1) - 1


def block_scores(queries, key_rows, seg_query, seg_key, place_query, place_key):
    raw_scores = jnp.einsum(
        "qhd,khd->hqk", queries, key_rows, preferred_element_type=jnp.float32
    ) * HS ** (-0.5)
    allowed = (
        (seg_query[:, None] == seg_key[None, :])
        & (place_key[None, :] <= place_query[:, None])
        & (seg_query[:, None] >= 0)
    )
    return jnp.where(allowed[None], raw_scores, MASKED)


def per_device(
    tokens,
    seq_lengths,
    norm1_gain,
    norm1_shift,
    qkv_weight,
    qv_bias,
    out_weight,
    out_bias,
    norm2_gain,
    norm2_shift,
    fc_weight,
    fc_bias,
    proj_weight,
    proj_bias,
    out_grad,
):
    tensor_size = lax.axis_size("tensor")
    tensor_pos = lax.axis_index("tensor")
    local_rows = tokens.shape[0]
    capacity = local_rows * tensor_size
    model_width = tokens.shape[1]
    head_cols = qkv_weight.shape[2]
    hidden_cols = fc_weight.shape[1]
    scale = HS ** (-0.5)
    block_count = capacity // QB
    full_qkv, out_rows, fc_cols, proj_rows = (
        lax.all_gather(qkv_weight, "dp", axis=0, tiled=True),
        lax.all_gather(out_weight, "dp", axis=1, tiled=True),
        lax.all_gather(fc_weight, "dp", axis=0, tiled=True),
        lax.all_gather(proj_weight, "dp", axis=1, tiled=True),
    )
    seg = segment_ids(seq_lengths, capacity)[0]
    places = jnp.arange(capacity, dtype=jnp.int32)
    live_here = lax.dynamic_slice_in_dim(seg, tensor_pos * local_rows, local_rows, 0) >= 0
    stream = tokens.astype(jnp.float32)
    first_norm, first_back = jax.vjp(layer_norm, stream, norm1_gain, norm1_shift)
    first_all = lax.all_gather(first_norm.astype(jnp.bfloat16), "tensor", axis=0, tiled=True)
    projected = jnp.dot(
        first_all, full_qkv.reshape(model_width, 3 * head_cols), preferred_element_type=jnp.float32
    ).reshape(capacity, 3, head_cols)
    bias_here = lax.dynamic_slice_in_dim(qv_bias, tensor_pos * head_cols, head_cols, 1)
    queries = (projected[:, 0] + bias_here[0]).astype(jnp.bfloat16).reshape(capacity, -1, HS)
    key_rows = projected[:, 1].astype(jnp.bfloat16).reshape(capacity, -1, HS)
    values = (projected[:, 2] + bias_here[1]).astype(jnp.bfloat16).reshape(capacity, -1, HS)
    outputs = []
    log_totals = []
    for block_index in range(block_count):
        block_begin = block_index * QB
        block_end = block_begin + QB
        scores = block_scores(
            queries[block_begin:block_end],
            key_rows[:block_end],
            seg[block_begin:block_end],
            seg[:block_end],
            places[block_begin:block_end],
            places[:block_end],
        )
        row_peak = jnp.max(scores, axis=-1, keepdims=True)
        weights = jnp.exp(scores - row_peak)
        row_total = jnp.sum(weights, axis=-1, keepdims=True)
        probability = (weights / row_total).astype(jnp.bfloat16)
        outputs.append(
            jnp.einsum(
                "hqk,khd->qhd", probability, values[:block_end], preferred_element_type=jnp.float32
            )
        )
        log_totals.append(row_peak + jnp.log(row_total))
    attended = jnp.concatenate(outputs, 0).reshape(capacity, head_cols).astype(jnp.bfloat16)
    log_total = jnp.concatenate(log_totals, 1)
    branch = lax.psum_scatter(
        jnp.dot(attended, out_rows, preferred_element_type=jnp.float32),
        "tensor",
        scatter_dimension=0,
        tiled=True,
    )
    middle = stream + branch + out_bias
    second_norm, second_back = jax.vjp(layer_norm, middle, norm2_gain, norm2_shift)
    second_all = lax.all_gather(second_norm.astype(jnp.bfloat16), "tensor", axis=0, tiled=True)
    fc_bias_here = lax.dynamic_slice_in_dim(fc_bias, tensor_pos * hidden_cols, hidden_cols, 0)
    pre_gelu = jnp.dot(second_all, fc_cols, preferred_element_type=jnp.float32) + fc_bias_here
    activated_f, gelu_back = jax.vjp(gelu_tanh, pre_gelu)
    activated = activated_f.astype(jnp.bfloat16)
    mlp_out = lax.psum_scatter(
        jnp.dot(activated, proj_rows, preferred_element_type=jnp.float32).astype(jnp.bfloat16),
        "tensor",
        scatter_dimension=0,
        tiled=True,
    ).astype(jnp.float32)
    result = jnp.where(live_here[:, None], middle + mlp_out + proj_bias, 0.0).astype(jnp.bfloat16)
    full_qkv, out_rows, fc_cols, proj_rows = (
        lax.all_gather(qkv_weight, "dp", axis=0, tiled=True),
        lax.all_gather(out_weight, "dp", axis=1, tiled=True),
        lax.all_gather(fc_weight, "dp", axis=0, tiled=True),
        lax.all_gather(proj_weight, "dp", axis=1, tiled=True),
    )
    grad_mlp = jnp.where(live_here[:, None], out_grad, jnp.zeros_like(out_grad))
    grad_all = lax.all_gather(grad_mlp, "tensor", axis=0, tiled=True)
    grad_here = grad_mlp.astype(jnp.float32)
    grad_proj = jnp.einsum("tf,td->fd", activated, grad_all, preferred_element_type=jnp.float32)
    grad_act = jnp.einsum("td,fd->tf", grad_all, proj_rows, preferred_element_type=jnp.float32)
    grad_pre = gelu_back(grad_act)[0].astype(jnp.bfloat16)
    grad_fc = jnp.einsum("td,tf->df", second_all, grad_pre, preferred_element_type=jnp.float32)
    grad_fc_cols = jnp.sum(grad_pre.astype(jnp.float32), axis=0)
    grad_second = lax.psum_scatter(
        jnp.einsum("tf,df->td", grad_pre, fc_cols, preferred_element_type=jnp.float32).astype(
            jnp.bfloat16
        ),
        "tensor",
        scatter_dimension=0,
        tiled=True,
    ).astype(jnp.float32)
    middle_part, grad_gain_two, grad_shift_two = second_back(grad_second)
    grad_middle = grad_here + middle_part
    grad_branch = grad_middle.astype(jnp.bfloat16)
    branch_all = lax.all_gather(grad_branch, "tensor", axis=0, tiled=True)
    grad_out = jnp.einsum("tc,td->cd", attended, branch_all, preferred_element_type=jnp.float32)
    grad_attended = (
        jnp.einsum("td,cd->tc", branch_all, out_rows, preferred_element_type=jnp.float32)
        .astype(jnp.bfloat16)
        .reshape(capacity, -1, HS)
    )
    query_grads = []
    grad_keys = jnp.zeros(key_rows.shape, jnp.float32)
    grad_values = jnp.zeros(values.shape, jnp.float32)
    for block_index in range(block_count):
        block_begin = block_index * QB
        block_end = block_begin + QB
        query_block = queries[block_begin:block_end]
        attended_grad_block = grad_attended[block_begin:block_end]
        scores = block_scores(
            query_block,
            key_rows[:block_end],
            seg[block_begin:block_end],
            seg[:block_end],
            places[block_begin:block_end],
            places[:block_end],
        )
        probability = jnp.exp(scores - log_total[:, block_begin:block_end])
        grad_probs = jnp.einsum(
            "qhd,khd->hqk",
            attended_grad_block,
            values[:block_end],
            preferred_element_type=jnp.float32,
        )
        centre = jnp.sum(grad_probs * probability, axis=-1, keepdims=True)
        grad_scores = (probability * (grad_probs - centre)).astype(jnp.bfloat16)
        query_grads.append(
            jnp.einsum(
                "hqk,khd->qhd",
                grad_scores,
                key_rows[:block_end],
                preferred_element_type=jnp.float32,
            )
            * scale
        )
        grad_keys = grad_keys.at[:block_end].add(
            jnp.einsum("hqk,qhd->khd", grad_scores, query_block, preferred_element_type=jnp.float32)
            * scale
        )
        grad_values = grad_values.at[:block_end].add(
            jnp.einsum(
                "hqk,qhd->khd",
                probability.astype(jnp.bfloat16),
                attended_grad_block,
                preferred_element_type=jnp.float32,
            )
        )
    grad_queries = jnp.concatenate(query_grads, 0)
    grad_qkv = (
        jnp.stack([grad_queries, grad_keys, grad_values], 1)
        .reshape(capacity, 3, head_cols)
        .astype(jnp.bfloat16)
    )
    grad_qkv_w = jnp.einsum("td,tcf->dcf", first_all, grad_qkv, preferred_element_type=jnp.float32)
    grad_bias_cols = jnp.sum(grad_qkv[:, 0::2].astype(jnp.float32), axis=0)
    flat_qkv = full_qkv.reshape(model_width, 3 * head_cols)
    grad_slice = grad_qkv.reshape(local_rows * lax.axis_size("tensor"), 3 * head_cols)
    grad_first = lax.psum_scatter(
        jnp.einsum("tc,dc->td", grad_slice, flat_qkv, preferred_element_type=jnp.float32).astype(
            jnp.bfloat16
        ),
        "tensor",
        scatter_dimension=0,
        tiled=True,
    ).astype(jnp.float32)
    input_part, grad_gain_one, grad_shift_one = first_back(grad_first)
    grad_tokens = (grad_middle + input_part).astype(jnp.bfloat16)
    sum_qkv, sum_out, sum_fc, sum_proj = (
        lax.psum_scatter(grad_qkv_w, "dp", scatter_dimension=0, tiled=True),
        lax.psum_scatter(grad_out, "dp", scatter_dimension=1, tiled=True),
        lax.psum_scatter(grad_fc, "dp", scatter_dimension=0, tiled=True),
        lax.psum_scatter(grad_proj, "dp", scatter_dimension=1, tiled=True),
    )
    qv_full = lax.dynamic_update_slice_in_dim(
        jnp.zeros((2, model_width), jnp.float32), grad_bias_cols, tensor_pos * head_cols, 1
    )
    fc_full = lax.dynamic_update_slice_in_dim(
        jnp.zeros(fc_bias.shape, jnp.float32), grad_fc_cols, tensor_pos * hidden_cols, 0
    )
    out_bias_part = jnp.sum(grad_branch.astype(jnp.float32), axis=0)
    proj_bias_part = jnp.sum(grad_here, axis=0)
    small_sums = lax.psum(
        (
            grad_gain_one,
            grad_shift_one,
            qv_full,
            out_bias_part,
            grad_gain_two,
            grad_shift_two,
            fc_full,
            proj_bias_part,
        ),
        ("dp", "tensor"),
    )
    return (
        result,
        grad_tokens,
        small_sums[0],
        small_sums[1],
        sum_qkv,
        small_sums[2],
        sum_out,
        small_sums[3],
        small_sums[4],
        small_sums[5],
        sum_fc,
        small_sums[6],
        sum_proj,
        small_sums[7],
    )


def solution(mesh):
    placed = (
        P(("dp", "tensor"), None),
        P("dp", None),
        P(),
        P(),
        P("dp", None, "tensor"),
        P(),
        P("tensor", "dp"),
        P(),
        P(),
        P(),
        P("dp", "tensor"),
        P(),
        P("tensor", "dp"),
        P(),
        P(("dp", "tensor"), None),
    )
    return jax.shard_map(
        per_device,
        mesh=mesh,
        in_specs=placed,
        out_specs=(
            P(("dp", "tensor"), None),
            P(("dp", "tensor"), None),
            P(),
            P(),
            P("dp", None, "tensor"),
            P(),
            P("tensor", "dp"),
            P(),
            P(),
            P(),
            P("dp", "tensor"),
            P(),
            P("tensor", "dp"),
            P(),
        ),
        check_vma=False,
    )
```

profile of v0, /device:TPU:0, one launch (start us, length us, event | category | flops | bytes accessed | tf_op | source)
XLA Modules:
  0.0 771.4 jit_solution(4972562643246310161)
XLA Ops:
  17.8 35.5 %all_gather.29 = bf16[768,3,192]{2,0,1:T(8,128)(2,1)S(1)} all-gather(bf16[96,3,192]{2,0,1:T(8,128)(2,1)S(1)} %copy-done.57), channel_id=1, replica_groups=mesh['dp'=8,'tensor'=4] {'dp'}, dimensions={0}, use_global_device_ids=true | all-gather | bytes 995328 | tf_op jit(solution)/shard_map/all_gather | solution.py:78
  54.1 33.0 %all_gather.30 = bf16[192,768]{0,1:T(8,128)(2,1)} all-gather(bf16[192,96]{0,1:T(8,128)(2,1)S(1)} %copy.49), channel_id=1, replica_groups=mesh['dp'=8,'tensor'=4] {'dp'}, dimensions={1}, use_global_device_ids=true | all-gather | bytes 331776 | tf_op jit(solution)/shard_map/all_gather | solution.py:79
  135.5 58.6 %reduce-scatter.11.cloned.1.call-done = f32[512,768]{1,0:T(8,128)} async-done(((f32[2048,768]{1,0:T(8,128)}), f32[512,768]{1,0:T(8,128)}) %reduce-scatter.11.cloned.1.call-update) | async-done | bytes 1572880 | tf_op jit(solution)/shard_map/reduce_scatter | solution.py:121
  204.0 23.5 %all-gather.9.cloned.1.call-done = bf16[2048,768]{1,0:T(8,128)(2,1)} async-done(((bf16[512,768]{1,0:T(8,128)(2,1)}), bf16[2048,768]{1,0:T(8,128)(2,1)}) %all-gather.9.cloned.1.call-update) | async-done | bytes 3145744 | tf_op jit(solution)/shard_map/all_gather | solution.py:129
  227.5 7.5 fusion.133
  235.0 36.4 %all-gather.13.cloned.1.call-done = bf16[768,768]{0,1:T(8,128)(2,1)} async-done(((bf16[768,96]{0,1:T(8,128)(2,1)}), bf16[768,768]{0,1:T(8,128)(2,1)}) %all-gather.13.cloned.1.call-update) | async-done | bytes 1179664 | tf_op jit(solution)/shard_map/all_gather | solution.py:81
  271.4 28.6 %all-gather.15.cloned.1.call-done = bf16[2048,768]{1,0:T(8,128)(2,1)} async-done(((bf16[512,768]{1,0:T(8,128)(2,1)}), bf16[2048,768]{1,0:T(8,128)(2,1)}) %all-gather.15.cloned.1.call-update) | async-done | bytes 3145744 | tf_op jit(solution)/shard_map/all_gather | solution.py:148
  299.9 12.1 %convert_reduce_fusion = (f32[768]{0:T(1024)}, bf16[2048,768]{1,0:T(8,128)(2,1)S(1)}, bf16[2048,768]{1,0:T(8,128)(2,1)}) fusion(f32[2048,768]{1,0:T(8,128)} %fusion.133, f32[768]{0:T(1024)S(1)} %dynamic_slice.8, bf16[2048,768]{1,0:T(8,128)(2,1)} %all-gather.15.cloned.1.call-done, bf16[768,768]{0,1:T(8,128)(2,1)} %all-gather.13.cloned.1.call-done), kind=kOutput, calls=%fused_computation.28 | convolution fusion | flops 2461531392 | bytes 16914432 | tf_op jit(solution)/shard_map/td,fd->tf/dot_general | solution.py:151
  317.8 6.5 convolution_convert_fusion.1
  324.3 31.3 %reduce-scatter.15.cloned.1.call-done = bf16[512,768]{1,0:T(8,128)(2,1)} async-done(((bf16[2048,768]{1,0:T(8,128)(2,1)}), bf16[512,768]{1,0:T(8,128)(2,1)}) %reduce-scatter.15.cloned.1.call-update) | async-done | bytes 786448 | tf_op jit(solution)/shard_map/reduce_scatter | solution.py:155
  359.8 36.3 %reduce-scatter.13.cloned.1.call-done = bf16[512,768]{1,0:T(8,128)(2,1)} async-done(((bf16[2048,768]{1,0:T(8,128)(2,1)}), bf16[512,768]{1,0:T(8,128)(2,1)}) %reduce-scatter.13.cloned.1.call-update) | async-done | bytes 786448 | tf_op jit(solution)/shard_map/reduce_scatter | solution.py:134
  406.8 24.6 %all-gather.17.cloned.1.call-done = bf16[2048,768]{1,0:T(8,128)(2,1)} async-done(((bf16[512,768]{1,0:T(8,128)(2,1)}), bf16[2048,768]{1,0:T(8,128)(2,1)}) %all-gather.17.cloned.1.call-update) | async-done | bytes 3145744 | tf_op jit(solution)/shard_map/all_gather | solution.py:166
  447.6 4.4 fusion.85
  472.2 4.9 multiply_convert_fusion
  477.1 5.0 fusion.106
  486.0 4.2 bitcast_convert_fusion
  490.2 6.9 fusion.134
  497.2 6.9 fusion.135
  504.4 6.0 fusion.24
  513.8 31.3 %reduce-scatter.17.cloned.1.call-done = bf16[512,768]{1,0:T(8,128)(2,1)} async-done(((bf16[2048,768]{1,0:T(8,128)(2,1)}), bf16[512,768]{1,0:T(8,128)(2,1)}) %reduce-scatter.17.cloned.1.call-update) | async-done | bytes 786448 | tf_op jit(solution)/shard_map/reduce_scatter | solution.py:229
  549.0 41.4 %all-reduce.2 = (f32[768]{0:T(1024)}, f32[768]{0:T(1024)}, f32[2,768]{1,0:T(2,128)}, f32[768]{0:T(1024)}, f32[768]{0:T(1024)}, /*index=5*/f32[768]{0:T(1024)}, f32[3072]{0:T(1024)}, f32[768]{0:T(1024)}) all-reduce(f32[768]{0:T(1024)S(1)} %get-tuple-element.128, ...), channel_id=1, replica_groups=mesh['dp'=8,'tensor'=4] {'dp','tensor'}, use_global_device_ids=true, to_apply=%region_27.28 | all-reduce | flops 9216 | bytes 73728 | tf_op jit(solution)/shard_map/psum | solution.py:253
  593.2 25.7 %reduce-scatter.21.cloned.1.call-done = f32[96,768]{1,0:T(8,128)} async-done(((f32[768,768]{1,0:T(8,128)}), f32[96,768]{1,0:T(8,128)}) %reduce-scatter.21.cloned.1.call-update) | async-done | bytes 294928 | tf_op jit(solution)/shard_map/reduce_scatter | solution.py:242
  618.9 72.6 %reduce-scatter.23.cloned.1.call-done = f32[768,96]{0,1:T(8,128)} async-done(((f32[768,768]{0,1:T(8,128)}), f32[768,96]{0,1:T(8,128)}) %reduce-scatter.23.cloned.1.call-update) | async-done | bytes 294928 | tf_op jit(solution)/shard_map/reduce_scatter | solution.py:243
  691.5 72.4 %reduce-scatter.19.cloned.1.call-done = f32[96,3,192]{2,0,1:T(8,128)} async-done(((f32[768,3,192]{2,0,1:T(8,128)}), f32[96,3,192]{2,0,1:T(8,128)}) %reduce-scatter.19.cloned.1.call-update) | async-done | bytes 221200 | tf_op jit(solution)/shard_map/reduce_scatter | solution.py:240
  (354 shorter events, 138.6 us)
Async XLA Ops:
  8.0 85.8 %all-gather.7.cloned.1.call-start = ((), (), s32[]{:S(2)}) async-start(), calls=%async_computation.8 | async-start | bytes 3932160 | tf_op jit(solution)/shard_map/all_gather | solution.py:88
  14.6 179.6 %reduce-scatter.11.cloned.1.call-start = ((), (), s32[]{:S(2)}) async-start(), calls=%async_computation.9 | async-start | bytes 7864320 | tf_op jit(solution)/shard_map/reduce_scatter | solution.py:121
  53.3 44.4 %copy-start.22 = (bf16[768,3,192]{2,0,1:T(8,128)(2,1)}, bf16[768,3,192]{2,0,1:T(8,128)(2,1)S(1)}, u32[]{:S(2)}) copy-start(bf16[768,3,192]{2,0,1:T(8,128)(2,1)S(1)} %all_gather.29) | copy-start | bytes 2654212
  134.9 69.1 %all-gather.11.cloned.1.call-start = ((), (), s32[]{:S(2)}) async-start(), calls=%async_computation.11 | async-start | bytes 1327104 | tf_op jit(solution)/shard_map/all_gather | solution.py:80
  135.5 92.0 %all-gather.9.cloned.1.call-start = ((), (), s32[]{:S(2)}) async-start(), calls=%async_computation.10 | async-start | bytes 3932160 | tf_op jit(solution)/shard_map/all_gather | solution.py:129
  199.0 72.3 %all-gather.13.cloned.1.call-start = ((), (), s32[]{:S(2)}) async-start(), calls=%async_computation.12 | async-start | bytes 1327104 | tf_op jit(solution)/shard_map/all_gather | solution.py:81
  199.6 100.3 %all-gather.15.cloned.1.call-start = ((), (), s32[]{:S(2)}) async-start(), calls=%async_computation.14 | async-start | bytes 3932160 | tf_op jit(solution)/shard_map/all_gather | solution.py:148
  203.1 152.5 %reduce-scatter.15.cloned.1.call-start = ((), (), s32[]{:S(2)}) async-start(), calls=%async_computation.15 | async-start | bytes 3932160 | tf_op jit(solution)/shard_map/reduce_scatter | solution.py:155
  317.7 78.4 %reduce-scatter.13.cloned.1.call-start = ((), (), s32[]{:S(2)}) async-start(), calls=%async_computation.13 | async-start | bytes 3932160 | tf_op jit(solution)/shard_map/reduce_scatter | solution.py:134
  324.3 107.0 %all-gather.17.cloned.1.call-start = ((), (), s32[]{:S(2)}) async-start(), calls=%async_computation.16 | async-start | bytes 3932160 | tf_op jit(solution)/shard_map/all_gather | solution.py:166
  402.6 109.0 %reduce-scatter.25.cloned.1.call-start = ((), (), s32[]{:S(2)}) async-start(), calls=%async_computation.21 | async-start | bytes 884736
  443.1 102.0 %reduce-scatter.17.cloned.1.call-start = ((), (), s32[]{:S(2)}) async-start(), calls=%async_computation.17 | async-start | bytes 3932160 | tf_op jit(solution)/shard_map/reduce_scatter | solution.py:229
  490.2 128.7 %reduce-scatter.21.cloned.1.call-start = ((), (), s32[]{:S(2)}) async-start(), calls=%async_computation.19 | async-start | bytes 2654208 | tf_op jit(solution)/shard_map/reduce_scatter | solution.py:242
  497.2 194.3 %reduce-scatter.23.cloned.1.call-start = ((), (), s32[]{:S(2)}) async-start(), calls=%async_computation.20 | async-start | bytes 2654208 | tf_op jit(solution)/shard_map/reduce_scatter | solution.py:243
  504.2 259.7 %reduce-scatter.19.cloned.1.call-start = ((), (), s32[]{:S(2)}) async-start(), calls=%async_computation.18 | async-start | bytes 2654208 | tf_op jit(solution)/shard_map/reduce_scatter | solution.py:240
  510.8 36.0 %copy-start.85 = (f32[512]{0:T(512)S(1)}, f32[512]{0:T(512)}, u32[]{:S(2)}) copy-start(f32[512]{0:T(512)} %copy-done.84) | copy-start | bytes 6148
  510.8 36.0 %copy-start.75 = (f32[512]{0:T(512)S(1)}, f32[512]{0:T(512)}, u32[]{:S(2)}) copy-start(f32[512]{0:T(512)} %copy-done.74) | copy-start | bytes 6148
  511.1 37.8 %copy-start.87 = (f32[768]{0:T(1024)S(1)}, f32[768]{0:T(1024)}, u32[]{:S(2)}) copy-start(f32[768]{0:T(1024)} %get-tuple-element.141) | copy-start | bytes 9220
  511.1 37.8 %copy-start.88 = (f32[768]{0:T(1024)S(1)}, f32[768]{0:T(1024)}, u32[]{:S(2)}) copy-start(f32[768]{0:T(1024)} %get-tuple-element.126) | copy-start | bytes 9220
  511.1 37.8 %copy-start.89 = (f32[768]{0:T(1024)S(1)}, f32[768]{0:T(1024)}, u32[]{:S(2)}) copy-start(f32[768]{0:T(1024)} %get-tuple-element.130) | copy-start | bytes 9220
  511.2 37.8 %copy-start.90 = (f32[768]{0:T(1024)S(1)}, f32[768]{0:T(1024)}, u32[]{:S(2)}) copy-start(f32[768]{0:T(1024)} %get-tuple-element.145) | copy-start | bytes 9220
  511.2 79.2 %copy-start.11 = (f32[512,768]{1,0:T(8,128)S(1)}, f32[512,768]{1,0:T(8,128)}, u32[]{:S(2)}) copy-start(f32[512,768]{1,0:T(8,128)} %copy-done.10) | copy-start | bytes 4718596
  511.2 79.2 %copy-start.13 = (bf16[512,768]{1,0:T(8,128)(2,1)S(1)}, bf16[512,768]{1,0:T(8,128)(2,1)}, u32[]{:S(2)}) copy-start(bf16[512,768]{1,0:T(8,128)(2,1)} %get-tuple-element.142) | copy-start | bytes 2359300
  511.2 79.2 %copy-start.83 = (f32[512]{0:T(512)S(1)}, f32[512]{0:T(512)}, u32[]{:S(2)}) copy-start(f32[512]{0:T(512)} %copy-done.82) | copy-start | bytes 6148
  (95 other events, 528.3 us)
Sparse Core Ops, SparseCore 0:
  14.7 31.2 all-gather.6
  135.0 59.0 reduce-scatter.10
  402.8 28.5 all-gather.16
Sparse Core Ops, SparseCore 1:
  137.6 42.1 all-gather.10
  199.1 28.4 all-gather.8
  229.8 41.5 all-gather.12
  273.0 26.8 all-gather.14
  317.8 37.8 reduce-scatter.14
  358.2 37.8 reduce-scatter.12
  443.2 62.5 reduce-scatter.24
  508.2 36.9 reduce-scatter.16
  549.5 69.4 reduce-scatter.20
  623.4 68.0 reduce-scatter.22
  695.8 68.0 reduce-scatter.18
where the time goes:
time: 775 us; the launch traced here: 771 us
  waiting for transfers between devices  443 us (57%)
  matrix products  120 us (15%)
  blocking collectives  110 us (14%)
  other arithmetic  54.1 us (7%)
  local copies, waits for them, and re-layouts  26.8 us (3%)
  between operations  17.1 us (2%)
    reduce_scatter x1, waiting for transfers between devices, per_device(): lax.psum_scatter(grad_proj, 'dp', scatter_dimension=1, tiled=True)  72.6 us
    reduce_scatter x1, waiting for transfers between devices, per_device(): lax.psum_scatter(grad_qkv_w, 'dp', scatter_dimension=0, tiled=True)  72.4 us
    reduce_scatter x1, waiting for transfers between devices, per_device(): lax.psum_scatter(jnp.dot(attended, out_rows, preferred_element_type=jnp.f...  58.6 us
    psum x1, blocking collectives, per_device(): lax.psum((grad_gain_one, grad_shift_one, qv_full, out_bias_part, grad_gai...  41.4 us
    all_gather x1, waiting for transfers between devices, per_device(): lax.all_gather(proj_weight, 'dp', axis=1, tiled=True)  36.4 us
    reduce_scatter x1, waiting for transfers between devices, per_device(): lax.psum_scatter(jnp.dot(activated, proj_rows, preferred_element_type=jnp...  36.3 us
    all_gather x1, blocking collectives, per_device(): lax.all_gather(qkv_weight, 'dp', axis=0, tiled=True)  35.5 us
    all_gather x1, blocking collectives, per_device(): lax.all_gather(out_weight, 'dp', axis=1, tiled=True)  33 us
  transfers between devices with their start and end apart: 14, of which 11 were waited for; matrix products, arithmetic and copies ran while one was open for 15% of the time, Pallas kernels for 0%

commit v1 on v0

v1 whole, which is shorter than its diff:
```python
import jax
import jax.numpy as jnp
from jax import lax
from jax.sharding import PartitionSpec as P

HS = 64
BLK = 128
QB = 512


EPSILON = 1e-05
MASKED = -1e30
GELU_SCALE = 0.7978845608028654

BF = jnp.bfloat16
F32 = jnp.float32


def layer_norm(values, norm_gain, norm_shift):
    centre = values - jnp.mean(values, axis=-1, keepdims=True)
    spread = jnp.mean(centre * centre, axis=-1, keepdims=True)
    return centre * lax.rsqrt(spread + EPSILON) * norm_gain + norm_shift


def gelu_tanh(values):
    return (
        0.5 * values * (1.0 + jnp.tanh(GELU_SCALE * (values + 0.044715 * values * values * values)))
    )


def segment_ids(lengths, capacity):
    padded = (lengths + BLK - 1) // BLK * BLK
    starts = jnp.cumsum(padded, axis=1) - padded
    places = jnp.arange(capacity, dtype=jnp.int32)
    inside = (places[None, None, :] >= starts[:, :, None]) & (
        places[None, None, :] < (starts + lengths)[:, :, None]
    )
    labels = jnp.arange(lengths.shape[1], dtype=jnp.int32)[None, :, None] + 1
    return jnp.sum(jnp.where(inside, labels, 0), axis=1) - 1


def swap(value, axis, bits):
    size = lax.axis_size(axis)
    return lax.ppermute(value, axis, [(i, i ^ bits) for i in range(size)])


def bits_of(axis):
    size = lax.axis_size(axis)
    count = size.bit_length() - 1
    assert 1 << count == size
    return [1 << b for b in range(count)]


def gather_rows(shard, axis):
    here = lax.axis_index(axis)
    full = shard[None]
    for bit in reversed(bits_of(axis)):
        other = swap(full, axis, bit)
        high = (here & bit) > 0
        full = jnp.where(
            high, jnp.stack([other, full], 1), jnp.stack([full, other], 1)
        ).reshape(-1, *shard.shape)
    return full


def scatter_sum(part, axis):
    here = lax.axis_index(axis)
    for bit in bits_of(axis):
        high = ((here & bit) > 0).astype(jnp.int32)
        pairs = part.reshape(-1, 2, *part.shape[1:])
        keep = lax.dynamic_index_in_dim(pairs, high, 1, keepdims=False)
        give = lax.dynamic_index_in_dim(pairs, 1 - high, 1, keepdims=False)
        part = keep.astype(F32) + swap(give.astype(BF), axis, bit).astype(F32)
    return part[0]


def relative_gather(rows, axis):
    placed = {0: rows}
    for bit in reversed(bits_of(axis)):
        placed.update({r ^ bit: swap(b, axis, bit) for r, b in list(placed.items())})
    return [placed[r] for r in range(len(placed))]


def relative_scatter(blocks, axis):
    live = {r: b for r, b in enumerate(blocks)}
    for bit in bits_of(axis):
        fresh = {}
        for r in sorted(live):
            if not r & bit:
                got = swap(live[r | bit].astype(BF), axis, bit)
                fresh[r] = live[r].astype(F32) + got.astype(F32)
        live = fresh
    return live[0]


def exchange(blocks, axis):
    return [b if r == 0 else swap(b, axis, r) for r, b in enumerate(blocks)]


def everyone_sum(value, axes):
    for axis in axes:
        for bit in bits_of(axis):
            value = value + swap(value, axis, bit)
    return value


def absolute(blocks, axis):
    here = lax.axis_index(axis)
    rows = blocks[0].shape[0]
    full = jnp.zeros((rows * len(blocks), *blocks[0].shape[1:]), blocks[0].dtype)
    for r, b in enumerate(blocks):
        full = lax.dynamic_update_slice_in_dim(full, b, (here ^ r) * rows, 0)
    return full


def block_scores(queries, key_rows, seg_query, seg_key, place_query, place_key):
    raw_scores = jnp.einsum(
        "qhd,khd->hqk", queries, key_rows, preferred_element_type=jnp.float32
    ) * HS ** (-0.5)
    allowed = (
        (seg_query[:, None] == seg_key[None, :])
        & (place_key[None, :] <= place_query[:, None])
        & (seg_query[:, None] >= 0)
    )
    return jnp.where(allowed[None], raw_scores, MASKED)


def attention_forward(queries, key_rows, values, seg):
    capacity = queries.shape[0]
    places = jnp.arange(capacity, dtype=jnp.int32)
    outputs = []
    log_totals = []
    for block_begin in range(0, capacity, QB):
        block_end = block_begin + QB
        scores = block_scores(
            queries[block_begin:block_end],
            key_rows[:block_end],
            seg[block_begin:block_end],
            seg[:block_end],
            places[block_begin:block_end],
            places[:block_end],
        )
        row_peak = jnp.max(scores, axis=-1, keepdims=True)
        weights = jnp.exp(scores - row_peak)
        row_total = jnp.sum(weights, axis=-1, keepdims=True)
        probability = (weights / row_total).astype(BF)
        outputs.append(
            jnp.einsum("hqk,khd->qhd", probability, values[:block_end], preferred_element_type=F32)
        )
        log_totals.append(row_peak + jnp.log(row_total))
    return jnp.concatenate(outputs, 0).astype(BF), jnp.concatenate(log_totals, 1)


def attention_backward(queries, key_rows, values, seg, log_total, grad_attended):
    capacity = queries.shape[0]
    scale = HS ** (-0.5)
    places = jnp.arange(capacity, dtype=jnp.int32)
    query_grads = []
    grad_keys = jnp.zeros(key_rows.shape, F32)
    grad_values = jnp.zeros(values.shape, F32)
    for block_begin in range(0, capacity, QB):
        block_end = block_begin + QB
        query_block = queries[block_begin:block_end]
        attended_grad_block = grad_attended[block_begin:block_end]
        scores = block_scores(
            query_block,
            key_rows[:block_end],
            seg[block_begin:block_end],
            seg[:block_end],
            places[block_begin:block_end],
            places[:block_end],
        )
        probability = jnp.exp(scores - log_total[:, block_begin:block_end])
        grad_probs = jnp.einsum(
            "qhd,khd->hqk", attended_grad_block, values[:block_end], preferred_element_type=F32
        )
        centre = jnp.sum(grad_probs * probability, axis=-1, keepdims=True)
        grad_scores = (probability * (grad_probs - centre)).astype(BF)
        query_grads.append(
            jnp.einsum("hqk,khd->qhd", grad_scores, key_rows[:block_end], preferred_element_type=F32)
            * scale
        )
        grad_keys = grad_keys.at[:block_end].add(
            jnp.einsum("hqk,qhd->khd", grad_scores, query_block, preferred_element_type=F32) * scale
        )
        grad_values = grad_values.at[:block_end].add(
            jnp.einsum(
                "hqk,qhd->khd", probability.astype(BF), attended_grad_block, preferred_element_type=F32
            )
        )
    return jnp.concatenate(query_grads, 0), grad_keys, grad_values


def per_device(
    tokens,
    seq_lengths,
    norm1_gain,
    norm1_shift,
    qkv_weight,
    qv_bias,
    out_weight,
    out_bias,
    norm2_gain,
    norm2_shift,
    fc_weight,
    fc_bias,
    proj_weight,
    proj_bias,
    out_grad,
):
    tensor_size = lax.axis_size("tensor")
    dp_size = lax.axis_size("dp")
    tensor_pos = lax.axis_index("tensor")
    local_rows, model_width = tokens.shape
    capacity = local_rows * tensor_size
    shard_rows = qkv_weight.shape[0]
    head_cols = qkv_weight.shape[2]
    hidden_cols = fc_weight.shape[1]

    full_qkv = gather_rows(qkv_weight.reshape(shard_rows, 3 * head_cols), "dp").reshape(
        model_width, 3 * head_cols
    )
    out_turned = gather_rows(out_weight.T, "dp").reshape(model_width, head_cols)
    fc_cols = gather_rows(fc_weight, "dp").reshape(model_width, hidden_cols)
    proj_turned = gather_rows(proj_weight.T, "dp").reshape(model_width, hidden_cols)
    outs = relative_gather(out_turned, "tensor")

    seg = segment_ids(seq_lengths, capacity)[0]
    live_here = lax.dynamic_slice_in_dim(seg, tensor_pos * local_rows, local_rows, 0) >= 0
    stream = tokens.astype(F32)
    first_norm, first_back = jax.vjp(layer_norm, stream, norm1_gain, norm1_shift)
    firsts = relative_gather(first_norm.astype(BF), "tensor")
    first_all = absolute(firsts, "tensor")
    grad_mlp = jnp.where(live_here[:, None], out_grad, jnp.zeros_like(out_grad))
    grads = relative_gather(grad_mlp, "tensor")

    projected = jnp.dot(first_all, full_qkv, preferred_element_type=F32).reshape(
        capacity, 3, head_cols
    )
    bias_here = lax.dynamic_slice_in_dim(qv_bias, tensor_pos * head_cols, head_cols, 1)
    queries = (projected[:, 0] + bias_here[0]).astype(BF).reshape(capacity, -1, HS)
    key_rows = projected[:, 1].astype(BF).reshape(capacity, -1, HS)
    values = (projected[:, 2] + bias_here[1]).astype(BF).reshape(capacity, -1, HS)
    attended, log_total = attention_forward(queries, key_rows, values, seg)
    attended = attended.reshape(capacity, head_cols)

    mine = exchange(
        [
            lax.dynamic_slice_in_dim(attended, (tensor_pos ^ r) * local_rows, local_rows, 0)
            for r in range(tensor_size)
        ],
        "tensor",
    )
    branch = sum(
        jnp.einsum("tc,dc->td", a, w, preferred_element_type=F32) for a, w in zip(mine, outs, strict=True)
    )
    middle = stream + branch + out_bias
    second_norm, second_back = jax.vjp(layer_norm, middle, norm2_gain, norm2_shift)
    second_all = jnp.concatenate(relative_gather(second_norm.astype(BF), "tensor"), 0)
    grad_all = jnp.concatenate(grads, 0)
    fc_bias_here = lax.dynamic_slice_in_dim(fc_bias, tensor_pos * hidden_cols, hidden_cols, 0)
    pre_gelu = jnp.dot(second_all, fc_cols, preferred_element_type=F32) + fc_bias_here
    activated_f, gelu_back = jax.vjp(gelu_tanh, pre_gelu)
    activated = activated_f.astype(BF)
    grad_act = jnp.dot(grad_all, proj_turned, preferred_element_type=F32)
    grad_pre = gelu_back(grad_act)[0].astype(BF)
    grad_second_part = jnp.einsum("tf,df->td", grad_pre, fc_cols, preferred_element_type=F32).astype(
        BF
    )
    grad_second = relative_scatter(
        list(grad_second_part.reshape(tensor_size, local_rows, model_width)), "tensor"
    )
    mlp_part = jnp.einsum("tf,df->td", activated, proj_turned, preferred_element_type=F32).astype(BF)
    mlp_out = relative_scatter(
        list(mlp_part.reshape(tensor_size, local_rows, model_width)), "tensor"
    )
    result = jnp.where(live_here[:, None], middle + mlp_out + proj_bias, 0.0).astype(BF)

    grad_here = grad_mlp.astype(F32)
    grad_proj = jnp.einsum("td,tf->df", grad_all, activated, preferred_element_type=F32)
    grad_fc = jnp.einsum("td,tf->df", second_all, grad_pre, preferred_element_type=F32)
    grad_fc_cols = jnp.sum(grad_pre.astype(F32), axis=0)
    sum_fc = scatter_sum(grad_fc.reshape(dp_size, shard_rows, hidden_cols), "dp")
    sum_proj = scatter_sum(grad_proj.reshape(dp_size, shard_rows, hidden_cols), "dp").T

    middle_part, grad_gain_two, grad_shift_two = second_back(grad_second)
    grad_middle = grad_here + middle_part
    grad_branch = grad_middle.astype(BF)
    grad_mine = [
        jnp.dot(grad_branch, w, preferred_element_type=F32).astype(BF) for w in outs
    ]
    grad_attended = absolute(exchange(grad_mine, "tensor"), "tensor").reshape(capacity, -1, HS)
    grad_out_parts = exchange(
        [
            jnp.einsum("td,tc->dc", grad_branch, a, preferred_element_type=F32).astype(BF)
            for a in mine
        ],
        "tensor",
    )
    grad_out = sum(g.astype(F32) for g in grad_out_parts)
    sum_out = scatter_sum(grad_out.reshape(dp_size, shard_rows, head_cols), "dp").T

    grad_queries, grad_keys, grad_values = attention_backward(
        queries, key_rows, values, seg, log_total, grad_attended
    )
    grad_qkv = (
        jnp.stack([grad_queries, grad_keys, grad_values], 1)
        .reshape(capacity, 3 * head_cols)
        .astype(BF)
    )
    grad_first_part = jnp.einsum("tc,dc->td", grad_qkv, full_qkv, preferred_element_type=F32).astype(
        BF
    )
    grad_first = scatter_sum(
        grad_first_part.reshape(tensor_size, local_rows, model_width), "tensor"
    )
    grad_qkv_w = jnp.einsum("td,tc->dc", first_all, grad_qkv, preferred_element_type=F32)
    sum_qkv = scatter_sum(grad_qkv_w.reshape(dp_size, shard_rows, 3 * head_cols), "dp").reshape(
        shard_rows, 3, head_cols
    )
    grad_bias_cols = jnp.sum(grad_qkv.reshape(capacity, 3, head_cols).astype(F32), axis=0)[0::2]
    input_part, grad_gain_one, grad_shift_one = first_back(grad_first)
    grad_tokens = (grad_middle + input_part).astype(BF)

    qv_full = lax.dynamic_update_slice_in_dim(
        jnp.zeros((2, model_width), F32), grad_bias_cols, tensor_pos * head_cols, 1
    )
    fc_full = lax.dynamic_update_slice_in_dim(
        jnp.zeros(fc_bias.shape, F32), grad_fc_cols, tensor_pos * hidden_cols, 0
    )
    out_bias_part = jnp.sum(grad_branch.astype(F32), axis=0)
    proj_bias_part = jnp.sum(grad_here, axis=0)
    early = everyone_sum(
        jnp.concatenate(
            [out_bias_part, grad_gain_two, grad_shift_two, proj_bias_part, fc_full]
        ).reshape(-1, 128),
        ("tensor", "dp"),
    ).reshape(-1)
    late = everyone_sum(
        jnp.concatenate([grad_gain_one, grad_shift_one, qv_full.reshape(-1)]).reshape(-1, 128),
        ("tensor", "dp"),
    ).reshape(-1)
    w = model_width
    return (
        result,
        grad_tokens,
        late[:w],
        late[w : 2 * w],
        sum_qkv,
        late[2 * w :].reshape(2, w),
        sum_out,
        early[:w],
        early[w : 2 * w],
        early[2 * w : 3 * w],
        sum_fc,
        early[4 * w :],
        sum_proj,
        early[3 * w : 4 * w],
    )


def solution(mesh):
    placed = (
        P(("dp", "tensor"), None),
        P("dp", None),
        P(),
        P(),
        P("dp", None, "tensor"),
        P(),
        P("tensor", "dp"),
        P(),
        P(),
        P(),
        P("dp", "tensor"),
        P(),
        P("tensor", "dp"),
        P(),
        P(("dp", "tensor"), None),
    )
    return jax.shard_map(
        per_device,
        mesh=mesh,
        in_specs=placed,
        out_specs=(
            P(("dp", "tensor"), None),
            P(("dp", "tensor"), None),
            P(),
            P(),
            P("dp", None, "tensor"),
            P(),
            P("tensor", "dp"),
            P(),
            P(),
            P(),
            P("dp", "tensor"),
            P(),
            P("tensor", "dp"),
            P(),
        ),
        check_vma=False,
    )
```

time: 775 us -> 422 us (0.54)
  waiting for transfers between devices: 443 us -> 96.7 us
  blocking collectives: 110 us -> 0 us
  starting transfers between devices: 0.98 us -> 66.3 us
  local copies, waits for them, and re-layouts: 26.8 us -> 69.1 us
  other arithmetic: 54.1 us -> 76.4 us
  matrix products: 120 us -> 103 us
  between operations: 17.1 us -> 2.86 us
    reduce_scatter x7 -> x0, waiting for transfers between devices: 328 us -> none  [the longest x1 72.6 us: per_device(): lax.psum_scatter(grad_proj, 'dp', scatter_dimension=1, tiled=True)]
    all_gather x6 -> x0, waiting for transfers between devices: 113 us -> none  [the longest x1 36.4 us: per_device(): lax.all_gather(proj_weight, 'dp', axis=1, tiled=True)]
    ppermute x0 -> x63, waiting for transfers between devices: none -> 96.7 us  [swap(): return lax.ppermute(value, axis, [(i, i ^ bits) for i in range(size)])]
    all_gather x2 -> x0, blocking collectives: 68.5 us -> none  [the longest x1 35.5 us: per_device(): lax.all_gather(qkv_weight, 'dp', axis=0, tiled=True)]
    ppermute x0 -> x63, starting transfers between devices: none -> 66.3 us  [swap(): return lax.ppermute(value, axis, [(i, i ^ bits) for i in range(size)])]
    psum x1 -> x0, blocking collectives: 41.4 us -> none  [per_device(): lax.psum((grad_gain_one, grad_shift_one, qv_full, out_bias_part, grad_gai...]
    dot_general x31 -> x41, matrix products: 111 us -> 96.3 us  [the longest x4 16.9 us: attention_backward(): jnp.einsum('qhd,khd->hqk', attended_grad_block, values[:block_end], prefe...]
    select_n x0 -> x16, other arithmetic: none -> 9.72 us  [gather_rows(): jnp.where(high, jnp.stack([other, full], 1), jnp.stack([full, other], 1))]
  transfers between devices with their start and end apart: 14 -> 63, of which waited for: 11 -> 26; matrix products, arithmetic and copies ran while one was open for 15% -> 51% of each run, Pallas kernels for 0% -> 0%
where the time goes in v1:
time: 422 us; the launch traced here: 415 us
  matrix products  103 us (24%)
  waiting for transfers between devices  96.7 us (23%)
  other arithmetic  76.4 us (18%)
  local copies, waits for them, and re-layouts  69.1 us (16%)
  starting transfers between devices  66.3 us (16%)
    ppermute x63, waiting for transfers between devices, swap(): return lax.ppermute(value, axis, [(i, i ^ bits) for i in range(size)])  96.7 us
    ppermute x63, starting transfers between devices, swap(): return lax.ppermute(value, axis, [(i, i ^ bits) for i in range(size)])  66.3 us
    unnamed x231, local copies, waits for them, and re-layouts  22.1 us
    convert_element_type x4, other arithmetic, attention_backward(): grad_scores = (probability * (grad_probs - centre)).astype(BF)  18.3 us
    dot_general x4, matrix products, attention_backward(): jnp.einsum('qhd,khd->hqk', attended_grad_block, values[:block_end], prefe...  16.9 us
    dot_general x1, matrix products, per_device(): grad_act = jnp.dot(grad_all, proj_turned, preferred_element_type=F32)  11.3 us
    dot_general x4, matrix products, attention_forward(): jnp.einsum('hqk,khd->qhd', probability, values[:block_end], preferred_ele...  10 us
    select_n x16, other arithmetic, gather_rows(): jnp.where(high, jnp.stack([other, full], 1), jnp.stack([full, other], 1))  9.72 us
  transfers between devices with their start and end apart: 63, of which 26 were waited for; matrix products, arithmetic and copies ran while one was open for 51% of the time, Pallas kernels for 0%

profile of v1, /device:TPU:0, one launch (start us, length us, event | category | flops | bytes accessed | tf_op | source)
XLA Modules:
  0.0 414.7 jit_solution(9288818969058045352)
XLA Ops:
  34.7 5.4 %collective-permute-done.21 = bf16[1,96,768]{2,1,0:T(8,128)(2,1)S(1)} collective-permute-done((bf16[1,96,768]{2,1,0:T(8,128)(2,1)S(1)}, bf16[1,96,768]{2,1,0:T(8,128)(2,1)S(1)}, u32[]{:S(2)}, u32[]{:S(2)}) %collective-permute-start.21) | collective-permute-done | bytes 147488 | tf_op jit(solution)/shard_map/ppermute | solution.py:44
  40.5 7.1 %collective-permute-done.4 = bf16[2,96,576]{1,2,0:T(8,128)(2,1)S(1)} collective-permute-done((bf16[2,96,576]{1,2,0:T(8,128)(2,1)S(1)}, bf16[2,96,576]{1,2,0:T(8,128)(2,1)S(1)}, u32[]{:S(2)}, u32[]{:S(2)}) %collective-permute-start.4) | collective-permute-done | bytes 221216 | tf_op jit(solution)/shard_map/ppermute | solution.py:44
  58.2 4.7 %collective-permute-done.5 = bf16[4,96,576]{2,1,0:T(8,128)(2,1)} collective-permute-done((bf16[4,96,576]{2,1,0:T(8,128)(2,1)}, bf16[4,96,576]{2,1,0:T(8,128)(2,1)}, u32[]{:S(2)}, u32[]{:S(2)}) %collective-permute-start.5) | collective-permute-done | bytes 442400 | tf_op jit(solution)/shard_map/ppermute | solution.py:44
  109.0 5.4 %collective-permute-done.11 = bf16[512,192]{0,1:T(8,128)(2,1)S(1)} collective-permute-done((bf16[512,192]{0,1:T(8,128)(2,1)S(1)}, bf16[512,192]{0,1:T(8,128)(2,1)S(1)}, u32[]{:S(2)}, u32[]{:S(2)}) %collective-permute-start.11) | collective-permute-done | bytes 196640 | tf_op jit(solution)/shard_map/ppermute | solution.py:44
  118.2 5.1 %collective-permute-done.13 = bf16[512,192]{0,1:T(8,128)(2,1)S(1)} collective-permute-done((bf16[512,192]{0,1:T(8,128)(2,1)S(1)}, bf16[512,192]{0,1:T(8,128)(2,1)S(1)}, u32[]{:S(2)}, u32[]{:S(2)}) %collective-permute-start.13) | collective-permute-done | bytes 196640 | tf_op jit(solution)/shard_map/ppermute | solution.py:44
  134.8 9.9 %collective-permute-done.20 = bf16[4,96,768]{2,1,0:T(8,128)(2,1)} collective-permute-done((bf16[4,96,768]{2,1,0:T(8,128)(2,1)}, bf16[4,96,768]{2,1,0:T(8,128)(2,1)}, u32[]{:S(2)}, u32[]{:S(2)}) %collective-permute-start.20) | collective-permute-done | bytes 589856 | tf_op jit(solution)/shard_map/ppermute | solution.py:44
  148.7 5.1 %copy.132 = bf16[768,2048]{1,0:T(8,128)(2,1)} copy(bf16[768,2048]{0,1:T(8,128)(2,1)} %bitcast.343) | data formatting | bytes 6291456 | tf_op jit(solution)/shard_map/td,tc->dc/dot_general | solution.py:317
  154.5 5.0 %fusion.116 = f32[2048,768]{1,0:T(8,128)S(1)} fusion(bf16[768,768]{1,0:T(8,128)(2,1)} %bitcast.394, bf16[512,768]{1,0:T(8,128)(2,1)} %collective-permute-done.17, bf16[512,768]{1,0:T(8,128)(2,1)} %collective-permute-done.16, bf16[512,768]{1,0:T(8,128)(2,1)} %collective-permute-done.15, bf16[512,768]{1,0:T(8,128)(2,1)} %add_convert_fusion.3), kind=kOutput, calls=%fused_computation.193 | convolution fusion | flops 2428502016 | bytes 10616832 | tf_op jit(solution)/shard_map/dot_general | solution.py:262
  159.6 4.9 %fusion.113 = f32[768,768]{1,0:T(8,128)S(1)} fusion(bf16[512,768]{1,0:T(8,128)(2,1)} %collective-permute-done.29, bf16[512,768]{1,0:T(8,128)(2,1)} %collective-permute-done.28, bf16[512,768]{1,0:T(8,128)(2,1)} %collective-permute-done.27, bf16[512,768]{1,0:T(8,128)(2,1)} %get-tuple-element.174, f32[2048,768]{1,0:T(8,128)S(1)} %fusion.116, ...), kind=kOutput, calls=%fused_computation.190 | convolution fusion | flops 2444230656 | bytes 11799552 | tf_op jit(solution)/shard_map/td,tf->df/dot_general | solution.py:280
  166.5 4.2 %convolution_convert_fusion.2 = bf16[2048,768]{1,0:T(8,128)(2,1)S(1)} fusion(bf16[768,768]{1,0:T(8,128)(2,1)S(1)} %bitcast.396, f32[2048,768]{1,0:T(8,128)S(1)} %fusion.116, f32[768]{0:T(1024)S(1)} %copy-done.101), kind=kOutput, calls=%fused_computation.48 | convolution fusion | flops 2433220608 | bytes 10619904 | tf_op jit(solution)/shard_map/tf,df->td/dot_general | solution.py:273
  170.8 11.3 %convert_reduce_fusion = (f32[768]{0:T(1024)S(1)}, bf16[2048,768]{1,0:T(8,128)(2,1)S(1)}) fusion(bf16[768,768]{1,0:T(8,128)(2,1)S(1)} %bitcast.397, bf16[512,768]{1,0:T(8,128)(2,1)} %collective-permute-done.29, bf16[512,768]{1,0:T(8,128)(2,1)} %collective-permute-done.28, bf16[512,768]{1,0:T(8,128)(2,1)} %collective-permute-done.27, ...), kind=kOutput, calls=%fused_computation.27 | convolution fusion | flops 2470968576 | bytes 13768704 | tf_op jit(solution)/shard_map/dot_general | solution.py:265
  182.1 4.5 %fusion.115 = f32[768,768]{1,0:T(8,128)S(1)} fusion(bf16[2048,768]{1,0:T(8,128)(2,1)S(1)} %get-tuple-element.237, bf16[512,768]{1,0:T(8,128)(2,1)} %collective-permute-done.17, bf16[512,768]{1,0:T(8,128)(2,1)} %collective-permute-done.16, bf16[512,768]{1,0:T(8,128)(2,1)} %collective-permute-done.15, bf16[512,768]{1,0:T(8,128)(2,1)} %add_convert_fusion.3), kind=kOutput, calls=%fused_computation.192 | convolution fusion | flops 2428502016 | bytes 8650752 | tf_op jit(solution)/shard_map/td,tf->df/dot_general | solution.py:281
  220.6 5.0 %collective-permute-done.62 = bf16[1,96,768]{2,1,0:T(8,128)(2,1)S(1)} collective-permute-done((bf16[1,96,768]{2,1,0:T(8,128)(2,1)S(1)}, bf16[1,96,768]{2,1,0:T(8,128)(2,1)S(1)}, u32[]{:S(2)}, u32[]{:S(2)}) %collective-permute-start.62) | collective-permute-done | bytes 147488 | tf_op jit(solution)/shard_map/ppermute | solution.py:44
  227.3 4.2 %collective-permute-done.59 = bf16[1,96,768]{2,1,0:T(8,128)(2,1)S(1)} collective-permute-done((bf16[1,96,768]{2,1,0:T(8,128)(2,1)S(1)}, bf16[1,96,768]{2,1,0:T(8,128)(2,1)S(1)}, u32[]{:S(2)}, u32[]{:S(2)}) %collective-permute-start.59) | collective-permute-done | bytes 147488 | tf_op jit(solution)/shard_map/ppermute | solution.py:44
  232.3 9.7 %collective-permute-done.32 = bf16[512,768]{1,0:T(8,128)(2,1)S(1)} collective-permute-done((bf16[512,768]{1,0:T(8,128)(2,1)S(1)}, bf16[512,768]{1,0:T(8,128)(2,1)S(1)}, u32[]{:S(2)}, u32[]{:S(2)}) %collective-permute-start.32) | collective-permute-done | bytes 786464 | tf_op jit(solution)/shard_map/ppermute | solution.py:44
  256.8 5.1 %collective-permute-done.53 = f32[48,128]{1,0:T(8,128)S(1)} collective-permute-done((f32[48,128]{1,0:T(8,128)S(1)}, f32[48,128]{1,0:T(8,128)S(1)}, u32[]{:S(2)}, u32[]{:S(2)}) %collective-permute-start.53) | collective-permute-done | bytes 24608 | tf_op jit(solution)/shard_map/ppermute | solution.py:44
  282.3 4.3 %multiply_reduce_fusion.2 = (f32[3,512]{1,0:T(4,128)S(1)}, f32[3,512,1024]{2,1,0:T(8,128)}) fusion(f32[3,512,1024]{2,1,0:T(8,128)S(1)} %bitcast.342, f32[3,512]{1,0:T(4,128)S(1)} %copy-done.76, bf16[512,3,64]{0,2,1:T(8,128)(2,1)S(1)} %bitcast.381, bf16[1024,3,64]{0,2,1:T(8,128)(2,1)S(1)} %bitcast.384), kind=kOutput, calls=%fused_computation.30 | convolution fusion | flops 206043648 | bytes 13185024 | tf_op jit(solution)/shard_map/qhd,khd->hqk/dot_general | solution.py:174
  288.5 5.7 %multiply_reduce_fusion.1 = (f32[3,512]{1,0:T(4,128)S(1)}, f32[3,512,1536]{2,1,0:T(8,128)}) fusion(f32[3,512,1536]{2,1,0:T(8,128)S(1)} %bitcast.340, f32[3,512]{1,0:T(4,128)S(1)} %log_add_fusion.1, bf16[512,3,64]{0,2,1:T(8,128)(2,1)S(1)} %bitcast.371, bf16[1536,3,64]{0,2,1:T(8,128)(2,1)S(1)} %bitcast.364), kind=kOutput, calls=%fused_computation.11 | convolution fusion | flops 309066240 | bytes 19673088 | tf_op jit(solution)/shard_map/qhd,khd->hqk/dot_general | solution.py:174
  297.1 6.2 %multiply_reduce_fusion = (f32[3,512]{1,0:T(4,128)S(1)}, f32[3,512,2048]{2,1,0:T(8,128)}) fusion(f32[3,512,2048]{2,1,0:T(8,128)S(1)} %bitcast.338, f32[3,512]{1,0:T(4,128)S(1)} %log_add_fusion, bf16[512,3,64]{0,2,1:T(8,128)(2,1)S(1)} %bitcast.367, f32[2048,3,64]{0,2,1:T(8,128)S(1)} %bitcast.347, f32[3,64]{1,0:T(4,128)S(1)} %copy-done.80), kind=kOutput, calls=%fused_computation.1 | convolution fusion | flops 412875264 | bytes 26948352 | tf_op jit(solution)/shard_map/qhd,khd->hqk/dot_general | solution.py:174
  305.5 5.4 %multiply_convert_fusion.2 = bf16[3,512,1024]{2,1,0:T(8,128)(2,1)S(1)} fusion(f32[3,512,1024]{2,1,0:T(8,128)} %get-tuple-element.231, f32[3,512,1024]{2,1,0:T(8,128)} %copy-done.2, f32[3,512]{1,0:T(4,128)S(1)} %get-tuple-element.230, f32[3,512]{1,0:T(4,128)S(1)} %copy-done.76), kind=kLoop, calls=%fused_computation.29 | loop fusion | flops 6291456 | bytes 15740928 | tf_op jit(solution)/shard_map/convert_element_type | solution.py:178
  312.8 5.3 %multiply_convert_fusion.1 = bf16[3,512,1536]{2,1,0:T(8,128)(2,1)S(1)} fusion(f32[3,512,1536]{2,1,0:T(8,128)} %get-tuple-element.233, f32[3,512,1536]{2,1,0:T(8,128)S(1)} %bitcast.340, f32[3,512]{1,0:T(4,128)S(1)} %get-tuple-element.232, f32[3,512]{1,0:T(4,128)S(1)} %log_add_fusion.1), kind=kLoop, calls=%fused_computation.10 | loop fusion | flops 9437184 | bytes 23605248 | tf_op jit(solution)/shard_map/convert_element_type | solution.py:178
  320.6 6.7 %multiply_convert_fusion = bf16[3,512,2048]{2,1,0:T(8,128)(2,1)S(1)} fusion(f32[3,512,2048]{2,1,0:T(8,128)} %get-tuple-element.235, f32[3,512,2048]{2,1,0:T(8,128)S(1)} %bitcast.338, f32[3,512]{1,0:T(4,128)S(1)} %get-tuple-element.234, f32[3,512]{1,0:T(4,128)S(1)} %log_add_fusion), kind=kLoop, calls=%fused_computation | loop fusion | flops 12582912 | bytes 31469568 | tf_op jit(solution)/shard_map/convert_element_type | solution.py:178
  378.4 4.4 %collective-permute-done.44 = bf16[2,96,576]{1,2,0:T(8,128)(2,1)} collective-permute-done((bf16[2,96,576]{1,2,0:T(8,128)(2,1)S(1)}, bf16[2,96,576]{1,2,0:T(8,128)(2,1)}, u32[]{:S(2)}, u32[]{:S(2)}) %collective-permute-start.44) | collective-permute-done | bytes 221216 | tf_op jit(solution)/shard_map/ppermute | solution.py:44
  387.0 6.0 %collective-permute-done.37 = bf16[1,512,768]{2,1,0:T(8,128)(2,1)S(1)} collective-permute-done((bf16[1,512,768]{2,1,0:T(8,128)(2,1)}, bf16[1,512,768]{2,1,0:T(8,128)(2,1)S(1)}, u32[]{:S(2)}, u32[]{:S(2)}) %collective-permute-start.37) | collective-permute-done | bytes 786464 | tf_op jit(solution)/shard_map/ppermute | solution.py:44
  (555 shorter events, 271.2 us)
Async XLA Ops:
  7.4 61.7 %collective-permute-start = (bf16[512,768]{1,0:T(8,128)(2,1)}, bf16[512,768]{1,0:T(8,128)(2,1)}, u32[]{:S(2)}, u32[]{:S(2)}) collective-permute-start(bf16[512,768]{1,0:T(8,128)(2,1)} %get-tuple-element.186), channel_id=1, source_target_pairs={{0,1},{1,0},{2,3},{3,2},{4,5},{5,4},{6,7},{7,6},{8,9},{9,8},{10,11... | collective-permute-start | bytes 2359304 | tf_op jit(solution)/shard_map/ppermute | solution.py:44
  7.9 44.2 %collective-permute-start.1 = (bf16[512,768]{1,0:T(8,128)(2,1)}, bf16[512,768]{1,0:T(8,128)(2,1)}, u32[]{:S(2)}, u32[]{:S(2)}) collective-permute-start(bf16[512,768]{1,0:T(8,128)(2,1)} %get-tuple-element.186), channel_id=1, source_target_pairs={{0,2},{1,3},{2,0},{3,1},{4,6},{5,7},{6,4},{7,5},{8,10},{9,11},{10,... | collective-permute-start | bytes 2359304 | tf_op jit(solution)/shard_map/ppermute | solution.py:44
  13.2 19.6 %collective-permute-start.3 = (bf16[1,96,576]{1,2,0:T(8,128)(2,1)S(1)}, bf16[1,96,576]{1,2,0:T(8,128)(2,1)S(1)}, u32[]{:S(2)}, u32[]{:S(2)}) collective-permute-start(bf16[1,96,576]{1,2,0:T(8,128)(2,1)S(1)} %bitcast.389), channel_id=1, source_target_pairs={{0,16},{4,20},{8,24},{12,28},{16,0},{20,4},{24,8},{28,12},{1,17},{... | collective-permute-start | bytes 331784 | tf_op jit(solution)/shard_map/ppermute | solution.py:44
  13.6 37.0 %collective-permute-start.18 = (bf16[1,96,768]{2,1,0:T(8,128)(2,1)S(1)}, bf16[1,96,768]{2,1,0:T(8,128)(2,1)S(1)}, u32[]{:S(2)}, u32[]{:S(2)}) collective-permute-start(bf16[1,96,768]{2,1,0:T(8,128)(2,1)S(1)} %bitcast.410), channel_id=1, source_target_pairs={{0,16},{4,20},{8,24},{12,28},{16,0},{20,4},{24,8},{28,12},{1,17},{... | collective-permute-start | bytes 442376 | tf_op jit(solution)/shard_map/ppermute | solution.py:44
  32.8 20.0 %collective-permute-start.8 = (bf16[4,96,192]{2,1,0:T(8,128)(2,1)S(1)}, bf16[4,96,192]{2,1,0:T(8,128)(2,1)S(1)}, u32[]{:S(2)}, u32[]{:S(2)}) collective-permute-start(bf16[4,96,192]{2,1,0:T(8,128)(2,1)S(1)} %bitcast.403), channel_id=1, source_target_pairs={{0,4},{4,0},{8,12},{12,8},{16,20},{20,16},{24,28},{28,24},{1,5},{5... | collective-permute-start | bytes 442376 | tf_op jit(solution)/shard_map/ppermute | solution.py:44
  55.8 75.4 %collective-permute-start.28 = (bf16[512,768]{1,0:T(8,128)(2,1)}, bf16[512,768]{1,0:T(8,128)(2,1)}, u32[]{:S(2)}, u32[]{:S(2)}) collective-permute-start(bf16[512,768]{1,0:T(8,128)(2,1)} %get-tuple-element.174), channel_id=1, source_target_pairs={{0,2},{1,3},{2,0},{3,1},{4,6},{5,7},{6,4},{7,5},{8,10},{9,11},{10,... | collective-permute-start | bytes 2359304 | tf_op jit(solution)/shard_map/ppermute | solution.py:44
  62.9 64.0 %collective-permute-start.19 = (bf16[2,96,768]{2,1,0:T(8,128)(2,1)}, bf16[2,96,768]{2,1,0:T(8,128)(2,1)}, u32[]{:S(2)}, u32[]{:S(2)}) collective-permute-start(bf16[2,96,768]{2,1,0:T(8,128)(2,1)} %maximum_select_fusion.8), channel_id=1, source_target_pairs={{0,8},{4,12},{8,0},{12,4},{16,24},{20,28},{24,16},{28,20},{1,9},{5... | collective-permute-start | bytes 884744 | tf_op jit(solution)/shard_map/ppermute | solution.py:44
  68.4 46.4 %collective-permute-start.10 = (bf16[768,192]{0,1:T(8,128)(2,1)}, bf16[768,192]{0,1:T(8,128)(2,1)}, u32[]{:S(2)}, u32[]{:S(2)}) collective-permute-start(bf16[768,192]{0,1:T(8,128)(2,1)} %select_n.382), channel_id=1, source_target_pairs={{0,1},{1,0},{2,3},{3,2},{4,5},{5,4},{6,7},{7,6},{8,9},{9,8},{10,11... | collective-permute-start | bytes 884744 | tf_op jit(solution)/shard_map/ppermute | solution.py:44
  69.1 49.0 %collective-permute-start.14 = (bf16[768,192]{0,1:T(8,128)(2,1)}, bf16[768,192]{0,1:T(8,128)(2,1)S(1)}, u32[]{:S(2)}, u32[]{:S(2)}) collective-permute-start(bf16[768,192]{0,1:T(8,128)(2,1)} %copy-done.51), channel_id=1, source_target_pairs={{0,1},{1,0},{2,3},{3,2},{4,5},{5,4},{6,7},{7,6},{8,9},{9,8},{10,11... | collective-permute-start | bytes 884744 | tf_op jit(solution)/shard_map/ppermute | solution.py:44
  126.4 21.2 %collective-permute-start.16 = (bf16[512,768]{1,0:T(8,128)(2,1)}, bf16[512,768]{1,0:T(8,128)(2,1)}, u32[]{:S(2)}, u32[]{:S(2)}) collective-permute-start(bf16[512,768]{1,0:T(8,128)(2,1)} %add_convert_fusion.3), channel_id=1, source_target_pairs={{0,2},{1,3},{2,0},{3,1},{4,6},{5,7},{6,4},{7,5},{8,10},{9,11},{10,... | collective-permute-start | bytes 2359304 | tf_op jit(solution)/shard_map/ppermute | solution.py:44
  129.8 29.7 %collective-permute-start.27 = (bf16[512,768]{1,0:T(8,128)(2,1)}, bf16[512,768]{1,0:T(8,128)(2,1)}, u32[]{:S(2)}, u32[]{:S(2)}) collective-permute-start(bf16[512,768]{1,0:T(8,128)(2,1)} %get-tuple-element.174), channel_id=1, source_target_pairs={{0,1},{1,0},{2,3},{3,2},{4,5},{5,4},{6,7},{7,6},{8,9},{9,8},{10,11... | collective-permute-start | bytes 2359304 | tf_op jit(solution)/shard_map/ppermute | solution.py:44
  131.2 28.4 %collective-permute-start.29 = (bf16[512,768]{1,0:T(8,128)(2,1)}, bf16[512,768]{1,0:T(8,128)(2,1)}, u32[]{:S(2)}, u32[]{:S(2)}) collective-permute-start(bf16[512,768]{1,0:T(8,128)(2,1)} %collective-permute-done.28), channel_id=1, source_target_pairs={{0,1},{1,0},{2,3},{3,2},{4,5},{5,4},{6,7},{7,6},{8,9},{9,8},{10,11... | collective-permute-start | bytes 2359304 | tf_op jit(solution)/shard_map/ppermute | solution.py:44
  165.6 30.8 %collective-permute-start.60 = (bf16[4,96,768]{2,1,0:T(8,128)(2,1)}, bf16[4,96,768]{2,1,0:T(8,128)(2,1)}, u32[]{:S(2)}, u32[]{:S(2)}) collective-permute-start(bf16[4,96,768]{2,1,0:T(8,128)(2,1)} %fusion.112), channel_id=1, source_target_pairs={{0,4},{4,0},{8,12},{12,8},{16,20},{20,16},{24,28},{28,24},{1,5},{5... | collective-permute-start | bytes 1769480 | tf_op jit(solution)/shard_map/ppermute | solution.py:44
  189.8 54.3 %collective-permute-start.24 = (bf16[512,768]{1,0:T(8,128)(2,1)}, bf16[512,768]{1,0:T(8,128)(2,1)}, u32[]{:S(2)}, u32[]{:S(2)}) collective-permute-start(bf16[512,768]{1,0:T(8,128)(2,1)} %get-tuple-element.191), channel_id=1, source_target_pairs={{0,1},{1,0},{2,3},{3,2},{4,5},{5,4},{6,7},{7,6},{8,9},{9,8},{10,11... | collective-permute-start | bytes 2359304 | tf_op jit(solution)/shard_map/ppermute | solution.py:44
  196.1 36.3 %collective-permute-start.30 = (bf16[512,768]{1,0:T(8,128)(2,1)}, bf16[512,768]{1,0:T(8,128)(2,1)}, u32[]{:S(2)}, u32[]{:S(2)}) collective-permute-start(bf16[512,768]{1,0:T(8,128)(2,1)} %get-tuple-element.189), channel_id=1, source_target_pairs={{0,1},{1,0},{2,3},{3,2},{4,5},{5,4},{6,7},{7,6},{8,9},{9,8},{10,11... | collective-permute-start | bytes 2359304 | tf_op jit(solution)/shard_map/ppermute | solution.py:44
  207.4 36.7 %collective-permute-start.26 = (bf16[512,768]{1,0:T(8,128)(2,1)S(1)}, bf16[512,768]{1,0:T(8,128)(2,1)S(1)}, u32[]{:S(2)}, u32[]{:S(2)}) collective-permute-start(bf16[512,768]{1,0:T(8,128)(2,1)S(1)} %add_convert_fusion.2), channel_id=1, source_target_pairs={{0,2},{1,3},{2,0},{3,1},{4,6},{5,7},{6,4},{7,5},{8,10},{9,11},{10,... | collective-permute-start | bytes 2359304 | tf_op jit(solution)/shard_map/ppermute | solution.py:44
  212.6 29.4 %collective-permute-start.32 = (bf16[512,768]{1,0:T(8,128)(2,1)S(1)}, bf16[512,768]{1,0:T(8,128)(2,1)S(1)}, u32[]{:S(2)}, u32[]{:S(2)}) collective-permute-start(bf16[512,768]{1,0:T(8,128)(2,1)S(1)} %add_convert_fusion.1), channel_id=1, source_target_pairs={{0,2},{1,3},{2,0},{3,1},{4,6},{5,7},{6,4},{7,5},{8,10},{9,11},{10,... | collective-permute-start | bytes 2359304 | tf_op jit(solution)/shard_map/ppermute | solution.py:44
  252.6 24.7 %collective-permute-start.33 = (bf16[512,192]{0,1:T(8,128)(2,1)S(1)}, bf16[512,192]{0,1:T(8,128)(2,1)S(1)}, u32[]{:S(2)}, u32[]{:S(2)}) collective-permute-start(bf16[512,192]{0,1:T(8,128)(2,1)S(1)} %convolution_convert_fusion.9), channel_id=1, source_target_pairs={{0,1},{1,0},{2,3},{3,2},{4,5},{5,4},{6,7},{7,6},{8,9},{9,8},{10,11... | collective-permute-start | bytes 589832 | tf_op jit(solution)/shard_map/ppermute | solution.py:44
  253.6 23.7 %collective-permute-start.34 = (bf16[512,192]{0,1:T(8,128)(2,1)S(1)}, bf16[512,192]{0,1:T(8,128)(2,1)S(1)}, u32[]{:S(2)}, u32[]{:S(2)}) collective-permute-start(bf16[512,192]{0,1:T(8,128)(2,1)S(1)} %convolution_convert_fusion.8), channel_id=1, source_target_pairs={{0,2},{1,3},{2,0},{3,1},{4,6},{5,7},{6,4},{7,5},{8,10},{9,11},{10,... | collective-permute-start | bytes 589832 | tf_op jit(solution)/shard_map/ppermute | solution.py:44
  256.2 21.2 %collective-permute-start.35 = (bf16[512,192]{0,1:T(8,128)(2,1)S(1)}, bf16[512,192]{0,1:T(8,128)(2,1)S(1)}, u32[]{:S(2)}, u32[]{:S(2)}) collective-permute-start(bf16[512,192]{0,1:T(8,128)(2,1)S(1)} %convolution_convert_fusion.7), channel_id=1, source_target_pairs={{0,3},{1,2},{2,1},{3,0},{4,7},{5,6},{6,5},{7,4},{8,11},{9,10},{10,... | collective-permute-start | bytes 589832 | tf_op jit(solution)/shard_map/ppermute | solution.py:44
  264.1 77.1 %collective-permute-start.48 = (bf16[768,192]{0,1:T(8,128)(2,1)}, bf16[768,192]{0,1:T(8,128)(2,1)}, u32[]{:S(2)}, u32[]{:S(2)}) collective-permute-start(bf16[768,192]{0,1:T(8,128)(2,1)} %convolution_convert_fusion.3), channel_id=1, source_target_pairs={{0,3},{1,2},{2,1},{3,0},{4,7},{5,6},{6,5},{7,4},{8,11},{9,10},{10,... | collective-permute-start | bytes 884744 | tf_op jit(solution)/shard_map/ppermute | solution.py:44
  275.2 66.1 %collective-permute-start.47 = (bf16[768,192]{0,1:T(8,128)(2,1)}, bf16[768,192]{0,1:T(8,128)(2,1)}, u32[]{:S(2)}, u32[]{:S(2)}) collective-permute-start(bf16[768,192]{0,1:T(8,128)(2,1)} %convolution_convert_fusion.4), channel_id=1, source_target_pairs={{0,2},{1,3},{2,0},{3,1},{4,6},{5,7},{6,4},{7,5},{8,10},{9,11},{10,... | collective-permute-start | bytes 884744 | tf_op jit(solution)/shard_map/ppermute | solution.py:44
  277.3 64.0 %collective-permute-start.46 = (bf16[768,192]{0,1:T(8,128)(2,1)}, bf16[768,192]{0,1:T(8,128)(2,1)}, u32[]{:S(2)}, u32[]{:S(2)}) collective-permute-start(bf16[768,192]{0,1:T(8,128)(2,1)} %convolution_convert_fusion.5), channel_id=1, source_target_pairs={{0,1},{1,0},{2,3},{3,2},{4,5},{5,4},{6,7},{7,6},{8,9},{9,8},{10,11... | collective-permute-start | bytes 884744 | tf_op jit(solution)/shard_map/ppermute | solution.py:44
  336.2 33.0 %collective-permute-start.36 = (bf16[2,512,768]{2,1,0:T(8,128)(2,1)}, bf16[2,512,768]{2,1,0:T(8,128)(2,1)}, u32[]{:S(2)}, u32[]{:S(2)}) collective-permute-start(bf16[2,512,768]{2,1,0:T(8,128)(2,1)} %dynamic-slice_bitcast_fusion), channel_id=1, source_target_pairs={{0,1},{1,0},{2,3},{3,2},{4,5},{5,4},{6,7},{7,6},{8,9},{9,8},{10,11... | collective-permute-start | bytes 4718600 | tf_op jit(solution)/shard_map/ppermute | solution.py:44
  (150 other events, 1229.6 us)

commit v2 on v1

v2 whole, which is shorter than its diff:
```python
import functools

import jax
import jax.numpy as jnp
from jax import lax
from jax.experimental import pallas as pl
from jax.experimental.pallas import tpu as pltpu
from jax.sharding import PartitionSpec as P

HS = 64
BLK = 128


EPSILON = 1e-05
MASKED = -1e30
GELU_SCALE = 0.7978845608028654

BF = jnp.bfloat16
F32 = jnp.float32


def segment_ids(lengths, capacity):
    padded = (lengths + BLK - 1) // BLK * BLK
    starts = jnp.cumsum(padded, axis=1) - padded
    places = jnp.arange(capacity, dtype=jnp.int32)
    inside = (places[None, None, :] >= starts[:, :, None]) & (
        places[None, None, :] < (starts + lengths)[:, :, None]
    )
    labels = jnp.arange(lengths.shape[1], dtype=jnp.int32)[None, :, None] + 1
    return jnp.sum(jnp.where(inside, labels, 0), axis=1) - 1


def swap(value, axis, bits):
    size = lax.axis_size(axis)
    return lax.ppermute(value, axis, [(i, i ^ bits) for i in range(size)])


def bits_of(axis):
    size = lax.axis_size(axis)
    count = size.bit_length() - 1
    assert 1 << count == size
    return [1 << b for b in range(count)]


def after(value, *others):
    return lax.optimization_barrier((value, *others))[0]


def gather_step(full, axis, bit, other=None):
    high = (lax.axis_index(axis) & bit) > 0
    other = swap(full, axis, bit) if other is None else other
    return jnp.where(
        high, jnp.stack([other, full], 1), jnp.stack([full, other], 1)
    ).reshape(-1, *full.shape[1:])


def exchange(blocks, axis):
    return [b if r == 0 else swap(b, axis, r) for r, b in enumerate(blocks)]


def everyone_sum(value, axes):
    for axis in axes:
        for bit in bits_of(axis):
            value = value + swap(value, axis, bit)
    return value


def first_keys(seg, slots):
    places = jnp.arange(seg.shape[0], dtype=jnp.int32)
    begins = jnp.where(seg != jnp.concatenate([jnp.full((1,), -2, jnp.int32), seg[:-1]]), places, 0)
    labels = jnp.arange(slots, dtype=jnp.int32)
    starts = jnp.sum(jnp.where((seg[None] == labels[:, None]), begins[None], 0), axis=1)
    mine = jnp.sum(jnp.where(seg[:, None] == labels[None], starts[None], 0), axis=1)
    return jnp.where(seg >= 0, mine, places)


def nt(a, b):
    return lax.dot_general(a, b, (((1,), (1,)), ((), ())), preferred_element_type=F32)


def nn(a, b):
    return lax.dot_general(a, b, (((1,), (0,)), ((), ())), preferred_element_type=F32)


def tn(a, b):
    return lax.dot_general(a, b, (((0,), (0,)), ((), ())), preferred_element_type=F32)


def rows_at(block, size):
    return pl.ds(pl.multiple_of(block * size, size), size)


def masked_scores(keys, queries, low, first_key, first_query):
    scores = nt(keys, queries)
    key_at = lax.broadcasted_iota(jnp.int32, scores.shape, 0) + first_key
    query_at = lax.broadcasted_iota(jnp.int32, (1, scores.shape[1]), 1) + first_query
    return jnp.where((key_at >= low) & (key_at <= query_at), scores, MASKED)


def forward_kernel(heads, block, here_ref, start_ref, low_ref, *refs):
    count = here_ref.shape[0] - 1
    token_refs = refs[:count]
    weight_ref, bias_ref, gain_ref, shift_ref = refs[count : count + 4]
    (h1_ref, hat_ref, q_ref, k_ref, v_ref, out_ref, lse_ref, send_ref) = refs[count + 4 :]
    here = here_ref[count]
    local_rows = token_refs[0].shape[0]
    chunk = 256
    for r in range(count):

        def project(step, carry, r=r):
            base = pl.multiple_of((here_ref[r]) * local_rows + step * chunk, chunk)
            rows = token_refs[r][rows_at(step, chunk), :].astype(F32)
            centre = rows - jnp.mean(rows, axis=-1, keepdims=True)
            spread = jnp.mean(centre * centre, axis=-1, keepdims=True)
            hat = centre * lax.rsqrt(spread + EPSILON)
            h1 = (hat * gain_ref[...] + shift_ref[...]).astype(BF)
            hat_ref[pl.ds(base, chunk), :] = hat.astype(BF)
            h1_ref[pl.ds(base, chunk), :] = h1
            qkv = (nn(h1, weight_ref[...]) + bias_ref[...]).astype(BF)
            for h in range(heads):
                at = 3 * h * HS
                q_ref[h, pl.ds(base, chunk), :] = qkv[:, at : at + HS] * HS ** (-0.5)
                k_ref[h, pl.ds(base, chunk), :] = qkv[:, at + HS : at + 2 * HS]
                v_ref[h, pl.ds(base, chunk), :] = qkv[:, at + 2 * HS : at + 3 * HS]
            return carry

        lax.fori_loop(0, local_rows // chunk, project, 0)

    blocks = q_ref.shape[1] // block

    def query_step(i, carry):
        low = low_ref[0:1, rows_at(i, block)]

        def key_step(j, state):
            fresh = []
            for h in range(heads):
                peak, total, acc = state[3 * h : 3 * h + 3]
                scores = masked_scores(
                    k_ref[h, rows_at(j, block), :],
                    q_ref[h, rows_at(i, block), :],
                    low,
                    j * block,
                    i * block,
                )
                peak_now = jnp.maximum(peak, jnp.max(scores, axis=0, keepdims=True))
                decay = jnp.exp(peak - peak_now)
                weights = jnp.exp(scores - peak_now)
                total = total * decay + jnp.sum(weights, axis=0, keepdims=True)
                acc = acc * decay + tn(v_ref[h, rows_at(j, block), :], weights.astype(BF))
                fresh += [peak_now, total, acc]
            return tuple(fresh)

        init = (
            jnp.full((1, block), MASKED, F32),
            jnp.zeros((1, block), F32),
            jnp.zeros((HS, block), F32),
        ) * heads
        state = lax.fori_loop(start_ref[i], i + 1, key_step, init)
        slot = lax.bitwise_xor(i, here)
        for h in range(heads):
            peak, total, acc = state[3 * h : 3 * h + 3]
            rows = acc / total
            out_ref[h, :, rows_at(i, block)] = rows
            lse_ref[h, :, rows_at(i, block)] = peak + jnp.log(total)
            send_ref[slot, h * HS : (h + 1) * HS, :] = rows.astype(BF)
        return carry

    lax.fori_loop(0, blocks, query_step, 0)


def attention_forward(blocks, weight, bias, gain, shift, low, starts, order, heads):
    rows, width = blocks[0].shape
    count = len(blocks)
    total = rows * count
    flops = 2 * total * width * weight.shape[1] + 2 * heads * total * total * HS
    return pl.pallas_call(
        functools.partial(forward_kernel, heads, rows),
        out_shape=(
            shape((total, width), BF),
            shape((total, width), BF),
            shape((heads, total, HS), BF),
            shape((heads, total, HS), BF),
            shape((heads, total, HS), BF),
            shape((heads, HS, total), F32),
            shape((heads, 1, total), F32),
            shape((count, heads * HS, rows), BF),
        ),
        in_specs=[pl.BlockSpec(memory_space=pltpu.SMEM)] * 2
        + [pl.BlockSpec(memory_space=pltpu.VMEM)] * (count + 5),
        out_specs=[pl.BlockSpec(memory_space=pltpu.VMEM)] * 8,
        compiler_params=pltpu.CompilerParams(vmem_limit_bytes=60000 * 1024),
        cost_estimate=pl.CostEstimate(
            flops=flops, bytes_accessed=24 << 20, transcendentals=heads * total * total // 2
        ),
        name="attention_forward",
    )(order, starts, low, *blocks, weight, bias, gain, shift)


def backward_kernel(
    first_head, heads, block, start_ref, order_ref, low_ref, q_ref, k_ref, v_ref, out_ref, lse_ref, *refs
):
    count = order_ref.shape[0] - 1
    grad_refs = refs[:count]
    result_ref = refs[count]
    grad_t_ref, grad_ref, centre_ref, dk_ref, dv_ref, kt_ref, dq_ref = refs[count + 1 :]
    for r in range(count):
        for h in range(heads):
            whole = first_head + h
            piece = grad_refs[r][whole * HS : (whole + 1) * HS, :]
            at = rows_at(order_ref[r], block)
            grad_t_ref[h, :, at] = piece
            grad_ref[h, at, :] = piece.T
            centre_ref[h, :, at] = jnp.sum(
                piece.astype(F32) * out_ref[whole, :, at], axis=0, keepdims=True
            )
            kt_ref[h, :, r * block : (r + 1) * block] = k_ref[
                whole, r * block : (r + 1) * block, :
            ].T
    dk_ref[...] = jnp.zeros_like(dk_ref)
    dv_ref[...] = jnp.zeros_like(dv_ref)
    blocks = q_ref.shape[1] // block

    def query_step(i, carry):
        here = rows_at(i, block)
        low = low_ref[0:1, here]

        def key_step(j, state):
            there = rows_at(j, block)
            fresh = []
            for h in range(heads):
                whole = first_head + h
                queries = q_ref[whole, here, :]
                scores = masked_scores(k_ref[whole, there, :], queries, low, j * block, i * block)
                probs = jnp.exp(scores - lse_ref[whole, :, here])
                grad_probs = nn(v_ref[whole, there, :], grad_t_ref[h, :, here])
                grad_scores = (probs * (grad_probs - centre_ref[h, :, here])).astype(BF)
                dv_ref[h, there, :] += nn(probs.astype(BF), grad_ref[h, here, :])
                dk_ref[h, there, :] += nn(grad_scores, queries)
                fresh.append(state[h] + nn(kt_ref[h, :, there], grad_scores))
            return tuple(fresh)

        state = lax.fori_loop(
            start_ref[i], i + 1, key_step, (jnp.zeros((HS, block), F32),) * heads
        )
        for h in range(heads):
            dq_ref[h, here, :] = (state[h] * HS ** (-0.5)).T.astype(BF)
        return carry

    lax.fori_loop(0, blocks, query_step, 0)

    def finish(i, carry):
        here = rows_at(i, block)
        pieces = []
        for h in range(heads):
            pieces += [dq_ref[h, here, :], dk_ref[h, here, :].astype(BF), dv_ref[h, here, :].astype(BF)]
        result_ref[here, :] = jnp.concatenate(pieces, axis=1)
        return carry

    lax.fori_loop(0, blocks, finish, 0)


def vmem(count):
    return [pl.BlockSpec(memory_space=pltpu.VMEM)] * count


def smem(count):
    return [pl.BlockSpec(memory_space=pltpu.SMEM)] * count


def kernel_call(body, name, out_shape, scalars, arrays, flops, scratch=(), transcendentals=0):
    moved = sum(a.size * a.dtype.itemsize for a in arrays) + sum(
        o.size * jnp.dtype(o.dtype).itemsize for o in out_shape
    )
    return pl.pallas_call(
        body,
        out_shape=tuple(out_shape),
        in_specs=smem(len(scalars)) + vmem(len(arrays)),
        out_specs=vmem(len(out_shape)),
        scratch_shapes=list(scratch),
        compiler_params=pltpu.CompilerParams(vmem_limit_bytes=60000 * 1024),
        cost_estimate=pl.CostEstimate(
            flops=flops, bytes_accessed=moved, transcendentals=transcendentals
        ),
        name=name,
    )(*scalars, *arrays)


def shape(dims, kind):
    return jax.ShapeDtypeStruct(dims, kind)


def attention_backward(first_head, heads, q, k, v, out, lse, grads, low, starts, order):
    total = q.shape[1]
    rows = total // len(grads)
    return kernel_call(
        functools.partial(backward_kernel, first_head, heads, rows),
        "attention_backward",
        [shape((total, 3 * HS * heads), BF)],
        [starts, order],
        [low, q, k, v, out, lse, *grads],
        5 * heads * total * total * HS,
        [
            pltpu.VMEM((heads, HS, total), BF),
            pltpu.VMEM((heads, total, HS), BF),
            pltpu.VMEM((heads, 1, total), F32),
            pltpu.VMEM((heads, total, HS), F32),
            pltpu.VMEM((heads, total, HS), F32),
            pltpu.VMEM((heads, HS, total), BF),
            pltpu.VMEM((heads, total, HS), BF),
        ],
        heads * total * total // 2,
    )


def normalised(rows):
    centre = rows - jnp.mean(rows, axis=-1, keepdims=True)
    spread = jnp.mean(centre * centre, axis=-1, keepdims=True)
    scale = lax.rsqrt(spread + EPSILON)
    return centre * scale, scale


def norm_back(grad, gain, hat, scale):
    e = grad * gain
    return scale * (
        e - jnp.mean(e, axis=-1, keepdims=True) - hat * jnp.mean(e * hat, axis=-1, keepdims=True)
    )


def branch_kernel(count, *refs):
    att_refs, weight_refs = refs[:count], refs[count : 2 * count]
    token_ref, bias_ref, gain_ref, shift_ref, middle_ref, h2_ref = refs[2 * count :]
    branch = bias_ref[...]
    for att, weight in zip(att_refs, weight_refs, strict=True):
        branch = branch + nn(att[...].T, weight[...])
    middle = token_ref[...].astype(F32) + branch
    middle_ref[...] = middle
    hat, _ = normalised(middle)
    h2_ref[...] = (hat * gain_ref[...] + shift_ref[...]).astype(BF)


def hidden_kernel(count, chunk, *refs):
    h2_refs, grad_refs = refs[:count], refs[count : 2 * count]
    fc_ref, proj_ref, bias_ref = refs[2 * count : 2 * count + 3]
    rest = refs[2 * count + 3 :]
    back_refs, act_refs, pre_refs, sum_ref = rest[:count], rest[count : 2 * count], rest[2 * count : 3 * count], rest[3 * count]
    sum_ref[...] = jnp.zeros_like(sum_ref)
    for r in range(count):

        def step(i, carry, r=r):
            at = rows_at(i, chunk)
            u = nn(h2_refs[r][at, :], fc_ref[...]) + bias_ref[...]
            grad_act = nn(grad_refs[r][at, :], proj_ref[...])
            square = u * u
            bend = jnp.tanh(GELU_SCALE * (u + 0.044715 * square * u))
            act_refs[r][at, :] = (0.5 * u * (1.0 + bend)).astype(BF)
            slope = 0.5 * (1.0 + bend) + 0.5 * u * (1.0 - bend * bend) * GELU_SCALE * (
                1.0 + 3.0 * 0.044715 * square
            )
            grad_pre = (grad_act * slope).astype(BF)
            pre_refs[r][at, :] = grad_pre
            sum_ref[...] += jnp.sum(grad_pre.astype(F32), axis=0, keepdims=True)
            back_refs[r][at, :] = nt(grad_pre, fc_ref[...]).astype(BF)
            return carry

        lax.fori_loop(0, h2_refs[r].shape[0] // chunk, step, 0)


def hidden(h2s, grads, fc, proj, bias):
    count = len(h2s)
    rows, width = h2s[0].shape
    cols = fc.shape[1]
    return kernel_call(
        functools.partial(hidden_kernel, count, 256),
        "hidden",
        [shape((rows, width), BF)] * count
        + [shape((rows, cols), BF)] * (2 * count)
        + [shape((1, cols), F32)],
        [],
        [*h2s, *grads, fc, proj, bias],
        6 * count * rows * width * cols,
        transcendentals=count * rows * cols,
    )


def split_store(value, keep_ref, give_ref, high, lanes):
    pairs, rows, _ = keep_ref.shape
    for p in range(pairs):
        lower = value[2 * p * rows : (2 * p + 1) * rows, :]
        upper = value[(2 * p + 1) * rows : (2 * p + 2) * rows, :]
        keep_ref[p, :, lanes] = jnp.where(high, upper, lower)
        give_ref[p, :, lanes] = jnp.where(high, lower, upper).astype(BF)


def weight_kernel(count, high_ref, *refs):
    left_refs, right_refs = refs[:count], refs[count : 2 * count]
    keep_ref, give_ref = refs[2 * count :]
    total = tn(left_refs[0][...], right_refs[0][...])
    for r in range(1, count):
        total = total + tn(left_refs[r][...], right_refs[r][...])
    split_store(total, keep_ref, give_ref, high_ref[0] > 0, slice(0, total.shape[1]))


def hidden_weights(lefts, rights, high, dp_size):
    rows, width = lefts[0].shape
    cols = rights[0].shape[1]
    dims = (dp_size // 2, width // dp_size, cols)
    return kernel_call(
        functools.partial(weight_kernel, len(lefts)),
        "hidden_weights",
        [shape(dims, F32), shape(dims, BF)],
        [high],
        [*lefts, *rights],
        2 * len(lefts) * rows * width * cols,
    )


def project_kernel(count, *refs):
    act_refs, proj_ref, out_refs = refs[:count], refs[count], refs[count + 1 :]
    for act, out in zip(act_refs, out_refs, strict=True):
        out[...] = nt(act[...], proj_ref[...]).astype(BF)


def project(acts, proj):
    rows, cols = acts[0].shape
    width = proj.shape[0]
    return kernel_call(
        functools.partial(project_kernel, len(acts)),
        "project",
        [shape((rows, width), BF)] * len(acts),
        [],
        [*acts, proj],
        2 * len(acts) * rows * cols * width,
    )


def middle_kernel(count, middle_ref, live_grad_ref, own_ref, near_ref, far_ref, gain_ref, *refs):
    weight_refs = refs[:count]
    grad_ref, branch_ref, sums_ref = refs[count : count + 3]
    att_refs = refs[count + 3 :]
    hat, scale = normalised(middle_ref[...])
    grad = own_ref[...].astype(F32) + near_ref[...].astype(F32) + far_ref[...].astype(F32)
    here = live_grad_ref[...].astype(F32)
    total = here + norm_back(grad, gain_ref[...], hat, scale)
    grad_ref[...] = total
    branch = total.astype(BF)
    branch_ref[...] = branch
    sums_ref[0:1, :] = jnp.sum(branch.astype(F32), axis=0, keepdims=True)
    sums_ref[1:2, :] = jnp.sum(grad * hat, axis=0, keepdims=True)
    sums_ref[2:3, :] = jnp.sum(grad, axis=0, keepdims=True)
    sums_ref[3:4, :] = jnp.sum(here, axis=0, keepdims=True)
    for weight, att in zip(weight_refs, att_refs, strict=True):
        att[...] = nt(branch, weight[...]).T.astype(BF)


def out_weight_kernel(count, branch_ref, *refs):
    for att, out in zip(refs[:count], refs[count:], strict=True):
        out[...] = nn(att[...], branch_ref[...]).astype(BF)


def first_kernel(order_ref, hat_ref, weight_ref, part_ref, keep_ref, give_ref, sums_ref, bias_ref):
    count, rows = 2 * keep_ref.shape[0], keep_ref.shape[1]
    sums_ref[...] = jnp.zeros_like(sums_ref)
    bias_ref[...] = jnp.zeros_like(bias_ref)

    def block(r):
        at = rows_at(order_ref[r], rows)
        part = part_ref[at, :]
        bias_ref[...] += jnp.sum(part.astype(F32), axis=0, keepdims=True)
        total = nt(part, weight_ref[...])
        sums_ref[0:1, :] += jnp.sum(total * hat_ref[at, :].astype(F32), axis=0, keepdims=True)
        sums_ref[1:2, :] += jnp.sum(total, axis=0, keepdims=True)
        return total.astype(BF)

    def pair(p, carry):
        give_ref[p] = block(2 * p + 1)
        keep_ref[p] = block(2 * p)
        return carry

    lax.fori_loop(0, count // 2, pair, 0)


def qkv_weight_kernel(count, high_ref, h1_ref, part_ref, *refs):
    out_refs = refs[:count]
    keep_ref, give_ref = refs[count:]
    high = high_ref[0] > 0
    cols = part_ref.shape[1]
    split_store(tn(h1_ref[...], part_ref[...]), keep_ref, give_ref, high, slice(0, cols))
    total = out_refs[0][...].astype(F32).T
    split_store(total, keep_ref, give_ref, high, slice(cols, cols + total.shape[1]))


def qkv_weights(h1, part, outs, high, dp_size):
    total, width = h1.shape
    dims = (dp_size // 2, width // dp_size, part.shape[1] + outs[0].shape[0])
    return kernel_call(
        functools.partial(qkv_weight_kernel, len(outs)),
        "qkv_weights",
        [shape(dims, F32), shape(dims, BF)],
        [high],
        [h1, part, *outs],
        2 * total * width * part.shape[1],
    )


def halve_kernel(high_ref, keep_ref, got_ref, keep_out, give_out):
    high = high_ref[0] > 0
    for p in range(keep_out.shape[0]):
        lower = keep_ref[2 * p] + got_ref[2 * p].astype(F32)
        upper = keep_ref[2 * p + 1] + got_ref[2 * p + 1].astype(F32)
        keep_out[p] = jnp.where(high, upper, lower)
        give_out[p] = jnp.where(high, lower, upper).astype(BF)


def halve(keep, got, axis, bit):
    dims = (keep.shape[0] // 2, *keep.shape[1:])
    high = jnp.reshape((lax.axis_index(axis) & bit) // bit, (1,)).astype(jnp.int32)
    return kernel_call(
        halve_kernel,
        "halve",
        [shape(dims, F32), shape(dims, BF)],
        [high],
        [keep, got],
        3 * keep.size,
    )


def token_kernel(token_ref, gain_ref, own_ref, near_ref, far_ref, middle_ref, out_ref):
    hat, scale = normalised(token_ref[...].astype(F32))
    grad = own_ref[...].astype(F32) + near_ref[...].astype(F32) + far_ref[...].astype(F32)
    out_ref[...] = (middle_ref[...] + norm_back(grad, gain_ref[...], hat, scale)).astype(BF)


def per_device(
    tokens,
    seq_lengths,
    norm1_gain,
    norm1_shift,
    qkv_weight,
    qv_bias,
    out_weight,
    out_bias,
    norm2_gain,
    norm2_shift,
    fc_weight,
    fc_bias,
    proj_weight,
    proj_bias,
    out_grad,
):
    tensor_size = lax.axis_size("tensor")
    assert tensor_size == 4
    near, far = 1, 2
    dp_size = lax.axis_size("dp")
    tensor_pos = lax.axis_index("tensor")
    local_rows, model_width = tokens.shape
    capacity = local_rows * tensor_size
    shard_rows = qkv_weight.shape[0]
    head_cols = qkv_weight.shape[2]
    heads = head_cols // HS
    hidden_cols = fc_weight.shape[1]
    high = jnp.reshape(lax.axis_index("dp") & 1, (1,)).astype(jnp.int32)

    def row(vector):
        return vector.reshape(1, -1)

    qkv_heads = qkv_weight.reshape(shard_rows, 3, heads, HS).transpose(0, 2, 1, 3)
    ahead = jnp.concatenate([qkv_heads.reshape(shard_rows, -1), out_weight.T], 1)[None]
    later = jnp.concatenate([fc_weight, proj_weight.T], 1)[None]
    far_tokens = swap(tokens, "tensor", far)
    dp_bits = bits_of("dp")[::-1]
    for k, bit in enumerate(dp_bits):
        if k == len(dp_bits) - 1:
            ahead = after(ahead, far_tokens)
        ahead = gather_step(ahead, "dp", bit)
        if k == len(dp_bits) - 2:
            for early in dp_bits[:-2]:
                later = gather_step(after(later, ahead), "dp", early)
    ahead = ahead.reshape(model_width, -1)
    later_far = swap(after(later, ahead), "dp", dp_bits[-2])
    full_qkv = ahead[:, : 3 * head_cols]
    out_turned = ahead[:, 3 * head_cols :].T
    outs = exchange([out_turned] * tensor_size, "tensor")
    near_tokens = swap(tokens, "tensor", near)
    last_tokens = swap(far_tokens, "tensor", near)
    token_blocks = [tokens, near_tokens, far_tokens, last_tokens]

    seg = segment_ids(seq_lengths, capacity)[0]
    live_here = lax.dynamic_slice_in_dim(seg, tensor_pos * local_rows, local_rows, 0) >= 0
    low = first_keys(seg, seq_lengths.shape[1])
    starts = low.reshape(tensor_size, local_rows)[:, 0] // local_rows
    order = jnp.concatenate(
        [
            lax.bitwise_xor(jnp.arange(tensor_size, dtype=jnp.int32), tensor_pos),
            jnp.reshape(tensor_pos, (1,)).astype(jnp.int32),
        ]
    )
    low = low.reshape(1, capacity)
    grad_mlp = jnp.where(live_here[:, None], out_grad, jnp.zeros_like(out_grad))
    far_grad = swap(after(grad_mlp, far_tokens), "tensor", far)
    near_grad = swap(grad_mlp, "tensor", near)
    token_blocks = after(tuple(token_blocks), far_grad)

    bias_here = lax.dynamic_slice_in_dim(qv_bias, tensor_pos * head_cols, head_cols, 1).reshape(
        2, heads, HS
    )
    bias_row = row(
        jnp.stack([bias_here[0], jnp.zeros((heads, HS), F32), bias_here[1]], 1).reshape(-1)
    )
    first_all, first_hat, queries, key_rows, values, attended, log_total, sends = attention_forward(
        token_blocks,
        full_qkv,
        bias_row,
        row(norm1_gain),
        row(norm1_shift),
        low,
        starts,
        order,
        heads,
    )

    outs = list(after(tuple(outs), sends))
    sends = after(sends, *outs)
    mine = exchange([sends[r] for r in range(tensor_size)], "tensor")
    later = gather_step(later, "dp", dp_bits[-2], after(later_far, sends))
    later = gather_step(later, "dp", dp_bits[-1]).reshape(model_width, -1)
    fc_cols, proj_turned = later[:, :hidden_cols], later[:, hidden_cols:]
    last_grad = swap(after(far_grad, sends), "tensor", near)
    grads = [grad_mlp, near_grad, far_grad, last_grad]
    middle, second_norm = kernel_call(
        functools.partial(branch_kernel, tensor_size),
        "branch",
        [shape((local_rows, model_width), F32), shape((local_rows, model_width), BF)],
        [],
        [*mine, *outs, tokens, row(out_bias), row(norm2_gain), row(norm2_shift)],
        2 * local_rows * model_width * model_width,
    )
    far_second = swap(second_norm, "tensor", far)
    near_second = swap(second_norm, "tensor", near)
    fc_bias_here = row(lax.dynamic_slice_in_dim(fc_bias, tensor_pos * hidden_cols, hidden_cols, 0))
    back_0, back_1, act_0, act_1, pre_0, pre_1, sum_pre_a = hidden(
        [second_norm, near_second], grads[:2], fc_cols, proj_turned, fc_bias_here
    )
    far_second = after(far_second, back_0)
    last_second = swap(far_second, "tensor", near)
    back_2, back_3, act_2, act_3, pre_2, pre_3, sum_pre_b = hidden(
        [far_second, last_second], grads[2:], fc_cols, proj_turned, fc_bias_here
    )
    near_back = swap(back_1, "tensor", near)
    last_back = swap(back_3, "tensor", near)
    chip_back = (back_2.astype(F32) + last_back.astype(F32)).astype(BF)
    far_back = swap(chip_back, "tensor", far)
    act_0, act_1, act_2, act_3, _ = lax.optimization_barrier((act_0, act_1, act_2, act_3, chip_back))
    acts = [act_0, act_1, act_2, act_3]
    pres = [pre_0, pre_1, pre_2, pre_3]
    keep_fc, give_fc = hidden_weights(
        [second_norm, near_second, far_second, last_second], pres, high, dp_size
    )
    got_fc = swap(give_fc, "dp", dp_bits[-1])
    keep_proj, give_proj = hidden_weights(
        [after(grads[0], keep_fc), *grads[1:]], acts, high, dp_size
    )
    got_proj = swap(give_proj, "dp", dp_bits[-1])
    mlp_parts = project(acts, after(proj_turned, keep_proj))
    mlp_near = swap(mlp_parts[1], "tensor", near)
    mlp_last = swap(mlp_parts[3], "tensor", near)
    mlp_far_sum = (mlp_parts[2].astype(F32) + mlp_last.astype(F32)).astype(BF)

    grad_middle, grad_branch, middle_sums, *grad_mine = kernel_call(
        functools.partial(middle_kernel, tensor_size),
        "middle",
        [
            shape((local_rows, model_width), F32),
            shape((local_rows, model_width), BF),
            shape((4, model_width), F32),
        ]
        + [shape((head_cols, local_rows), BF)] * tensor_size,
        [],
        [middle, grad_mlp, back_0, near_back, after(far_back, mlp_parts[0]), row(norm2_gain), *outs],
        2 * local_rows * model_width * model_width,
    )
    grad_attended = exchange(grad_mine, "tensor")
    mlp_far = swap(after(mlp_far_sum, grad_middle), "tensor", far)
    grad_out_parts = kernel_call(
        functools.partial(out_weight_kernel, tensor_size),
        "out_weights",
        [shape((head_cols, model_width), BF)] * tensor_size,
        [],
        [grad_branch, *mine],
        2 * local_rows * model_width * model_width,
    )
    keep_fc, give_fc = halve(keep_fc, after(got_fc, grad_out_parts[0]), "dp", dp_bits[-2])
    got_fc = swap(give_fc, "dp", dp_bits[-2])
    grad_out_parts = exchange(grad_out_parts, "tensor")
    (grad_qkv,) = attention_backward(
        0,
        heads,
        queries,
        key_rows,
        values,
        attended,
        log_total,
        grad_attended,
        after(low, keep_fc),
        starts,
        order,
    )
    grad_out_parts = after(tuple(grad_out_parts), grad_qkv)
    grad_out = sum(g.astype(F32) for g in grad_out_parts).astype(BF)
    grad_qkv = after(grad_qkv, grad_out)

    keep_first, give_first, first_sums, bias_sums = kernel_call(
        first_kernel,
        "first",
        [
            shape((tensor_size // 2, local_rows, model_width), BF),
            shape((tensor_size // 2, local_rows, model_width), BF),
            shape((2, model_width), F32),
            shape((1, 3 * head_cols), F32),
        ],
        [order],
        [first_hat, full_qkv, grad_qkv],
        2 * capacity * model_width * 3 * head_cols,
    )
    got_first = swap(give_first, "tensor", near)
    rest = dp_bits[:-2][::-1]
    got_fc = after(got_fc, keep_first)
    got_proj = after(got_proj, keep_first)
    for bit in rest:
        keep_fc, give_fc = halve(keep_fc, got_fc, "dp", bit)
        got_fc = swap(give_fc, "dp", bit)
    keep_proj, give_proj = halve(keep_proj, got_proj, "dp", dp_bits[-2])
    got_proj = swap(give_proj, "dp", dp_bits[-2])
    keep_qkv, give_qkv = qkv_weights(
        after(first_all, keep_fc, keep_proj), grad_qkv, [grad_out], high, dp_size
    )
    got_qkv = swap(give_qkv, "dp", dp_bits[-1])
    got_first = after(got_first, keep_qkv)
    chip_first = (keep_first[1].astype(F32) + got_first[1].astype(F32)).astype(BF)
    far_first = swap(chip_first, "tensor", far)
    got_proj = after(got_proj, chip_first)
    for bit in rest:
        keep_proj, give_proj = halve(keep_proj, got_proj, "dp", bit)
        got_proj = swap(give_proj, "dp", bit)
    mlp_out = mlp_parts[0].astype(F32) + mlp_near.astype(F32) + mlp_far.astype(F32)
    result = jnp.where(
        after(live_here, keep_proj)[:, None], middle + mlp_out + proj_bias, 0.0
    ).astype(BF)
    got_qkv = after(got_qkv, result)
    for k, bit in enumerate(dp_bits[:-1][::-1]):
        keep_qkv, give_qkv = halve(keep_qkv, got_qkv, "dp", bit)
        got_qkv = swap(give_qkv, "dp", bit)
        if k == 0:
            sum_fc = keep_fc[0] + after(got_fc, keep_qkv)[0].astype(F32)
            sum_proj = (keep_proj[0] + after(got_proj, keep_qkv)[0].astype(F32)).T
    far_first = after(far_first, keep_qkv)
    (grad_tokens,) = kernel_call(
        token_kernel,
        "token_gradient",
        [shape((local_rows, model_width), BF)],
        [],
        [tokens, row(norm1_gain), keep_first[0], got_first[0], far_first, grad_middle],
        0,
    )

    sum_qkv = keep_qkv[0] + after(got_qkv, grad_tokens)[0].astype(F32)
    sum_out = sum_qkv[:, 3 * head_cols :].T
    sum_qkv = (
        sum_qkv[:, : 3 * head_cols]
        .reshape(shard_rows, heads, 3, HS)
        .transpose(0, 2, 1, 3)
        .reshape(shard_rows, 3, head_cols)
    )
    bias_sums = bias_sums.reshape(heads, 3, HS)[:, 0::2].transpose(1, 0, 2).reshape(2, head_cols)
    qv_full = lax.dynamic_update_slice_in_dim(
        jnp.zeros((2, model_width), F32), bias_sums, tensor_pos * head_cols, 1
    )
    fc_full = lax.dynamic_update_slice_in_dim(
        jnp.zeros(fc_bias.shape, F32),
        (sum_pre_a + sum_pre_b).reshape(-1),
        tensor_pos * hidden_cols,
        0,
    )
    small = everyone_sum(
        jnp.concatenate(
            [after(first_sums, chip_first).reshape(-1), qv_full.reshape(-1), middle_sums.reshape(-1), fc_full]
        ).reshape(-1, 128),
        ("tensor", "dp"),
    ).reshape(-1)
    w = model_width
    return (
        result,
        grad_tokens,
        small[:w],
        small[w : 2 * w],
        sum_qkv,
        small[2 * w : 4 * w].reshape(2, w),
        sum_out,
        small[4 * w : 5 * w],
        small[5 * w : 6 * w],
        small[6 * w : 7 * w],
        sum_fc,
        small[8 * w :],
        sum_proj,
        small[7 * w : 8 * w],
    )


def solution(mesh):
    placed = (
        P(("dp", "tensor"), None),
        P("dp", None),
        P(),
        P(),
        P("dp", None, "tensor"),
        P(),
        P("tensor", "dp"),
        P(),
        P(),
        P(),
        P("dp", "tensor"),
        P(),
        P("tensor", "dp"),
        P(),
        P(("dp", "tensor"), None),
    )
    return jax.shard_map(
        per_device,
        mesh=mesh,
        in_specs=placed,
        out_specs=(
            P(("dp", "tensor"), None),
            P(("dp", "tensor"), None),
            P(),
            P(),
            P("dp", None, "tensor"),
            P(),
            P("tensor", "dp"),
            P(),
            P(),
            P(),
            P("dp", "tensor"),
            P(),
            P("tensor", "dp"),
            P(),
        ),
        check_vma=False,
    )
```

time: 422 us -> 304 us (0.72)
  Pallas kernels: 0 us -> 134 us
  matrix products: 103 us -> 0 us
  other arithmetic: 76.4 us -> 16.1 us
  local copies, waits for them, and re-layouts: 69.1 us -> 31 us
  waiting for transfers between devices: 96.7 us -> 61.9 us
  starting transfers between devices: 66.3 us -> 54.3 us
    pallas_call x0 -> x19, Pallas kernels: none -> 134 us  [the longest x18 108 us: kernel_call(): pl.pallas_call(body, out_shape=tuple(out_shape), in_specs=smem(len(scalar...]
    dot_general x45 -> x0, matrix products: 103 us -> none  [the longest x4 16.9 us: attention_backward(): jnp.einsum('qhd,khd->hqk', attended_grad_block, values[:block_end], prefe...]
    ppermute x63 -> x49, waiting for transfers between devices: 96.7 us -> 61.9 us  [swap(): return lax.ppermute(value, axis, [(i, i ^ bits) for i in range(size)])]
    reduce_sum x15 -> x2, other arithmetic: 22.5 us -> 0.23 us  [the longest x1 0.13 us: first_keys(): jnp.sum(jnp.where(seg[None] == labels[:, None], begins[None], 0), axis=1)]
    convert_element_type x9 -> x5, other arithmetic: 23.6 us -> 7.01 us  [the longest x1 2.7 us: per_device(): result = jnp.where(after(live_here, keep_proj)[:, None], middle + mlp_out...]
    unnamed x231 -> x92, local copies, waits for them, and re-layouts: 22.1 us -> 9.78 us
    ppermute x63 -> x49, starting transfers between devices: 66.3 us -> 54.3 us  [swap(): return lax.ppermute(value, axis, [(i, i ^ bits) for i in range(size)])]
    add x14 -> x2, other arithmetic: 10.8 us -> 0.04 us  [the longest x1 0.03 us: per_device(): sum_qkv = keep_qkv[0] + after(got_qkv, grad_tokens)[0].astype(F32)]
  transfers between devices with their start and end apart: 63 -> 49, of which waited for: 26 -> 19; matrix products, arithmetic and copies ran while one was open for 51% -> 12% of each run, Pallas kernels for 0% -> 39%
where the time goes in v2:
time: 304 us; the launch traced here: 299 us
  Pallas kernels  134 us (44%)
  waiting for transfers between devices  61.9 us (20%)
  starting transfers between devices  54.3 us (18%)
  local copies, waits for them, and re-layouts  31 us (10%)
  other arithmetic  16.1 us (5%)
    pallas_call x18, Pallas kernels, kernel_call(): pl.pallas_call(body, out_shape=tuple(out_shape), in_specs=smem(len(scalar...  108 us
    ppermute x49, waiting for transfers between devices, swap(): return lax.ppermute(value, axis, [(i, i ^ bits) for i in range(size)])  61.9 us
    ppermute x49, starting transfers between devices, swap(): return lax.ppermute(value, axis, [(i, i ^ bits) for i in range(size)])  54.3 us
    pallas_call x1, Pallas kernels, attention_forward(): pl.pallas_call(functools.partial(forward_kernel, heads, rows), out_shape=...  26.2 us
    unnamed x92, local copies, waits for them, and re-layouts  9.78 us
  transfers between devices with their start and end apart: 49, of which 19 were waited for; matrix products, arithmetic and copies ran while one was open for 12% of the time, Pallas kernels for 39%

profile of v2, /device:TPU:0, one launch (start us, length us, event | category | flops | bytes accessed | tf_op | source)
XLA Modules:
  0.0 298.8 jit_solution(12720795378664081011)
XLA Ops:
  13.4 4.5 %collective-permute-done.4 = bf16[1,96,768]{1,2,0:T(8,128)(2,1)S(1)} collective-permute-done((bf16[1,96,768]{1,2,0:T(8,128)(2,1)S(1)}, bf16[1,96,768]{1,2,0:T(8,128)(2,1)S(1)}, u32[]{:S(2)}, u32[]{:S(2)}) %collective-permute-start.4) | collective-permute-done | bytes 147488 | tf_op jit(solution)/shard_map/ppermute | solution.py:35
  19.4 9.0 %collective-permute-done.5 = bf16[2,96,768]{1,2,0:T(8,128)(2,1)S(1)} collective-permute-done((bf16[2,96,768]{1,2,0:T(8,128)(2,1)S(1)}, bf16[2,96,768]{1,2,0:T(8,128)(2,1)S(1)}, u32[]{:S(2)}, u32[]{:S(2)}) %collective-permute-start.5) | collective-permute-done | bytes 294944 | tf_op jit(solution)/shard_map/ppermute | solution.py:35
  36.7 8.0 %collective-permute-done.16 = bf16[1,96,1536]{2,1,0:T(8,128)(2,1)S(1)} collective-permute-done((bf16[1,96,1536]{2,1,0:T(8,128)(2,1)S(1)}, bf16[1,96,1536]{2,1,0:T(8,128)(2,1)S(1)}, u32[]{:S(2)}, u32[]{:S(2)}) %collective-permute-start.16) | collective-permute-done | bytes 294944 | tf_op jit(solution)/shard_map/ppermute | solution.py:35
  51.4 5.2 %collective-permute-done.3.refs_2_ = bf16[512,768]{1,0:T(8,128)(2,1)} collective-permute-done((bf16[512,768]{1,0:T(8,128)(2,1)S(1)}, bf16[512,768]{1,0:T(8,128)(2,1)}, u32[]{:S(2)}, u32[]{:S(2)}) %collective-permute-start.3) | collective-permute-done | bytes 786464 | tf_op jit(solution)/shard_map/ppermute | solution.py:35
  56.6 26.2 %attention_forward.1 = (bf16[2048,768]{1,0:T(8,128)(2,1)}, bf16[2048,768]{1,0:T(8,128)(2,1)}, bf16[3,2048,64]{2,1,0:T(8,128)(2,1)}, bf16[3,2048,64]{2,1,0:T(8,12...) custom-call(s32[5]{0:T(128)} %pad_add_fusion.here_ref.order_ref, ...), custom_call_target="tpu_custom_call" | custom-call | flops 3422552064 | bytes 25165824 | tf_op jit(solution)/shard_map/attention_forward/pallas_call | solution.py:176
  96.7 4.4 %branch.1 = (f32[512,768]{1,0:T(8,128)}, bf16[512,768]{1,0:T(8,128)(2,1)}) custom-call(bf16[192,512]{1,0:T(8,128)(2,1)} %get-tuple-element.285.refs_0_, bf16[192,512]{1,0:T(8,128)(2,1)} %collective-permute-done.10.refs_1_, bf16[192,512]{1,0:T(8,128)(2,1)} %collective-permute-done.11.refs_2_, bf16[192,512]{1,0:T(8,128)(2,1)} %collective-permute-done.12.refs_3_, ...), custom_call_target="tpu_custom_call" | custom-call | flops 603979776 | bytes 5121024 | tf_op jit(solution)/shard_map/branch/pallas_call | solution.py:274
  103.4 4.6 %collective-permute-done.18 = bf16[4,96,1536]{2,1,0:T(8,128)(2,1)S(1)} collective-permute-done((bf16[4,96,1536]{2,1,0:T(8,128)(2,1)S(1)}, bf16[4,96,1536]{2,1,0:T(8,128)(2,1)S(1)}, u32[]{:S(2)}, u32[]{:S(2)}) %collective-permute-start.18) | collective-permute-done | bytes 1179680 | tf_op jit(solution)/shard_map/ppermute | solution.py:35
  110.0 9.3 %hidden.2 = (bf16[512,768]{1,0:T(8,128)(2,1)}, bf16[512,768]{1,0:T(8,128)(2,1)}, bf16[512,768]{1,0:T(8,128)(2,1)}, bf16[512,768]{1,0:T(8,128)(2,1)}, bf16[512,76...) custom-call(bf16[512,768]{1,0:T(8,128)(2,1)} %get-tuple-element.130.refs_0_, ...), custom_call_target="tpu_custom_call" | custom-call | flops 3623878656 | bytes 10229760 | tf_op jit(solution)/shard_map/hidden/pallas_call | solution.py:274
  119.2 3.8 %collective-permute-done.14.refs_0_.refs_2_ = bf16[512,768]{1,0:T(8,128)(2,1)S(1)} collective-permute-done((bf16[512,768]{1,0:T(8,128)(2,1)}, bf16[512,768]{1,0:T(8,128)(2,1)S(1)}, u32[]{:S(2)}, u32[]{:S(2)}) %collective-permute-start.14) | collective-permute-done | bytes 786464 | tf_op jit(solution)/shard_map/ppermute | solution.py:35
  126.2 9.7 %hidden.3 = (bf16[512,768]{1,0:T(8,128)(2,1)}, bf16[512,768]{1,0:T(8,128)(2,1)}, bf16[512,768]{1,0:T(8,128)(2,1)}, bf16[512,768]{1,0:T(8,128)(2,1)}, bf16[512,76...) custom-call(bf16[512,768]{1,0:T(8,128)(2,1)} %copy-done.35, bf16[512,768]{1,0:T(8,128)(2,1)} %copy-done.37, ...), custom_call_target="tpu_custom_call" | custom-call | flops 3623878656 | bytes 10229760 | tf_op jit(solution)/shard_map/hidden/pallas_call | solution.py:274
  140.4 6.7 %hidden_weights.2 = (f32[4,96,768]{2,1,0:T(8,128)}, bf16[4,96,768]{2,1,0:T(8,128)(2,1)}) custom-call(s32[1]{0:T(128)} %bitcast.4.high_ref, bf16[512,768]{1,0:T(8,128)(2,1)} %get-tuple-element.130.refs_0_, bf16[512,768]{1,0:T(8,128)(2,1)} %collective-permute-done.13.refs_1_, bf16[512,768]{1,0:T(8,128)(2,1)} %copy-done.35, bf16[512,768]{1,0:T(8,128)(2,1)} %copy-done.37, ...), custom_call_target="tpu_custom_call" | custom-call | flops 2415919104 | bytes 8060928 | tf_op jit(solution)/shard_map/hidden_weights/pallas_call | solution.py:274
  148.9 6.7 %hidden_weights.3 = (f32[4,96,768]{2,1,0:T(8,128)}, bf16[4,96,768]{2,1,0:T(8,128)(2,1)}) custom-call(s32[1]{0:T(128)} %bitcast.4.high_ref, bf16[512,768]{1,0:T(8,128)(2,1)} %copy-done.1, bf16[512,768]{1,0:T(8,128)(2,1)} %collective-permute-done.15.refs_3_.refs_1_, bf16[512,768]{1,0:T(8,128)(2,1)} %collective-permute-done.3.refs_2_, ...), custom_call_target="tpu_custom_call" | custom-call | flops 2415919104 | bytes 8060928 | tf_op jit(solution)/shard_map/hidden_weights/pallas_call | solution.py:274
  155.6 5.8 %project.1 = (bf16[512,768]{1,0:T(8,128)(2,1)}, bf16[512,768]{1,0:T(8,128)(2,1)}, bf16[512,768]{1,0:T(8,128)(2,1)}, bf16[512,768]{1,0:T(8,128)(2,1)}) custom-call(bf16[512,768]{1,0:T(8,128)(2,1)} %get-tuple-element.149.refs_4_.refs_0_, bf16[512,768]{1,0:T(8,128)(2,1)} %get-tuple-element.150.refs_5_.refs_1_, ...), custom_call_target="tpu_custom_call" | custom-call | flops 2415919104 | bytes 7471104 | tf_op jit(solution)/shard_map/project/pallas_call | solution.py:274
  162.4 5.9 %middle.1 = (f32[512,768]{1,0:T(8,128)}, bf16[512,768]{1,0:T(8,128)(2,1)}, f32[4,768]{1,0:T(4,128)}, bf16[192,512]{1,0:T(8,128)(2,1)}, bf16[192,512]{1,0:T(8,128...) custom-call(f32[512,768]{1,0:T(8,128)} %get-tuple-element.157.middle_ref, bf16[512,768]{1,0:T(8,128)(2,1)} %copy-done.1, ...), custom_call_target="tpu_custom_call" | custom-call | flops 603979776 | bytes 9059328 | tf_op jit(solution)/shard_map/middle/pallas_call | solution.py:274
  180.3 24.9 %attention_backward.1.part_ref = bf16[2048,576]{1,0:T(8,128)(2,1)} custom-call(s32[4]{0:T(128)} %and_select_fusion.1.start_ref, s32[5]{0:T(128)} %pad_add_fusion.here_ref.order_ref, s32[1,2048]{1,0:T(1,128)} %compare_select_fusion.low_ref, bf16[3,2048,64]{2,1,0:T(8,128)(2,1)} %get-tuple-element.167.q_ref, bf16[3,2048,64]{2,1,0:T(8,128)(2,1)} %get-tuple-element.168.k_ref, ...), custom_call_target="tpu_custom_call" | custom-call | flops 4026531840 | bytes 7110656 | tf_op jit(solution)/shard_map/attention_backward/pallas_call | solution.py:274
  206.1 7.3 %first.1 = (bf16[2,512,768]{2,1,0:T(8,128)(2,1)}, bf16[2,512,768]{2,1,0:T(8,128)(2,1)}, f32[2,768]{1,0:T(2,128)}, f32[1,576]{1,0:T(1,128)}) custom-call(s32[5]{0:T(128)} %pad_add_fusion.here_ref.order_ref, bf16[2048,768]{1,0:T(8,128)(2,1)} %get-tuple-element.155.hat_ref, bf16[768,576]{1,0:T(8,128)(2,1)} %slice.143.refs_4_.weight_ref, ...), custom_call_target="tpu_custom_call" | custom-call | flops 1811939328 | bytes 9543936 | tf_op jit(solution)/shard_map/first/pallas_call | solution.py:274
  215.0 4.6 %collective-permute-done.36 = bf16[512,768]{1,0:T(8,128)(2,1)S(1)} collective-permute-done((bf16[512,768]{1,0:T(8,128)(2,1)}, bf16[512,768]{1,0:T(8,128)(2,1)S(1)}, u32[]{:S(2)}, u32[]{:S(2)}) %collective-permute-start.36) | collective-permute-done | bytes 786464 | tf_op jit(solution)/shard_map/ppermute | solution.py:35
  226.4 3.7 %collective-permute-done.22.got_ref = bf16[4,96,768]{2,1,0:T(8,128)(2,1)} collective-permute-done((bf16[4,96,768]{2,1,0:T(8,128)(2,1)}, bf16[4,96,768]{2,1,0:T(8,128)(2,1)}, u32[]{:S(2)}, u32[]{:S(2)}) %collective-permute-start.22) | collective-permute-done | bytes 589856 | tf_op jit(solution)/shard_map/ppermute | solution.py:35
  233.0 6.7 %qkv_weights.1 = (f32[4,96,768]{2,1,0:T(8,128)}, bf16[4,96,768]{2,1,0:T(8,128)(2,1)}) custom-call(s32[1]{0:T(128)} %bitcast.4.high_ref, bf16[2048,768]{1,0:T(8,128)(2,1)} %get-tuple-element.193.h1_ref, bf16[2048,576]{1,0:T(8,128)(2,1)} %attention_backward.1.part_ref, bf16[192,768]{1,0:T(8,128)(2,1)} %add_convert_fusion.3.refs_0_), custom_call_target="tpu_custom_call" | custom-call | flops 1811939328 | bytes 7569408 | tf_op jit(solution)/shard_map/qkv_weights/pallas_call | solution.py:274
  246.0 4.4 %collective-permute-done.32.got_ref = bf16[2,96,768]{2,1,0:T(8,128)(2,1)S(1)} collective-permute-done((bf16[2,96,768]{2,1,0:T(8,128)(2,1)}, bf16[2,96,768]{2,1,0:T(8,128)(2,1)S(1)}, u32[]{:S(2)}, u32[]{:S(2)}) %collective-permute-start.32) | collective-permute-done | bytes 294944 | tf_op jit(solution)/shard_map/ppermute | solution.py:35
  250.5 12.8 %collective-permute-start.47 = (bf16[1,96,768]{2,1,0:T(8,128)(2,1)}, bf16[1,96,768]{2,1,0:T(8,128)(2,1)S(1)}, u32[]{:S(2)}, u32[]{:S(2)}) collective-permute-start(bf16[1,96,768]{2,1,0:T(8,128)(2,1)} %get-tuple-element.218), channel_id=1, source_target_pairs={{0,16},{4,20},{8,24},{12,28},{16,0},{20,4},{24,8},{28,12},{1,17},{... | collective-permute-start | bytes 442376 | tf_op jit(solution)/shard_map/ppermute | solution.py:35
  277.8 3.8 %collective-permute-start.45 = (f32[72,128]{1,0:T(8,128)S(1)}, f32[72,128]{1,0:T(8,128)S(1)}, u32[]{:S(2)}, u32[]{:S(2)}) collective-permute-start(f32[72,128]{1,0:T(8,128)S(1)} %add.151), channel_id=1, source_target_pairs={{0,16},{4,20},{8,24},{12,28},{16,0},{20,4},{24,8},{28,12},{1,17},{... | collective-permute-start | bytes 110600 | tf_op jit(solution)/shard_map/ppermute | solution.py:35
  288.2 3.4 %collective-permute-start.46 = (bf16[1,96,768]{2,1,0:T(8,128)(2,1)}, bf16[1,96,768]{2,1,0:T(8,128)(2,1)S(1)}, u32[]{:S(2)}, u32[]{:S(2)}) collective-permute-start(bf16[1,96,768]{2,1,0:T(8,128)(2,1)} %get-tuple-element.216), channel_id=1, source_target_pairs={{0,16},{4,20},{8,24},{12,28},{16,0},{20,4},{24,8},{28,12},{1,17},{... | collective-permute-start | bytes 442376 | tf_op jit(solution)/shard_map/ppermute | solution.py:35
  292.2 4.5 %token_gradient.1 = bf16[512,768]{1,0:T(8,128)(2,1)} custom-call(bf16[512,768]{1,0:T(8,128)(2,1)} %token_ref.1, f32[1,768]{1,0:T(1,128)} %reshape.520.refs_6_.gain_ref, bf16[512,768]{1,0:T(8,128)(2,1)} %slice_bitcast_fusion.1.own_ref, bf16[512,768]{1,0:T(8,128)(2,1)} %slice_bitcast_fusion.near_ref, bf16[512,768]{1,0:T(8,128)(2,1)} %collective-permute-done.38.far_ref, ...), custom_call_target="tpu_custom_call" | custom-call | bytes 5508096 | tf_op jit(solution)/shard_map/token_gradient/pallas_call | solution.py:274
  (273 shorter events, 111.6 us)
Async XLA Ops:
  0.6 48.9 %collective-permute-start = (bf16[512,768]{1,0:T(8,128)(2,1)}, bf16[512,768]{1,0:T(8,128)(2,1)}, u32[]{:S(2)}, u32[]{:S(2)}) collective-permute-start(bf16[512,768]{1,0:T(8,128)(2,1)} %token_ref.1), channel_id=1, source_target_pairs={{0,1},{1,0},{2,3},{3,2},{4,5},{5,4},{6,7},{7,6},{8,9},{9,8},{10,11... | collective-permute-start | bytes 2359304 | tf_op jit(solution)/shard_map/ppermute | solution.py:35
  1.2 30.6 %collective-permute-start.1 = (bf16[512,768]{1,0:T(8,128)(2,1)}, bf16[512,768]{1,0:T(8,128)(2,1)}, u32[]{:S(2)}, u32[]{:S(2)}) collective-permute-start(bf16[512,768]{1,0:T(8,128)(2,1)} %token_ref.1), channel_id=1, source_target_pairs={{0,2},{1,3},{2,0},{3,1},{4,6},{5,7},{6,4},{7,5},{8,10},{9,11},{10,... | collective-permute-start | bytes 2359304 | tf_op jit(solution)/shard_map/ppermute | solution.py:35
  36.2 20.5 %collective-permute-start.3 = (bf16[512,768]{1,0:T(8,128)(2,1)S(1)}, bf16[512,768]{1,0:T(8,128)(2,1)}, u32[]{:S(2)}, u32[]{:S(2)}) collective-permute-start(bf16[512,768]{1,0:T(8,128)(2,1)S(1)} %broadcast_select_fusion.refs_2_.refs_0_.live_grad_ref), channel_id=1, source_target_pairs={{0,2},{1,3},{2,0},{3,1},{4,6},{5,7},{6,4},{7,5},{8,10},{9,11},{10,... | collective-permute-start | bytes 2359304 | tf_op jit(solution)/shard_map/ppermute | solution.py:35
  46.7 36.2 %collective-permute-start.17 = (bf16[2,96,1536]{2,1,0:T(8,128)(2,1)}, bf16[2,96,1536]{2,1,0:T(8,128)(2,1)S(1)}, u32[]{:S(2)}, u32[]{:S(2)}) collective-permute-start(bf16[2,96,1536]{2,1,0:T(8,128)(2,1)} %maximum_select_fusion.4), channel_id=1, source_target_pairs={{0,8},{4,12},{8,0},{12,4},{16,24},{20,28},{24,16},{28,20},{1,9},{5... | collective-permute-start | bytes 1769480 | tf_op jit(solution)/shard_map/ppermute | solution.py:35
  49.5 33.3 %collective-permute-start.7 = (bf16[192,768]{0,1:T(8,128)(2,1)S(1)}, bf16[192,768]{0,1:T(8,128)(2,1)S(1)}, u32[]{:S(2)}, u32[]{:S(2)}) collective-permute-start(bf16[192,768]{0,1:T(8,128)(2,1)S(1)} %slice_bitcast_fusion.2), channel_id=1, source_target_pairs={{0,1},{1,0},{2,3},{3,2},{4,5},{5,4},{6,7},{7,6},{8,9},{9,8},{10,11... | collective-permute-start | bytes 884744 | tf_op jit(solution)/shard_map/ppermute | solution.py:35
  49.6 33.2 %collective-permute-start.8 = (bf16[192,768]{0,1:T(8,128)(2,1)S(1)}, bf16[192,768]{0,1:T(8,128)(2,1)S(1)}, u32[]{:S(2)}, u32[]{:S(2)}) collective-permute-start(bf16[192,768]{0,1:T(8,128)(2,1)S(1)} %slice_bitcast_fusion.2), channel_id=1, source_target_pairs={{0,2},{1,3},{2,0},{3,1},{4,6},{5,7},{6,4},{7,5},{8,10},{9,11},{10,... | collective-permute-start | bytes 884744 | tf_op jit(solution)/shard_map/ppermute | solution.py:35
  50.2 32.7 %collective-permute-start.9 = (bf16[192,768]{0,1:T(8,128)(2,1)S(1)}, bf16[192,768]{0,1:T(8,128)(2,1)S(1)}, u32[]{:S(2)}, u32[]{:S(2)}) collective-permute-start(bf16[192,768]{0,1:T(8,128)(2,1)S(1)} %slice_bitcast_fusion.2), channel_id=1, source_target_pairs={{0,3},{1,2},{2,1},{3,0},{4,7},{5,6},{6,5},{7,4},{8,11},{9,10},{10,... | collective-permute-start | bytes 884744 | tf_op jit(solution)/shard_map/ppermute | solution.py:35
  84.0 24.1 %collective-permute-start.18 = (bf16[4,96,1536]{2,1,0:T(8,128)(2,1)S(1)}, bf16[4,96,1536]{2,1,0:T(8,128)(2,1)S(1)}, u32[]{:S(2)}, u32[]{:S(2)}) collective-permute-start(bf16[4,96,1536]{2,1,0:T(8,128)(2,1)S(1)} %bitcast.96), channel_id=1, source_target_pairs={{0,4},{4,0},{8,12},{12,8},{16,20},{20,16},{24,28},{28,24},{1,5},{5... | collective-permute-start | bytes 3538952 | tf_op jit(solution)/shard_map/ppermute | solution.py:35
  87.1 22.9 %collective-permute-start.15 = (bf16[512,768]{1,0:T(8,128)(2,1)S(1)}, bf16[512,768]{1,0:T(8,128)(2,1)}, u32[]{:S(2)}, u32[]{:S(2)}) collective-permute-start(bf16[512,768]{1,0:T(8,128)(2,1)S(1)} %broadcast_select_fusion.refs_2_.refs_0_.live_grad_ref), channel_id=1, source_target_pairs={{0,1},{1,0},{2,3},{3,2},{4,5},{5,4},{6,7},{7,6},{8,9},{9,8},{10,11... | collective-permute-start | bytes 2359304 | tf_op jit(solution)/shard_map/ppermute | solution.py:35
  102.8 20.2 %collective-permute-start.20 = (bf16[512,768]{1,0:T(8,128)(2,1)}, bf16[512,768]{1,0:T(8,128)(2,1)S(1)}, u32[]{:S(2)}, u32[]{:S(2)}) collective-permute-start(bf16[512,768]{1,0:T(8,128)(2,1)} %collective-permute-done.3.refs_2_), channel_id=1, source_target_pairs={{0,1},{1,0},{2,3},{3,2},{4,5},{5,4},{6,7},{7,6},{8,9},{9,8},{10,11... | collective-permute-start | bytes 2359304 | tf_op jit(solution)/shard_map/ppermute | solution.py:35
  103.0 20.1 %collective-permute-start.14 = (bf16[512,768]{1,0:T(8,128)(2,1)}, bf16[512,768]{1,0:T(8,128)(2,1)S(1)}, u32[]{:S(2)}, u32[]{:S(2)}) collective-permute-start(bf16[512,768]{1,0:T(8,128)(2,1)} %get-tuple-element.130.refs_0_), channel_id=1, source_target_pairs={{0,2},{1,3},{2,0},{3,1},{4,6},{5,7},{6,4},{7,5},{8,10},{9,11},{10,... | collective-permute-start | bytes 2359304 | tf_op jit(solution)/shard_map/ppermute | solution.py:35
  139.8 21.5 %collective-permute-start.25 = (bf16[512,768]{1,0:T(8,128)(2,1)S(1)}, bf16[512,768]{1,0:T(8,128)(2,1)S(1)}, u32[]{:S(2)}, u32[]{:S(2)}) collective-permute-start(bf16[512,768]{1,0:T(8,128)(2,1)S(1)} %add_convert_fusion.2), channel_id=1, source_target_pairs={{0,2},{1,3},{2,0},{3,1},{4,6},{5,7},{6,4},{7,5},{8,10},{9,11},{10,... | collective-permute-start | bytes 2359304 | tf_op jit(solution)/shard_map/ppermute | solution.py:35
  140.4 20.9 %collective-permute-start.24 = (bf16[512,768]{1,0:T(8,128)(2,1)S(1)}, bf16[512,768]{1,0:T(8,128)(2,1)S(1)}, u32[]{:S(2)}, u32[]{:S(2)}) collective-permute-start(bf16[512,768]{1,0:T(8,128)(2,1)S(1)} %copy-done.34), channel_id=1, source_target_pairs={{0,1},{1,0},{2,3},{3,2},{4,5},{5,4},{6,7},{7,6},{8,9},{9,8},{10,11... | collective-permute-start | bytes 2359304 | tf_op jit(solution)/shard_map/ppermute | solution.py:35
  147.1 26.0 %collective-permute-start.23 = (bf16[4,96,768]{2,1,0:T(8,128)(2,1)}, bf16[4,96,768]{2,1,0:T(8,128)(2,1)S(1)}, u32[]{:S(2)}, u32[]{:S(2)}) collective-permute-start(bf16[4,96,768]{2,1,0:T(8,128)(2,1)} %get-tuple-element.156), channel_id=1, source_target_pairs={{0,4},{4,0},{8,12},{12,8},{16,20},{20,16},{24,28},{28,24},{1,5},{5... | collective-permute-start | bytes 1769480 | tf_op jit(solution)/shard_map/ppermute | solution.py:35
  176.4 28.8 %collective-permute-start.29 = (bf16[192,768]{1,0:T(8,128)(2,1)S(1)}, bf16[192,768]{1,0:T(8,128)(2,1)S(1)}, u32[]{:S(2)}, u32[]{:S(2)}) collective-permute-start(bf16[192,768]{1,0:T(8,128)(2,1)S(1)} %copy-done.40), channel_id=1, source_target_pairs={{0,1},{1,0},{2,3},{3,2},{4,5},{5,4},{6,7},{7,6},{8,9},{9,8},{10,11... | collective-permute-start | bytes 884744 | tf_op jit(solution)/shard_map/ppermute | solution.py:35
  176.9 28.3 %collective-permute-start.30 = (bf16[192,768]{1,0:T(8,128)(2,1)S(1)}, bf16[192,768]{1,0:T(8,128)(2,1)S(1)}, u32[]{:S(2)}, u32[]{:S(2)}) collective-permute-start(bf16[192,768]{1,0:T(8,128)(2,1)S(1)} %copy-done.39), channel_id=1, source_target_pairs={{0,2},{1,3},{2,0},{3,1},{4,6},{5,7},{6,4},{7,5},{8,10},{9,11},{10,... | collective-permute-start | bytes 884744 | tf_op jit(solution)/shard_map/ppermute | solution.py:35
  178.5 26.7 %collective-permute-start.31 = (bf16[192,768]{1,0:T(8,128)(2,1)S(1)}, bf16[192,768]{1,0:T(8,128)(2,1)S(1)}, u32[]{:S(2)}, u32[]{:S(2)}) collective-permute-start(bf16[192,768]{1,0:T(8,128)(2,1)S(1)} %copy-done.38), channel_id=1, source_target_pairs={{0,3},{1,2},{2,1},{3,0},{4,7},{5,6},{6,5},{7,4},{8,11},{9,10},{10,... | collective-permute-start | bytes 884744 | tf_op jit(solution)/shard_map/ppermute | solution.py:35
  213.4 26.2 %collective-permute-start.33 = (bf16[2,512,768]{2,1,0:T(8,128)(2,1)}, bf16[2,512,768]{2,1,0:T(8,128)(2,1)S(1)}, u32[]{:S(2)}, u32[]{:S(2)}) collective-permute-start(bf16[2,512,768]{2,1,0:T(8,128)(2,1)} %get-tuple-element.188), channel_id=1, source_target_pairs={{0,1},{1,0},{2,3},{3,2},{4,5},{5,4},{6,7},{7,6},{8,9},{9,8},{10,11... | collective-permute-start | bytes 4718600 | tf_op jit(solution)/shard_map/ppermute | solution.py:35
  214.5 52.2 %collective-permute-start.35 = (bf16[512,768]{1,0:T(8,128)(2,1)}, bf16[512,768]{1,0:T(8,128)(2,1)}, u32[]{:S(2)}, u32[]{:S(2)}) collective-permute-start(bf16[512,768]{1,0:T(8,128)(2,1)} %get-tuple-element.199), channel_id=1, source_target_pairs={{0,1},{1,0},{2,3},{3,2},{4,5},{5,4},{6,7},{7,6},{8,9},{9,8},{10,11... | collective-permute-start | bytes 2359304 | tf_op jit(solution)/shard_map/ppermute | solution.py:35
  220.7 46.9 %collective-permute-start.37 = (bf16[512,768]{1,0:T(8,128)(2,1)}, bf16[512,768]{1,0:T(8,128)(2,1)}, u32[]{:S(2)}, u32[]{:S(2)}) collective-permute-start(bf16[512,768]{1,0:T(8,128)(2,1)} %add_convert_fusion), channel_id=1, source_target_pairs={{0,2},{1,3},{2,0},{3,1},{4,6},{5,7},{6,4},{7,5},{8,10},{9,11},{10,... | collective-permute-start | bytes 2359304 | tf_op jit(solution)/shard_map/ppermute | solution.py:35
  242.0 23.2 %collective-permute-start.42 = (f32[72,128]{1,0:T(8,128)S(1)}, f32[72,128]{1,0:T(8,128)S(1)}, u32[]{:S(2)}, u32[]{:S(2)}) collective-permute-start(f32[72,128]{1,0:T(8,128)S(1)} %fusion.7), channel_id=1, source_target_pairs={{0,2},{1,3},{2,0},{3,1},{4,6},{5,7},{6,4},{7,5},{8,10},{9,11},{10,... | collective-permute-start | bytes 110600 | tf_op jit(solution)/shard_map/ppermute | solution.py:35
  245.7 28.5 %collective-permute-start.39 = (bf16[4,96,768]{2,1,0:T(8,128)(2,1)}, bf16[4,96,768]{2,1,0:T(8,128)(2,1)S(1)}, u32[]{:S(2)}, u32[]{:S(2)}) collective-permute-start(bf16[4,96,768]{2,1,0:T(8,128)(2,1)} %get-tuple-element.204), channel_id=1, source_target_pairs={{0,4},{4,0},{8,12},{12,8},{16,20},{20,16},{24,28},{28,24},{1,5},{5... | collective-permute-start | bytes 1769480 | tf_op jit(solution)/shard_map/ppermute | solution.py:35
  250.5 27.4 %collective-permute-start.47 = (bf16[1,96,768]{2,1,0:T(8,128)(2,1)}, bf16[1,96,768]{2,1,0:T(8,128)(2,1)S(1)}, u32[]{:S(2)}, u32[]{:S(2)}) collective-permute-start(bf16[1,96,768]{2,1,0:T(8,128)(2,1)} %get-tuple-element.218), channel_id=1, source_target_pairs={{0,16},{4,20},{8,24},{12,28},{16,0},{20,4},{24,8},{28,12},{1,17},{... | collective-permute-start | bytes 442376 | tf_op jit(solution)/shard_map/ppermute | solution.py:35
  265.2 27.0 %collective-permute-start.38 = (bf16[512,768]{1,0:T(8,128)(2,1)}, bf16[512,768]{1,0:T(8,128)(2,1)}, u32[]{:S(2)}, u32[]{:S(2)}) collective-permute-start(bf16[512,768]{1,0:T(8,128)(2,1)} %fusion), channel_id=1, source_target_pairs={{0,2},{1,3},{2,0},{3,1},{4,6},{5,7},{6,4},{7,5},{8,10},{9,11},{10,... | collective-permute-start | bytes 2359304 | tf_op jit(solution)/shard_map/ppermute | solution.py:35
  (69 other events, 583.6 us)

commit v3 on v2

--- a/solution.py
+++ b/solution.py
@@ -101,22 +101,26 @@
     count = here_ref.shape[0] - 1
     token_refs = refs[:count]
     weight_ref, bias_ref, gain_ref, shift_ref = refs[count : count + 4]
-    (h1_ref, hat_ref, q_ref, k_ref, v_ref, out_ref, lse_ref, send_ref) = refs[count + 4 :]
+    h1_ref, hat_ref, q_ref, k_ref, v_ref, out_ref, lse_ref = refs[count + 4 : count + 11]
+    send_refs, token_all = refs[count + 11 : -1], refs[-1]
     here = here_ref[count]
     local_rows = token_refs[0].shape[0]
     chunk = 256
     for r in range(count):
-
-        def project(step, carry, r=r):
-            base = pl.multiple_of((here_ref[r]) * local_rows + step * chunk, chunk)
-            rows = token_refs[r][rows_at(step, chunk), :].astype(F32)
+        token_all[r] = token_refs[r][...]
+    if True:
+
+        def project(step, carry):
+            r, part = step // (local_rows // chunk), step % (local_rows // chunk)
+            base = pl.multiple_of(here_ref[r] * local_rows + part * chunk, chunk)
+            rows = token_all[r, rows_at(part, chunk), :].astype(F32)
             centre = rows - jnp.mean(rows, axis=-1, keepdims=True)
             spread = jnp.mean(centre * centre, axis=-1, keepdims=True)
             hat = centre * lax.rsqrt(spread + EPSILON)
             h1 = (hat * gain_ref[...] + shift_ref[...]).astype(BF)
             hat_ref[pl.ds(base, chunk), :] = hat.astype(BF)
             h1_ref[pl.ds(base, chunk), :] = h1
-            qkv = (nn(h1, weight_ref[...]) + bias_ref[...]).astype(BF)
+            qkv = (nn(h1, weight_ref[:, : 3 * heads * HS]) + bias_ref[...]).astype(BF)
             for h in range(heads):
                 at = 3 * h * HS
                 q_ref[h, pl.ds(base, chunk), :] = qkv[:, at : at + HS] * HS ** (-0.5)
@@ -124,7 +128,7 @@
                 v_ref[h, pl.ds(base, chunk), :] = qkv[:, at + 2 * HS : at + 3 * HS]
             return carry
 
-        lax.fori_loop(0, local_rows // chunk, project, 0)
+        lax.fori_loop(0, count * local_rows // chunk, project, 0)
 
     blocks = q_ref.shape[1] // block
 
@@ -162,7 +166,12 @@
             rows = acc / total
             out_ref[h, :, rows_at(i, block)] = rows
             lse_ref[h, :, rows_at(i, block)] = peak + jnp.log(total)
-            send_ref[slot, h * HS : (h + 1) * HS, :] = rows.astype(BF)
+            for r in range(count):
+
+                @pl.when(slot == r)
+                def _(r=r, h=h, rows=rows):
+                    send_refs[r][h * HS : (h + 1) * HS, :] = rows.astype(BF)
+
         return carry
 
     lax.fori_loop(0, blocks, query_step, 0)
@@ -183,11 +192,12 @@
             shape((heads, total, HS), BF),
             shape((heads, HS, total), F32),
             shape((heads, 1, total), F32),
-            shape((count, heads * HS, rows), BF),
-        ),
+        )
+        + (shape((heads * HS, rows), BF),) * count,
         in_specs=[pl.BlockSpec(memory_space=pltpu.SMEM)] * 2
         + [pl.BlockSpec(memory_space=pltpu.VMEM)] * (count + 5),
-        out_specs=[pl.BlockSpec(memory_space=pltpu.VMEM)] * 8,
+        out_specs=[pl.BlockSpec(memory_space=pltpu.VMEM)] * (7 + count),
+        scratch_shapes=[pltpu.VMEM((count, rows, width), BF)],
         compiler_params=pltpu.CompilerParams(vmem_limit_bytes=60000 * 1024),
         cost_estimate=pl.CostEstimate(
             flops=flops, bytes_accessed=24 << 20, transcendentals=heads * total * total // 2
@@ -326,6 +336,10 @@
     )
 
 
+def turn_kernel(packed_ref, out_ref):
+    out_ref[...] = packed_ref[:, packed_ref.shape[1] - out_ref.shape[0] :].T
+
+
 def branch_kernel(count, *refs):
     att_refs, weight_refs = refs[:count], refs[count : 2 * count]
     token_ref, bias_ref, gain_ref, shift_ref, middle_ref, h2_ref = refs[2 * count :]
@@ -340,44 +354,56 @@
 
 def hidden_kernel(count, chunk, *refs):
     h2_refs, grad_refs = refs[:count], refs[count : 2 * count]
-    fc_ref, proj_ref, bias_ref = refs[2 * count : 2 * count + 3]
-    rest = refs[2 * count + 3 :]
-    back_refs, act_refs, pre_refs, sum_ref = rest[:count], rest[count : 2 * count], rest[2 * count : 3 * count], rest[3 * count]
+    packed_ref, bias_ref = refs[2 * count : 2 * count + 2]
+    back_refs = refs[2 * count + 2 : 3 * count + 2]
+    act_ref, pre_ref, sum_ref, h2_all, grad_all = refs[3 * count + 2 :]
+    rows, cols = h2_refs[0].shape[0], packed_ref.shape[1] // 2
+    fc_ref, proj_ref = packed_ref.at[:, :cols], packed_ref.at[:, cols:]
     sum_ref[...] = jnp.zeros_like(sum_ref)
     for r in range(count):
-
-        def step(i, carry, r=r):
-            at = rows_at(i, chunk)
-            u = nn(h2_refs[r][at, :], fc_ref[...]) + bias_ref[...]
-            grad_act = nn(grad_refs[r][at, :], proj_ref[...])
-            square = u * u
-            bend = jnp.tanh(GELU_SCALE * (u + 0.044715 * square * u))
-            act_refs[r][at, :] = (0.5 * u * (1.0 + bend)).astype(BF)
-            slope = 0.5 * (1.0 + bend) + 0.5 * u * (1.0 - bend * bend) * GELU_SCALE * (
-                1.0 + 3.0 * 0.044715 * square
-            )
-            grad_pre = (grad_act * slope).astype(BF)
-            pre_refs[r][at, :] = grad_pre
-            sum_ref[...] += jnp.sum(grad_pre.astype(F32), axis=0, keepdims=True)
-            back_refs[r][at, :] = nt(grad_pre, fc_ref[...]).astype(BF)
-            return carry
-
-        lax.fori_loop(0, h2_refs[r].shape[0] // chunk, step, 0)
-
-
-def hidden(h2s, grads, fc, proj, bias):
+        h2_all[r] = h2_refs[r][...]
+        grad_all[r] = grad_refs[r][...]
+
+    def step(i, carry):
+        r = i // (rows // chunk)
+        at = rows_at(i % (rows // chunk), chunk)
+        u = nn(h2_all[r, at, :], fc_ref[...]) + bias_ref[...]
+        grad_act = nn(grad_all[r, at, :], proj_ref[...])
+        square = u * u
+        bend = jnp.tanh(GELU_SCALE * (u + 0.044715 * square * u))
+        act_ref[r, at, :] = (0.5 * u * (1.0 + bend)).astype(BF)
+        slope = 0.5 * (1.0 + bend) + 0.5 * u * (1.0 - bend * bend) * GELU_SCALE * (
+            1.0 + 3.0 * 0.044715 * square
+        )
+        grad_pre = (grad_act * slope).astype(BF)
+        pre_ref[r, at, :] = grad_pre
+        sum_ref[...] += jnp.sum(grad_pre.astype(F32), axis=0, keepdims=True)
+        back = nt(grad_pre, fc_ref[...]).astype(BF)
+        for k in range(count):
+
+            @pl.when(r == k)
+            def _(k=k, back=back, at=at):
+                back_refs[k][at, :] = back
+
+        return carry
+
+    lax.fori_loop(0, count * rows // chunk, step, 0)
+
+
+def hidden(h2s, grads, packed, bias):
     count = len(h2s)
     rows, width = h2s[0].shape
-    cols = fc.shape[1]
+    cols = packed.shape[1] // 2
     return kernel_call(
         functools.partial(hidden_kernel, count, 256),
         "hidden",
         [shape((rows, width), BF)] * count
-        + [shape((rows, cols), BF)] * (2 * count)
+        + [shape((count, rows, cols), BF)] * 2
         + [shape((1, cols), F32)],
         [],
-        [*h2s, *grads, fc, proj, bias],
+        [*h2s, *grads, packed, bias],
         6 * count * rows * width * cols,
+        [pltpu.VMEM((count, rows, width), BF)] * 2,
         transcendentals=count * rows * cols,
     )
 
@@ -392,17 +418,18 @@
 
 
 def weight_kernel(count, high_ref, *refs):
-    left_refs, right_refs = refs[:count], refs[count : 2 * count]
-    keep_ref, give_ref = refs[2 * count :]
-    total = tn(left_refs[0][...], right_refs[0][...])
+    left_refs, right_refs = refs[:count], refs[count:-2]
+    keep_ref, give_ref = refs[-2:]
+    each = count // len(right_refs)
+    total = tn(left_refs[0][...], right_refs[0][0])
     for r in range(1, count):
-        total = total + tn(left_refs[r][...], right_refs[r][...])
+        total = total + tn(left_refs[r][...], right_refs[r // each][r % each])
     split_store(total, keep_ref, give_ref, high_ref[0] > 0, slice(0, total.shape[1]))
 
 
 def hidden_weights(lefts, rights, high, dp_size):
     rows, width = lefts[0].shape
-    cols = rights[0].shape[1]
+    cols = rights[0].shape[2]
     dims = (dp_size // 2, width // dp_size, cols)
     return kernel_call(
         functools.partial(weight_kernel, len(lefts)),
@@ -415,21 +442,24 @@
 
 
 def project_kernel(count, *refs):
-    act_refs, proj_ref, out_refs = refs[:count], refs[count], refs[count + 1 :]
-    for act, out in zip(act_refs, out_refs, strict=True):
-        out[...] = nt(act[...], proj_ref[...]).astype(BF)
-
-
-def project(acts, proj):
-    rows, cols = acts[0].shape
-    width = proj.shape[0]
+    act_refs, proj_ref, out_refs = refs[: -count - 1], refs[-count - 1], refs[-count:]
+    each = count // len(act_refs)
+    for r, out in enumerate(out_refs):
+        act = act_refs[r // each].at[r % each]
+        out[...] = nt(act[...], proj_ref[:, act.shape[1] :]).astype(BF)
+
+
+def project(acts, packed):
+    each, rows, cols = acts[0].shape
+    width = packed.shape[0]
+    count = each * len(acts)
     return kernel_call(
-        functools.partial(project_kernel, len(acts)),
+        functools.partial(project_kernel, count),
         "project",
-        [shape((rows, width), BF)] * len(acts),
+        [shape((rows, width), BF)] * count,
         [],
-        [*acts, proj],
-        2 * len(acts) * rows * cols * width,
+        [*acts, packed],
+        2 * count * rows * cols * width,
     )
 
 
@@ -457,26 +487,37 @@
         out[...] = nn(att[...], branch_ref[...]).astype(BF)
 
 
-def first_kernel(order_ref, hat_ref, weight_ref, part_ref, keep_ref, give_ref, sums_ref, bias_ref):
-    count, rows = 2 * keep_ref.shape[0], keep_ref.shape[1]
+def first_kernel(
+    order_ref, hat_ref, weight_ref, part_ref, own_ref, far_ref, give_ref, sums_ref, bias_ref
+):
+    rows, cols = own_ref.shape[0], part_ref.shape[1]
     sums_ref[...] = jnp.zeros_like(sums_ref)
     bias_ref[...] = jnp.zeros_like(bias_ref)
 
-    def block(r):
+    def step(r, carry):
         at = rows_at(order_ref[r], rows)
         part = part_ref[at, :]
         bias_ref[...] += jnp.sum(part.astype(F32), axis=0, keepdims=True)
-        total = nt(part, weight_ref[...])
+        total = nt(part, weight_ref[:, :cols])
         sums_ref[0:1, :] += jnp.sum(total * hat_ref[at, :].astype(F32), axis=0, keepdims=True)
         sums_ref[1:2, :] += jnp.sum(total, axis=0, keepdims=True)
-        return total.astype(BF)
-
-    def pair(p, carry):
-        give_ref[p] = block(2 * p + 1)
-        keep_ref[p] = block(2 * p)
+        done = total.astype(BF)
+
+        @pl.when(r == 0)
+        def _():
+            own_ref[...] = done
+
+        @pl.when(r == 2)
+        def _():
+            far_ref[...] = done
+
+        @pl.when((r & 1) == 1)
+        def _():
+            give_ref[r // 2] = done
+
         return carry
 
-    lax.fori_loop(0, count // 2, pair, 0)
+    lax.fori_loop(0, 4, step, 0)
 
 
 def qkv_weight_kernel(count, high_ref, h1_ref, part_ref, *refs):
@@ -526,7 +567,7 @@
 
 def token_kernel(token_ref, gain_ref, own_ref, near_ref, far_ref, middle_ref, out_ref):
     hat, scale = normalised(token_ref[...].astype(F32))
-    grad = own_ref[...].astype(F32) + near_ref[...].astype(F32) + far_ref[...].astype(F32)
+    grad = own_ref[...].astype(F32) + near_ref[0].astype(F32) + far_ref[...].astype(F32)
     out_ref[...] = (middle_ref[...] + norm_back(grad, gain_ref[...], hat, scale)).astype(BF)
 
 
@@ -577,8 +618,10 @@
                 later = gather_step(after(later, ahead), "dp", early)
     ahead = ahead.reshape(model_width, -1)
     later_far = swap(after(later, ahead), "dp", dp_bits[-2])
-    full_qkv = ahead[:, : 3 * head_cols]
-    out_turned = ahead[:, 3 * head_cols :].T
+    full_qkv = ahead
+    (out_turned,) = kernel_call(
+        turn_kernel, "turn", [shape((head_cols, model_width), BF)], [], [ahead], 0
+    )
     outs = exchange([out_turned] * tensor_size, "tensor")
     near_tokens = swap(tokens, "tensor", near)
     last_tokens = swap(far_tokens, "tensor", near)
@@ -598,7 +641,6 @@
     grad_mlp = jnp.where(live_here[:, None], out_grad, jnp.zeros_like(out_grad))
     far_grad = swap(after(grad_mlp, far_tokens), "tensor", far)
     near_grad = swap(grad_mlp, "tensor", near)
-    token_blocks = after(tuple(token_blocks), far_grad)
 
     bias_here = lax.dynamic_slice_in_dim(qv_bias, tensor_pos * head_cols, head_cols, 1).reshape(
         2, heads, HS
@@ -606,7 +648,7 @@
     bias_row = row(
         jnp.stack([bias_here[0], jnp.zeros((heads, HS), F32), bias_here[1]], 1).reshape(-1)
     )
-    first_all, first_hat, queries, key_rows, values, attended, log_total, sends = attention_forward(
+    first_all, first_hat, queries, key_rows, values, attended, log_total, *sends = attention_forward(
         token_blocks,
         full_qkv,
         bias_row,
@@ -618,13 +660,12 @@
         heads,
     )
 
-    outs = list(after(tuple(outs), sends))
-    sends = after(sends, *outs)
-    mine = exchange([sends[r] for r in range(tensor_size)], "tensor")
-    later = gather_step(later, "dp", dp_bits[-2], after(later_far, sends))
+    outs = list(after(tuple(outs), sends[0]))
+    sends = after(tuple(sends), far_grad, *outs)
+    mine = exchange(sends, "tensor")
+    later = gather_step(later, "dp", dp_bits[-2], after(later_far, sends[0]))
     later = gather_step(later, "dp", dp_bits[-1]).reshape(model_width, -1)
-    fc_cols, proj_turned = later[:, :hidden_cols], later[:, hidden_cols:]
-    last_grad = swap(after(far_grad, sends), "tensor", near)
+    last_grad = swap(after(far_grad, sends[0]), "tensor", near)
     grads = [grad_mlp, near_grad, far_grad, last_grad]
     middle, second_norm = kernel_call(
         functools.partial(branch_kernel, tensor_size),
@@ -637,21 +678,21 @@
     far_second = swap(second_norm, "tensor", far)
     near_second = swap(second_norm, "tensor", near)
     fc_bias_here = row(lax.dynamic_slice_in_dim(fc_bias, tensor_pos * hidden_cols, hidden_cols, 0))
-    back_0, back_1, act_0, act_1, pre_0, pre_1, sum_pre_a = hidden(
-        [second_norm, near_second], grads[:2], fc_cols, proj_turned, fc_bias_here
+    back_0, back_1, act_a, pre_a, sum_pre_a = hidden(
+        [second_norm, near_second], grads[:2], later, fc_bias_here
     )
     far_second = after(far_second, back_0)
     last_second = swap(far_second, "tensor", near)
-    back_2, back_3, act_2, act_3, pre_2, pre_3, sum_pre_b = hidden(
-        [far_second, last_second], grads[2:], fc_cols, proj_turned, fc_bias_here
+    back_2, back_3, act_b, pre_b, sum_pre_b = hidden(
+        [far_second, last_second], grads[2:], later, fc_bias_here
     )
     near_back = swap(back_1, "tensor", near)
     last_back = swap(back_3, "tensor", near)
     chip_back = (back_2.astype(F32) + last_back.astype(F32)).astype(BF)
     far_back = swap(chip_back, "tensor", far)
-    act_0, act_1, act_2, act_3, _ = lax.optimization_barrier((act_0, act_1, act_2, act_3, chip_back))
-    acts = [act_0, act_1, act_2, act_3]
-    pres = [pre_0, pre_1, pre_2, pre_3]
+    act_a, act_b = after((act_a, act_b), chip_back)
+    acts = [act_a, act_b]
+    pres = [pre_a, pre_b]
     keep_fc, give_fc = hidden_weights(
         [second_norm, near_second, far_second, last_second], pres, high, dp_size
     )
@@ -660,7 +701,7 @@
         [after(grads[0], keep_fc), *grads[1:]], acts, high, dp_size
     )
     got_proj = swap(give_proj, "dp", dp_bits[-1])
-    mlp_parts = project(acts, after(proj_turned, keep_proj))
+    mlp_parts = project(acts, after(later, keep_proj))
     mlp_near = swap(mlp_parts[1], "tensor", near)
     mlp_last = swap(mlp_parts[3], "tensor", near)
     mlp_far_sum = (mlp_parts[2].astype(F32) + mlp_last.astype(F32)).astype(BF)
@@ -685,7 +726,7 @@
         "out_weights",
         [shape((head_cols, model_width), BF)] * tensor_size,
         [],
-        [grad_branch, *mine],
+        [after(grad_branch, mlp_far_sum), *mine],
         2 * local_rows * model_width * model_width,
     )
     keep_fc, give_fc = halve(keep_fc, after(got_fc, grad_out_parts[0]), "dp", dp_bits[-2])
@@ -708,34 +749,34 @@
     grad_out = sum(g.astype(F32) for g in grad_out_parts).astype(BF)
     grad_qkv = after(grad_qkv, grad_out)
 
-    keep_first, give_first, first_sums, bias_sums = kernel_call(
+    grad_qkv = after(grad_qkv, got_fc, got_proj, mlp_far)
+    keep_qkv, give_qkv = qkv_weights(first_all, grad_qkv, [grad_out], high, dp_size)
+    got_qkv = swap(give_qkv, "dp", dp_bits[-1])
+    own_first, chip_first, give_first, first_sums, bias_sums = kernel_call(
         first_kernel,
         "first",
         [
-            shape((tensor_size // 2, local_rows, model_width), BF),
+            shape((local_rows, model_width), BF),
+            shape((local_rows, model_width), BF),
             shape((tensor_size // 2, local_rows, model_width), BF),
             shape((2, model_width), F32),
             shape((1, 3 * head_cols), F32),
         ],
         [order],
-        [first_hat, full_qkv, grad_qkv],
+        [first_hat, full_qkv, after(grad_qkv, keep_qkv)],
         2 * capacity * model_width * 3 * head_cols,
     )
     got_first = swap(give_first, "tensor", near)
     rest = dp_bits[:-2][::-1]
-    got_fc = after(got_fc, keep_first)
-    got_proj = after(got_proj, keep_first)
+    got_fc = after(got_fc, own_first)
+    got_proj = after(got_proj, own_first)
     for bit in rest:
         keep_fc, give_fc = halve(keep_fc, got_fc, "dp", bit)
         got_fc = swap(give_fc, "dp", bit)
     keep_proj, give_proj = halve(keep_proj, got_proj, "dp", dp_bits[-2])
     got_proj = swap(give_proj, "dp", dp_bits[-2])
-    keep_qkv, give_qkv = qkv_weights(
-        after(first_all, keep_fc, keep_proj), grad_qkv, [grad_out], high, dp_size
-    )
-    got_qkv = swap(give_qkv, "dp", dp_bits[-1])
-    got_first = after(got_first, keep_qkv)
-    chip_first = (keep_first[1].astype(F32) + got_first[1].astype(F32)).astype(BF)
+    got_first = after(got_first, keep_fc, keep_proj)
+    chip_first = (chip_first.astype(F32) + got_first[1].astype(F32)).astype(BF)
     far_first = swap(chip_first, "tensor", far)
     got_proj = after(got_proj, chip_first)
     for bit in rest:
@@ -758,7 +799,7 @@
         "token_gradient",
         [shape((local_rows, model_width), BF)],
         [],
-        [tokens, row(norm1_gain), keep_first[0], got_first[0], far_first, grad_middle],
+        [tokens, row(norm1_gain), own_first, got_first, far_first, grad_middle],
         0,
     )
 

time: 304 us -> 300 us (0.987); the launches traced: 299 us -> 299 us
  Pallas kernels: 134 us -> 154 us
  local copies, waits for them, and re-layouts: 31 us -> 18.1 us
  starting transfers between devices: 54.3 us -> 43.4 us
  waiting for transfers between devices: 61.9 us -> 65.1 us
    pallas_call x18 -> x19, Pallas kernels: 108 us -> 122 us  [kernel_call(): pl.pallas_call(body, out_shape=tuple(out_shape), in_specs=smem(len(scalar...]
    ppermute x49, starting transfers between devices: 54.3 us -> 43.4 us  [swap(): return lax.ppermute(value, axis, [(i, i ^ bits) for i in range(size)])]
    pallas_call x1, Pallas kernels: 26.2 us -> 31.9 us  [attention_forward(): pl.pallas_call(functools.partial(forward_kernel, heads, rows), out_shape=...]
    optimization_barrier x5 -> x1, local copies, waits for them, and re-layouts: 5.79 us -> 0.28 us  [after(): return lax.optimization_barrier((value, *others))[0]]
    squeeze x3 -> x0, local copies, waits for them, and re-layouts: 3.91 us -> none  [the longest x1 2.09 us: per_device(): keep_first[0]]
    select_n x8, other arithmetic: 2.18 us -> 5.56 us  [gather_step(): jnp.where(high, jnp.stack([other, full], 1), jnp.stack([full, other], 1))]
    ppermute x49, waiting for transfers between devices: 61.9 us -> 65.1 us  [swap(): return lax.ppermute(value, axis, [(i, i ^ bits) for i in range(size)])]
    unnamed x92 -> x106, local copies, waits for them, and re-layouts: 9.78 us -> 9.04 us
  transfers between devices with their start and end apart: 49 -> 49, of which waited for: 19 -> 17; matrix products, arithmetic and copies ran while one was open for 12% -> 9% of each run, Pallas kernels for 39% -> 43%
where the time goes in v3:
time: 300 us; the launch traced here: 299 us
  Pallas kernels  154 us (51%)
  waiting for transfers between devices  65.1 us (22%)
  starting transfers between devices  43.4 us (14%)
  local copies, waits for them, and re-layouts  18.1 us (6%)
  other arithmetic  17.3 us (6%)
    pallas_call x19, Pallas kernels, kernel_call(): pl.pallas_call(body, out_shape=tuple(out_shape), in_specs=smem(len(scalar...  122 us
    ppermute x49, waiting for transfers between devices, swap(): return lax.ppermute(value, axis, [(i, i ^ bits) for i in range(size)])  65.1 us
    ppermute x49, starting transfers between devices, swap(): return lax.ppermute(value, axis, [(i, i ^ bits) for i in range(size)])  43.4 us
    pallas_call x1, Pallas kernels, attention_forward(): pl.pallas_call(functools.partial(forward_kernel, heads, rows), out_shape=...  31.9 us
    unnamed x106, local copies, waits for them, and re-layouts  9.04 us
  transfers between devices with their start and end apart: 49, of which 17 were waited for; matrix products, arithmetic and copies ran while one was open for 9% of the time, Pallas kernels for 43%

profile of v3, /device:TPU:0, one launch (start us, length us, event | category | flops | bytes accessed | tf_op | source)
XLA Modules:
  0.0 299.0 jit_solution(10191417483566968563)
XLA Ops:
  12.6 5.3 %collective-permute-done.3 = bf16[1,96,768]{1,2,0:T(8,128)(2,1)S(1)} collective-permute-done((bf16[1,96,768]{1,2,0:T(8,128)(2,1)S(1)}, bf16[1,96,768]{1,2,0:T(8,128)(2,1)S(1)}, u32[]{:S(2)}, u32[]{:S(2)}) %collective-permute-start.3) | collective-permute-done | bytes 147488 | tf_op jit(solution)/shard_map/ppermute | solution.py:35
  19.0 9.4 %collective-permute-done.4 = bf16[2,96,768]{1,2,0:T(8,128)(2,1)S(1)} collective-permute-done((bf16[2,96,768]{1,2,0:T(8,128)(2,1)S(1)}, bf16[2,96,768]{1,2,0:T(8,128)(2,1)S(1)}, u32[]{:S(2)}, u32[]{:S(2)}) %collective-permute-start.4) | collective-permute-done | bytes 294944 | tf_op jit(solution)/shard_map/ppermute | solution.py:35
  28.7 3.1 %collective-permute-start.16 = (bf16[1,96,1536]{2,1,0:T(8,128)(2,1)S(1)}, bf16[1,96,1536]{2,1,0:T(8,128)(2,1)S(1)}, u32[]{:S(2)}, u32[]{:S(2)}) collective-permute-start(bf16[1,96,1536]{2,1,0:T(8,128)(2,1)S(1)} %maximum_bitcast_fusion), channel_id=1, source_target_pairs={{0,16},{4,20},{8,24},{12,28},{16,0},{20,4},{24,8},{28,12},{1,17},{... | collective-permute-start | bytes 884744 | tf_op jit(solution)/shard_map/ppermute | solution.py:35
  37.1 7.7 %collective-permute-done.16 = bf16[1,96,1536]{2,1,0:T(8,128)(2,1)S(1)} collective-permute-done((bf16[1,96,1536]{2,1,0:T(8,128)(2,1)S(1)}, bf16[1,96,1536]{2,1,0:T(8,128)(2,1)S(1)}, u32[]{:S(2)}, u32[]{:S(2)}) %collective-permute-start.16) | collective-permute-done | bytes 294944 | tf_op jit(solution)/shard_map/ppermute | solution.py:35
  53.5 31.9 %attention_forward.1 = (bf16[2048,768]{1,0:T(8,128)(2,1)}, bf16[2048,768]{1,0:T(8,128)(2,1)}, bf16[3,2048,64]{2,1,0:T(8,128)(2,1)}, bf16[3,2048,64]{2,1,0:T(8,12...) custom-call(s32[5]{0:T(128)} %pad_add_fusion.here_ref.order_ref, ...), custom_call_target="tpu_custom_call" | custom-call | flops 4026531840 | bytes 25165824 | tf_op jit(solution)/shard_map/attention_forward/pallas_call | solution.py:185
  91.3 3.8 %collective-permute-done.11.refs_2_ = bf16[192,512]{1,0:T(8,128)(2,1)S(1)} collective-permute-done((bf16[192,512]{1,0:T(8,128)(2,1)S(1)}, bf16[192,512]{1,0:T(8,128)(2,1)S(1)}, u32[]{:S(2)}, u32[]{:S(2)}) %collective-permute-start.11) | collective-permute-done | bytes 196640 | tf_op jit(solution)/shard_map/ppermute | solution.py:35
  95.1 3.3 %collective-permute-done.12.refs_3_ = bf16[192,512]{1,0:T(8,128)(2,1)S(1)} collective-permute-done((bf16[192,512]{1,0:T(8,128)(2,1)S(1)}, bf16[192,512]{1,0:T(8,128)(2,1)S(1)}, u32[]{:S(2)}, u32[]{:S(2)}) %collective-permute-start.12) | collective-permute-done | bytes 196640 | tf_op jit(solution)/shard_map/ppermute | solution.py:35
  99.1 4.4 %branch.1 = (f32[512,768]{1,0:T(8,128)}, bf16[512,768]{1,0:T(8,128)(2,1)}) custom-call(bf16[192,512]{1,0:T(8,128)(2,1)} %get-tuple-element.127.refs_0_, bf16[192,512]{1,0:T(8,128)(2,1)} %copy-done.24, bf16[192,512]{1,0:T(8,128)(2,1)} %copy-done.25, bf16[192,512]{1,0:T(8,128)(2,1)} %copy-done.26, bf16[192,768]{1,0:T(8,128)(2,1)} %turn.1.refs_4_.refs_0_, ...), custom_call_target="tpu_custom_call" | custom-call | flops 603979776 | bytes 5121024 | tf_op jit(solution)/shard_map/branch/pallas_call | solution.py:284
  106.0 8.1 %collective-permute-done.18 = bf16[4,96,1536]{2,1,0:T(8,128)(2,1)} collective-permute-done((bf16[4,96,1536]{2,1,0:T(8,128)(2,1)S(1)}, bf16[4,96,1536]{2,1,0:T(8,128)(2,1)}, u32[]{:S(2)}, u32[]{:S(2)}) %collective-permute-start.18) | collective-permute-done | bytes 1179680 | tf_op jit(solution)/shard_map/ppermute | solution.py:35
  114.1 3.4 %maximum_select_fusion = bf16[4,2,96,1536]{3,2,1,0:T(8,128)(2,1)} fusion(bf16[4,1,96,1536]{3,2,1,0:T(8,128)(2,1)S(1)} %bitcast.84, bf16[4,1,96,1536]{3,2,1,0:T(8,128)(2,1)} %bitcast.27, pred[]{:T(512)S(6)} %gt.12), kind=kLoop, calls=%fused_computation | loop fusion | flops 3538944 | bytes 4718593 | tf_op jit(solution)/shard_map/jit(_where)/select_n | solution.py:52
  118.7 10.3 %hidden.2 = (bf16[512,768]{1,0:T(8,128)(2,1)}, bf16[512,768]{1,0:T(8,128)(2,1)}, bf16[2,512,768]{2,1,0:T(8,128)(2,1)}, bf16[2,512,768]{2,1,0:T(8,128)(2,1)}, f32[1,768]{1,0:T(1,128)}) custom-call(bf16[512,768]{1,0:T(8,128)(2,1)} %get-tuple-element.131.refs_0_, bf16[512,768]{1,0:T(8,128)(2,1)} %copy-done.41, bf16[512,768]{1,0:T(8,128)(2,1)} %copy-done.2, ...), custom_call_target="tpu_custom_call" | custom-call | flops 3623878656 | bytes 10229760 | tf_op jit(solution)/shard_map/hidden/pallas_call | solution.py:284
  132.4 10.2 %hidden.3 = (bf16[512,768]{1,0:T(8,128)(2,1)}, bf16[512,768]{1,0:T(8,128)(2,1)}, bf16[2,512,768]{2,1,0:T(8,128)(2,1)}, bf16[2,512,768]{2,1,0:T(8,128)(2,1)}, f32[1,768]{1,0:T(1,128)}) custom-call(bf16[512,768]{1,0:T(8,128)(2,1)} %collective-permute-done.14.refs_0_.refs_2_, bf16[512,768]{1,0:T(8,128)(2,1)} %copy-done.43, ...), custom_call_target="tpu_custom_call" | custom-call | flops 3623878656 | bytes 10229760 | tf_op jit(solution)/shard_map/hidden/pallas_call | solution.py:284
  143.2 6.8 %hidden_weights.2 = (f32[4,96,768]{2,1,0:T(8,128)}, bf16[4,96,768]{2,1,0:T(8,128)(2,1)}) custom-call(s32[1]{0:T(128)} %bitcast.4.high_ref, bf16[512,768]{1,0:T(8,128)(2,1)} %get-tuple-element.131.refs_0_, bf16[512,768]{1,0:T(8,128)(2,1)} %copy-done.41, bf16[512,768]{1,0:T(8,128)(2,1)} %collective-permute-done.14.refs_0_.refs_2_, ...), custom_call_target="tpu_custom_call" | custom-call | flops 2415919104 | bytes 8060928 | tf_op jit(solution)/shard_map/hidden_weights/pallas_call | solution.py:284
  150.8 6.7 %hidden_weights.3 = (f32[4,96,768]{2,1,0:T(8,128)}, bf16[4,96,768]{2,1,0:T(8,128)(2,1)}) custom-call(s32[1]{0:T(128)} %bitcast.4.high_ref, bf16[512,768]{1,0:T(8,128)(2,1)} %copy-done.2, bf16[512,768]{1,0:T(8,128)(2,1)} %copy-done.39, bf16[512,768]{1,0:T(8,128)(2,1)} %collective-permute-done.6.refs_2_, bf16[512,768]{1,0:T(8,128)(2,1)} %copy-done.42, ...), custom_call_target="tpu_custom_call" | custom-call | flops 2415919104 | bytes 8060928 | tf_op jit(solution)/shard_map/hidden_weights/pallas_call | solution.py:284
  157.5 6.2 %project.1 = (bf16[512,768]{1,0:T(8,128)(2,1)}, bf16[512,768]{1,0:T(8,128)(2,1)}, bf16[512,768]{1,0:T(8,128)(2,1)}, bf16[512,768]{1,0:T(8,128)(2,1)}) custom-call(bf16[2,512,768]{2,1,0:T(8,128)(2,1)} %get-tuple-element.146.refs_4_.refs_0_, bf16[2,512,768]{2,1,0:T(8,128)(2,1)} %get-tuple-element.147.refs_5_.refs_1_, bf16[768,1536]{1,0:T(8,128)(2,1)} %bitcast.89), custom_call_target="tpu_custom_call" | custom-call | flops 2415919104 | bytes 8650752 | tf_op jit(solution)/shard_map/project/pallas_call | solution.py:284
  165.2 4.7 %collective-permute-done.25.far_ref = bf16[512,768]{1,0:T(8,128)(2,1)S(1)} collective-permute-done((bf16[512,768]{1,0:T(8,128)(2,1)S(1)}, bf16[512,768]{1,0:T(8,128)(2,1)S(1)}, u32[]{:S(2)}, u32[]{:S(2)}) %collective-permute-start.25) | collective-permute-done | bytes 786464 | tf_op jit(solution)/shard_map/ppermute | solution.py:35
  171.0 6.0 %middle.1 = (f32[512,768]{1,0:T(8,128)}, bf16[512,768]{1,0:T(8,128)(2,1)}, f32[4,768]{1,0:T(4,128)}, bf16[192,512]{1,0:T(8,128)(2,1)}, bf16[192,512]{1,0:T(8,128...) custom-call(f32[512,768]{1,0:T(8,128)} %get-tuple-element.152.middle_ref, bf16[512,768]{1,0:T(8,128)(2,1)} %copy-done.2, ...), custom_call_target="tpu_custom_call" | custom-call | flops 603979776 | bytes 9059328 | tf_op jit(solution)/shard_map/middle/pallas_call | solution.py:284
  193.5 32.3 %attention_backward.1.part_ref = bf16[2048,576]{1,0:T(8,128)(2,1)} custom-call(s32[4]{0:T(128)} %and_select_fusion.1.start_ref, s32[5]{0:T(128)} %pad_add_fusion.here_ref.order_ref, s32[1,2048]{1,0:T(1,128)} %compare_select_fusion.low_ref, bf16[3,2048,64]{2,1,0:T(8,128)(2,1)} %get-tuple-element.165.q_ref, bf16[3,2048,64]{2,1,0:T(8,128)(2,1)} %get-tuple-element.166.k_ref, ...), custom_call_target="tpu_custom_call" | custom-call | flops 4026531840 | bytes 7110656 | tf_op jit(solution)/shard_map/attention_backward/pallas_call | solution.py:284
  226.7 7.1 %qkv_weights.1 = (f32[4,96,768]{2,1,0:T(8,128)}, bf16[4,96,768]{2,1,0:T(8,128)(2,1)}) custom-call(s32[1]{0:T(128)} %bitcast.4.high_ref, bf16[2048,768]{1,0:T(8,128)(2,1)} %get-tuple-element.186.h1_ref, bf16[2048,576]{1,0:T(8,128)(2,1)} %attention_backward.1.part_ref, bf16[192,768]{1,0:T(8,128)(2,1)} %add_convert_fusion.2.refs_0_), custom_call_target="tpu_custom_call" | custom-call | flops 1811939328 | bytes 7569408 | tf_op jit(solution)/shard_map/qkv_weights/pallas_call | solution.py:284
  233.9 8.5 %first.1 = (bf16[512,768]{1,0:T(8,128)(2,1)}, bf16[512,768]{1,0:T(8,128)(2,1)}, bf16[2,512,768]{2,1,0:T(8,128)(2,1)}, f32[2,768]{1,0:T(2,128)}, f32[1,576]{1,0:T(1,128)}) custom-call(s32[5]{0:T(128)} %pad_add_fusion.here_ref.order_ref, bf16[2048,768]{1,0:T(8,128)(2,1)} %get-tuple-element.150.hat_ref, bf16[768,768]{1,0:T(8,128)(2,1)} %bitcast.82, ...), custom_call_target="tpu_custom_call" | custom-call | flops 1811939328 | bytes 9838848 | tf_op jit(solution)/shard_map/first/pallas_call | solution.py:284
  252.8 3.2 %collective-permute-start.39 = (bf16[4,96,768]{2,1,0:T(8,128)(2,1)}, bf16[4,96,768]{2,1,0:T(8,128)(2,1)S(1)}, u32[]{:S(2)}, u32[]{:S(2)}) collective-permute-start(bf16[4,96,768]{2,1,0:T(8,128)(2,1)} %get-tuple-element.202), channel_id=1, source_target_pairs={{0,4},{4,0},{8,12},{12,8},{16,20},{20,16},{24,28},{28,24},{1,5},{5... | collective-permute-start | bytes 1769480 | tf_op jit(solution)/shard_map/ppermute | solution.py:35
  257.1 6.5 %collective-permute-done.35.got_ref = bf16[2,96,768]{2,1,0:T(8,128)(2,1)S(1)} collective-permute-done((bf16[2,96,768]{2,1,0:T(8,128)(2,1)S(1)}, bf16[2,96,768]{2,1,0:T(8,128)(2,1)S(1)}, u32[]{:S(2)}, u32[]{:S(2)}) %collective-permute-start.35) | collective-permute-done | bytes 294944 | tf_op jit(solution)/shard_map/ppermute | solution.py:35
  266.3 3.7 %collective-permute-done.43 = f32[72,128]{1,0:T(8,128)S(1)} collective-permute-done((f32[72,128]{1,0:T(8,128)S(1)}, f32[72,128]{1,0:T(8,128)S(1)}, u32[]{:S(2)}, u32[]{:S(2)}) %collective-permute-start.43) | collective-permute-done | bytes 36896 | tf_op jit(solution)/shard_map/ppermute | solution.py:35
  292.3 4.7 %token_gradient.1 = bf16[512,768]{1,0:T(8,128)(2,1)} custom-call(bf16[512,768]{1,0:T(8,128)(2,1)} %token_ref.1, f32[1,768]{1,0:T(1,128)} %reshape.518.refs_6_.gain_ref, bf16[512,768]{1,0:T(8,128)(2,1)} %get-tuple-element.189.own_ref, bf16[2,512,768]{2,1,0:T(8,128)(2,1)} %copy-done.1, bf16[512,768]{1,0:T(8,128)(2,1)} %collective-permute-done.38.far_ref, ...), custom_call_target="tpu_custom_call" | custom-call | bytes 6294528 | tf_op jit(solution)/shard_map/token_gradient/pallas_call | solution.py:284
  (278 shorter events, 100.3 us)
Async XLA Ops:
  0.7 51.0 %collective-permute-start = (bf16[512,768]{1,0:T(8,128)(2,1)}, bf16[512,768]{1,0:T(8,128)(2,1)}, u32[]{:S(2)}, u32[]{:S(2)}) collective-permute-start(bf16[512,768]{1,0:T(8,128)(2,1)} %token_ref.1), channel_id=1, source_target_pairs={{0,1},{1,0},{2,3},{3,2},{4,5},{5,4},{6,7},{7,6},{8,9},{9,8},{10,11... | collective-permute-start | bytes 2359304 | tf_op jit(solution)/shard_map/ppermute | solution.py:35
  1.2 30.6 %collective-permute-start.1 = (bf16[512,768]{1,0:T(8,128)(2,1)}, bf16[512,768]{1,0:T(8,128)(2,1)}, u32[]{:S(2)}, u32[]{:S(2)}) collective-permute-start(bf16[512,768]{1,0:T(8,128)(2,1)} %token_ref.1), channel_id=1, source_target_pairs={{0,2},{1,3},{2,0},{3,1},{4,6},{5,7},{6,4},{7,5},{8,10},{9,11},{10,... | collective-permute-start | bytes 2359304 | tf_op jit(solution)/shard_map/ppermute | solution.py:35
  34.2 18.0 %collective-permute-start.2 = (bf16[512,768]{1,0:T(8,128)(2,1)}, bf16[512,768]{1,0:T(8,128)(2,1)}, u32[]{:S(2)}, u32[]{:S(2)}) collective-permute-start(bf16[512,768]{1,0:T(8,128)(2,1)} %collective-permute-done.1.refs_2_), channel_id=1, source_target_pairs={{0,1},{1,0},{2,3},{3,2},{4,5},{5,4},{6,7},{7,6},{8,9},{9,8},{10,11... | collective-permute-start | bytes 2359304 | tf_op jit(solution)/shard_map/ppermute | solution.py:35
  36.6 49.0 %collective-permute-start.6 = (bf16[512,768]{1,0:T(8,128)(2,1)S(1)}, bf16[512,768]{1,0:T(8,128)(2,1)}, u32[]{:S(2)}, u32[]{:S(2)}) collective-permute-start(bf16[512,768]{1,0:T(8,128)(2,1)S(1)} %broadcast_select_fusion.refs_2_.refs_0_.live_grad_ref), channel_id=1, source_target_pairs={{0,2},{1,3},{2,0},{3,1},{4,6},{5,7},{6,4},{7,5},{8,10},{9,11},{10,... | collective-permute-start | bytes 2359304 | tf_op jit(solution)/shard_map/ppermute | solution.py:35
  47.9 37.7 %collective-permute-start.17 = (bf16[2,96,1536]{2,1,0:T(8,128)(2,1)S(1)}, bf16[2,96,1536]{2,1,0:T(8,128)(2,1)S(1)}, u32[]{:S(2)}, u32[]{:S(2)}) collective-permute-start(bf16[2,96,1536]{2,1,0:T(8,128)(2,1)S(1)} %maximum_select_fusion.4), channel_id=1, source_target_pairs={{0,8},{4,12},{8,0},{12,4},{16,24},{20,28},{24,16},{28,20},{1,9},{5... | collective-permute-start | bytes 1769480 | tf_op jit(solution)/shard_map/ppermute | solution.py:35
  51.6 33.9 %collective-permute-start.7 = (bf16[192,768]{1,0:T(8,128)(2,1)}, bf16[192,768]{1,0:T(8,128)(2,1)S(1)}, u32[]{:S(2)}, u32[]{:S(2)}) collective-permute-start(bf16[192,768]{1,0:T(8,128)(2,1)} %turn.1.refs_4_.refs_0_), channel_id=1, source_target_pairs={{0,1},{1,0},{2,3},{3,2},{4,5},{5,4},{6,7},{7,6},{8,9},{9,8},{10,11... | collective-permute-start | bytes 884744 | tf_op jit(solution)/shard_map/ppermute | solution.py:35
  51.6 33.9 %collective-permute-start.8 = (bf16[192,768]{1,0:T(8,128)(2,1)}, bf16[192,768]{1,0:T(8,128)(2,1)S(1)}, u32[]{:S(2)}, u32[]{:S(2)}) collective-permute-start(bf16[192,768]{1,0:T(8,128)(2,1)} %turn.1.refs_4_.refs_0_), channel_id=1, source_target_pairs={{0,2},{1,3},{2,0},{3,1},{4,6},{5,7},{6,4},{7,5},{8,10},{9,11},{10,... | collective-permute-start | bytes 884744 | tf_op jit(solution)/shard_map/ppermute | solution.py:35
  52.1 33.4 %collective-permute-start.9 = (bf16[192,768]{1,0:T(8,128)(2,1)}, bf16[192,768]{1,0:T(8,128)(2,1)S(1)}, u32[]{:S(2)}, u32[]{:S(2)}) collective-permute-start(bf16[192,768]{1,0:T(8,128)(2,1)} %turn.1.refs_4_.refs_0_), channel_id=1, source_target_pairs={{0,3},{1,2},{2,1},{3,0},{4,7},{5,6},{6,5},{7,4},{8,11},{9,10},{10,... | collective-permute-start | bytes 884744 | tf_op jit(solution)/shard_map/ppermute | solution.py:35
  85.8 28.3 %collective-permute-start.18 = (bf16[4,96,1536]{2,1,0:T(8,128)(2,1)S(1)}, bf16[4,96,1536]{2,1,0:T(8,128)(2,1)}, u32[]{:S(2)}, u32[]{:S(2)}) collective-permute-start(bf16[4,96,1536]{2,1,0:T(8,128)(2,1)S(1)} %bitcast.83), channel_id=1, source_target_pairs={{0,4},{4,0},{8,12},{12,8},{16,20},{20,16},{24,28},{28,24},{1,5},{5... | collective-permute-start | bytes 3538952 | tf_op jit(solution)/shard_map/ppermute | solution.py:35
  89.2 28.3 %collective-permute-start.15 = (bf16[512,768]{1,0:T(8,128)(2,1)S(1)}, bf16[512,768]{1,0:T(8,128)(2,1)S(1)}, u32[]{:S(2)}, u32[]{:S(2)}) collective-permute-start(bf16[512,768]{1,0:T(8,128)(2,1)S(1)} %broadcast_select_fusion.refs_2_.refs_0_.live_grad_ref), channel_id=1, source_target_pairs={{0,1},{1,0},{2,3},{3,2},{4,5},{5,4},{6,7},{7,6},{8,9},{9,8},{10,11... | collective-permute-start | bytes 2359304 | tf_op jit(solution)/shard_map/ppermute | solution.py:35
  104.2 24.8 %collective-permute-start.14 = (bf16[512,768]{1,0:T(8,128)(2,1)}, bf16[512,768]{1,0:T(8,128)(2,1)}, u32[]{:S(2)}, u32[]{:S(2)}) collective-permute-start(bf16[512,768]{1,0:T(8,128)(2,1)} %get-tuple-element.131.refs_0_), channel_id=1, source_target_pairs={{0,2},{1,3},{2,0},{3,1},{4,6},{5,7},{6,4},{7,5},{8,10},{9,11},{10,... | collective-permute-start | bytes 2359304 | tf_op jit(solution)/shard_map/ppermute | solution.py:35
  106.0 23.0 %collective-permute-start.20 = (bf16[512,768]{1,0:T(8,128)(2,1)}, bf16[512,768]{1,0:T(8,128)(2,1)S(1)}, u32[]{:S(2)}, u32[]{:S(2)}) collective-permute-start(bf16[512,768]{1,0:T(8,128)(2,1)} %collective-permute-done.6.refs_2_), channel_id=1, source_target_pairs={{0,1},{1,0},{2,3},{3,2},{4,5},{5,4},{6,7},{7,6},{8,9},{9,8},{10,11... | collective-permute-start | bytes 2359304 | tf_op jit(solution)/shard_map/ppermute | solution.py:35
  142.8 27.1 %collective-permute-start.24 = (bf16[512,768]{1,0:T(8,128)(2,1)S(1)}, bf16[512,768]{1,0:T(8,128)(2,1)S(1)}, u32[]{:S(2)}, u32[]{:S(2)}) collective-permute-start(bf16[512,768]{1,0:T(8,128)(2,1)S(1)} %copy-done.40), channel_id=1, source_target_pairs={{0,1},{1,0},{2,3},{3,2},{4,5},{5,4},{6,7},{7,6},{8,9},{9,8},{10,11... | collective-permute-start | bytes 2359304 | tf_op jit(solution)/shard_map/ppermute | solution.py:35
  150.2 19.7 %collective-permute-start.25 = (bf16[512,768]{1,0:T(8,128)(2,1)S(1)}, bf16[512,768]{1,0:T(8,128)(2,1)S(1)}, u32[]{:S(2)}, u32[]{:S(2)}) collective-permute-start(bf16[512,768]{1,0:T(8,128)(2,1)S(1)} %add_convert_fusion.1), channel_id=1, source_target_pairs={{0,2},{1,3},{2,0},{3,1},{4,6},{5,7},{6,4},{7,5},{8,10},{9,11},{10,... | collective-permute-start | bytes 2359304 | tf_op jit(solution)/shard_map/ppermute | solution.py:35
  163.7 18.4 %collective-permute-start.23 = (bf16[4,96,768]{2,1,0:T(8,128)(2,1)}, bf16[4,96,768]{2,1,0:T(8,128)(2,1)S(1)}, u32[]{:S(2)}, u32[]{:S(2)}) collective-permute-start(bf16[4,96,768]{2,1,0:T(8,128)(2,1)} %get-tuple-element.151), channel_id=1, source_target_pairs={{0,4},{4,0},{8,12},{12,8},{16,20},{20,16},{24,28},{28,24},{1,5},{5... | collective-permute-start | bytes 1769480 | tf_op jit(solution)/shard_map/ppermute | solution.py:35
  182.1 44.6 %collective-permute-start.34 = (bf16[512,768]{1,0:T(8,128)(2,1)S(1)}, bf16[512,768]{1,0:T(8,128)(2,1)S(1)}, u32[]{:S(2)}, u32[]{:S(2)}) collective-permute-start(bf16[512,768]{1,0:T(8,128)(2,1)S(1)} %add_convert_fusion), channel_id=1, source_target_pairs={{0,2},{1,3},{2,0},{3,1},{4,6},{5,7},{6,4},{7,5},{8,10},{9,11},{10,... | collective-permute-start | bytes 2359304 | tf_op jit(solution)/shard_map/ppermute | solution.py:35
  185.4 41.2 %collective-permute-start.22 = (bf16[4,96,768]{2,1,0:T(8,128)(2,1)S(1)}, bf16[4,96,768]{2,1,0:T(8,128)(2,1)S(1)}, u32[]{:S(2)}, u32[]{:S(2)}) collective-permute-start(bf16[4,96,768]{2,1,0:T(8,128)(2,1)S(1)} %copy-done.44), channel_id=1, source_target_pairs={{0,4},{4,0},{8,12},{12,8},{16,20},{20,16},{24,28},{28,24},{1,5},{5... | collective-permute-start | bytes 1769480 | tf_op jit(solution)/shard_map/ppermute | solution.py:35
  188.8 37.0 %collective-permute-start.31 = (bf16[192,768]{1,0:T(8,128)(2,1)}, bf16[192,768]{1,0:T(8,128)(2,1)S(1)}, u32[]{:S(2)}, u32[]{:S(2)}) collective-permute-start(bf16[192,768]{1,0:T(8,128)(2,1)} %get-tuple-element.175), channel_id=1, source_target_pairs={{0,2},{1,3},{2,0},{3,1},{4,6},{5,7},{6,4},{7,5},{8,10},{9,11},{10,... | collective-permute-start | bytes 884744 | tf_op jit(solution)/shard_map/ppermute | solution.py:35
  191.2 34.6 %collective-permute-start.32 = (bf16[192,768]{1,0:T(8,128)(2,1)S(1)}, bf16[192,768]{1,0:T(8,128)(2,1)S(1)}, u32[]{:S(2)}, u32[]{:S(2)}) collective-permute-start(bf16[192,768]{1,0:T(8,128)(2,1)S(1)} %copy-done.45), channel_id=1, source_target_pairs={{0,3},{1,2},{2,1},{3,0},{4,7},{5,6},{6,5},{7,4},{8,11},{9,10},{10,... | collective-permute-start | bytes 884744 | tf_op jit(solution)/shard_map/ppermute | solution.py:35
  193.1 33.6 %collective-permute-start.33 = (bf16[2,96,768]{2,1,0:T(8,128)(2,1)}, bf16[2,96,768]{2,1,0:T(8,128)(2,1)S(1)}, u32[]{:S(2)}, u32[]{:S(2)}) collective-permute-start(bf16[2,96,768]{2,1,0:T(8,128)(2,1)} %get-tuple-element.182), channel_id=1, source_target_pairs={{0,8},{4,12},{8,0},{12,4},{16,24},{20,28},{24,16},{28,20},{1,9},{5... | collective-permute-start | bytes 884744 | tf_op jit(solution)/shard_map/ppermute | solution.py:35
  242.7 27.4 %collective-permute-start.37 = (bf16[512,768]{1,0:T(8,128)(2,1)}, bf16[512,768]{1,0:T(8,128)(2,1)}, u32[]{:S(2)}, u32[]{:S(2)}) collective-permute-start(bf16[512,768]{1,0:T(8,128)(2,1)} %get-tuple-element.201), channel_id=1, source_target_pairs={{0,1},{1,0},{2,3},{3,2},{4,5},{5,4},{6,7},{7,6},{8,9},{9,8},{10,11... | collective-permute-start | bytes 2359304 | tf_op jit(solution)/shard_map/ppermute | solution.py:35
  252.8 21.3 %collective-permute-start.39 = (bf16[4,96,768]{2,1,0:T(8,128)(2,1)}, bf16[4,96,768]{2,1,0:T(8,128)(2,1)S(1)}, u32[]{:S(2)}, u32[]{:S(2)}) collective-permute-start(bf16[4,96,768]{2,1,0:T(8,128)(2,1)} %get-tuple-element.202), channel_id=1, source_target_pairs={{0,4},{4,0},{8,12},{12,8},{16,20},{20,16},{24,28},{28,24},{1,5},{5... | collective-permute-start | bytes 1769480 | tf_op jit(solution)/shard_map/ppermute | solution.py:35
  257.1 21.1 %collective-permute-start.47 = (bf16[1,96,768]{2,1,0:T(8,128)(2,1)}, bf16[1,96,768]{2,1,0:T(8,128)(2,1)S(1)}, u32[]{:S(2)}, u32[]{:S(2)}) collective-permute-start(bf16[1,96,768]{2,1,0:T(8,128)(2,1)} %get-tuple-element.216), channel_id=1, source_target_pairs={{0,16},{4,20},{8,24},{12,28},{16,0},{20,4},{24,8},{28,12},{1,17},{... | collective-permute-start | bytes 442376 | tf_op jit(solution)/shard_map/ppermute | solution.py:35
  263.6 28.7 %collective-permute-start.38 = (bf16[512,768]{1,0:T(8,128)(2,1)}, bf16[512,768]{1,0:T(8,128)(2,1)}, u32[]{:S(2)}, u32[]{:S(2)}) collective-permute-start(bf16[512,768]{1,0:T(8,128)(2,1)} %fusion), channel_id=1, source_target_pairs={{0,2},{1,3},{2,0},{3,1},{4,6},{5,7},{6,4},{7,5},{8,10},{9,11},{10,... | collective-permute-start | bytes 2359304 | tf_op jit(solution)/shard_map/ppermute | solution.py:35
  (76 other events, 689.4 us)

commit v4 on v3

--- a/solution.py
+++ b/solution.py
@@ -105,7 +105,7 @@
     send_refs, token_all = refs[count + 11 : -1], refs[-1]
     here = here_ref[count]
     local_rows = token_refs[0].shape[0]
-    chunk = 256
+    chunk = 512
     for r in range(count):
         token_all[r] = token_refs[r][...]
     if True:
@@ -395,7 +395,7 @@
     rows, width = h2s[0].shape
     cols = packed.shape[1] // 2
     return kernel_call(
-        functools.partial(hidden_kernel, count, 256),
+        functools.partial(hidden_kernel, count, 512),
         "hidden",
         [shape((rows, width), BF)] * count
         + [shape((count, rows, cols), BF)] * 2

time: 300 us -> 301 us (level)
  transfers between devices with their start and end apart: 49 -> 49, of which waited for: 17 -> 18; matrix products, arithmetic and copies ran while one was open for 9% -> 9% of each run, Pallas kernels for 43% -> 43%
where the time goes in v4:
time: 301 us; the launch traced here: 297 us
  Pallas kernels  152 us (50%)
  waiting for transfers between devices  64.9 us (22%)
  starting transfers between devices  43.4 us (14%)
  local copies, waits for them, and re-layouts  17.6 us (6%)
  other arithmetic  17.3 us (6%)
    pallas_call x19, Pallas kernels, kernel_call(): pl.pallas_call(body, out_shape=tuple(out_shape), in_specs=smem(len(scalar...  120 us
    ppermute x49, waiting for transfers between devices, swap(): return lax.ppermute(value, axis, [(i, i ^ bits) for i in range(size)])  64.9 us
    ppermute x49, starting transfers between devices, swap(): return lax.ppermute(value, axis, [(i, i ^ bits) for i in range(size)])  43.4 us
    pallas_call x1, Pallas kernels, attention_forward(): pl.pallas_call(functools.partial(forward_kernel, heads, rows), out_shape=...  31.6 us
    unnamed x106, local copies, waits for them, and re-layouts  8.46 us
  transfers between devices with their start and end apart: 49, of which 18 were waited for; matrix products, arithmetic and copies ran while one was open for 9% of the time, Pallas kernels for 43%

profile of v4, /device:TPU:0, one launch (start us, length us, event | category | flops | bytes accessed | tf_op | source)
XLA Modules:
  0.0 297.0 jit_solution(17486300204970378488)
XLA Ops:
  12.6 5.3 %collective-permute-done.3 = bf16[1,96,768]{1,2,0:T(8,128)(2,1)S(1)} collective-permute-done((bf16[1,96,768]{1,2,0:T(8,128)(2,1)S(1)}, bf16[1,96,768]{1,2,0:T(8,128)(2,1)S(1)}, u32[]{:S(2)}, u32[]{:S(2)}) %collective-permute-start.3) | collective-permute-done | bytes 147488 | tf_op jit(solution)/shard_map/ppermute | solution.py:35
  19.0 9.4 %collective-permute-done.4 = bf16[2,96,768]{1,2,0:T(8,128)(2,1)S(1)} collective-permute-done((bf16[2,96,768]{1,2,0:T(8,128)(2,1)S(1)}, bf16[2,96,768]{1,2,0:T(8,128)(2,1)S(1)}, u32[]{:S(2)}, u32[]{:S(2)}) %collective-permute-start.4) | collective-permute-done | bytes 294944 | tf_op jit(solution)/shard_map/ppermute | solution.py:35
  28.7 3.1 %collective-permute-start.16 = (bf16[1,96,1536]{2,1,0:T(8,128)(2,1)S(1)}, bf16[1,96,1536]{2,1,0:T(8,128)(2,1)S(1)}, u32[]{:S(2)}, u32[]{:S(2)}) collective-permute-start(bf16[1,96,1536]{2,1,0:T(8,128)(2,1)S(1)} %maximum_bitcast_fusion), channel_id=1, source_target_pairs={{0,16},{4,20},{8,24},{12,28},{16,0},{20,4},{24,8},{28,12},{1,17},{... | collective-permute-start | bytes 884744 | tf_op jit(solution)/shard_map/ppermute | solution.py:35
  37.1 7.7 %collective-permute-done.16 = bf16[1,96,1536]{2,1,0:T(8,128)(2,1)S(1)} collective-permute-done((bf16[1,96,1536]{2,1,0:T(8,128)(2,1)S(1)}, bf16[1,96,1536]{2,1,0:T(8,128)(2,1)S(1)}, u32[]{:S(2)}, u32[]{:S(2)}) %collective-permute-start.16) | collective-permute-done | bytes 294944 | tf_op jit(solution)/shard_map/ppermute | solution.py:35
  53.5 31.6 %attention_forward.1 = (bf16[2048,768]{1,0:T(8,128)(2,1)}, bf16[2048,768]{1,0:T(8,128)(2,1)}, bf16[3,2048,64]{2,1,0:T(8,128)(2,1)}, bf16[3,2048,64]{2,1,0:T(8,12...) custom-call(s32[5]{0:T(128)} %pad_add_fusion.here_ref.order_ref, ...), custom_call_target="tpu_custom_call" | custom-call | flops 4026531840 | bytes 25165824 | tf_op jit(solution)/shard_map/attention_forward/pallas_call | solution.py:185
  91.0 3.8 %collective-permute-done.11.refs_2_ = bf16[192,512]{1,0:T(8,128)(2,1)S(1)} collective-permute-done((bf16[192,512]{1,0:T(8,128)(2,1)S(1)}, bf16[192,512]{1,0:T(8,128)(2,1)S(1)}, u32[]{:S(2)}, u32[]{:S(2)}) %collective-permute-start.11) | collective-permute-done | bytes 196640 | tf_op jit(solution)/shard_map/ppermute | solution.py:35
  94.8 3.3 %collective-permute-done.12.refs_3_ = bf16[192,512]{1,0:T(8,128)(2,1)S(1)} collective-permute-done((bf16[192,512]{1,0:T(8,128)(2,1)S(1)}, bf16[192,512]{1,0:T(8,128)(2,1)S(1)}, u32[]{:S(2)}, u32[]{:S(2)}) %collective-permute-start.12) | collective-permute-done | bytes 196640 | tf_op jit(solution)/shard_map/ppermute | solution.py:35
  98.8 4.4 %branch.1 = (f32[512,768]{1,0:T(8,128)}, bf16[512,768]{1,0:T(8,128)(2,1)}) custom-call(bf16[192,512]{1,0:T(8,128)(2,1)} %get-tuple-element.127.refs_0_, bf16[192,512]{1,0:T(8,128)(2,1)} %copy-done.24, bf16[192,512]{1,0:T(8,128)(2,1)} %copy-done.25, bf16[192,512]{1,0:T(8,128)(2,1)} %copy-done.26, bf16[192,768]{1,0:T(8,128)(2,1)} %turn.1.refs_4_.refs_0_, ...), custom_call_target="tpu_custom_call" | custom-call | flops 603979776 | bytes 5121024 | tf_op jit(solution)/shard_map/branch/pallas_call | solution.py:284
  105.7 8.1 %collective-permute-done.18 = bf16[4,96,1536]{2,1,0:T(8,128)(2,1)} collective-permute-done((bf16[4,96,1536]{2,1,0:T(8,128)(2,1)S(1)}, bf16[4,96,1536]{2,1,0:T(8,128)(2,1)}, u32[]{:S(2)}, u32[]{:S(2)}) %collective-permute-start.18) | collective-permute-done | bytes 1179680 | tf_op jit(solution)/shard_map/ppermute | solution.py:35
  113.8 3.4 %maximum_select_fusion = bf16[4,2,96,1536]{3,2,1,0:T(8,128)(2,1)} fusion(bf16[4,1,96,1536]{3,2,1,0:T(8,128)(2,1)S(1)} %bitcast.84, bf16[4,1,96,1536]{3,2,1,0:T(8,128)(2,1)} %bitcast.27, pred[]{:T(512)S(6)} %gt.12), kind=kLoop, calls=%fused_computation | loop fusion | flops 3538944 | bytes 4718593 | tf_op jit(solution)/shard_map/jit(_where)/select_n | solution.py:52
  118.4 9.6 %hidden.2 = (bf16[512,768]{1,0:T(8,128)(2,1)}, bf16[512,768]{1,0:T(8,128)(2,1)}, bf16[2,512,768]{2,1,0:T(8,128)(2,1)}, bf16[2,512,768]{2,1,0:T(8,128)(2,1)}, f32[1,768]{1,0:T(1,128)}) custom-call(bf16[512,768]{1,0:T(8,128)(2,1)} %get-tuple-element.131.refs_0_, bf16[512,768]{1,0:T(8,128)(2,1)} %copy-done.41, bf16[512,768]{1,0:T(8,128)(2,1)} %copy-done.2, ...), custom_call_target="tpu_custom_call" | custom-call | flops 3623878656 | bytes 10229760 | tf_op jit(solution)/shard_map/hidden/pallas_call | solution.py:284
  131.4 9.6 %hidden.3 = (bf16[512,768]{1,0:T(8,128)(2,1)}, bf16[512,768]{1,0:T(8,128)(2,1)}, bf16[2,512,768]{2,1,0:T(8,128)(2,1)}, bf16[2,512,768]{2,1,0:T(8,128)(2,1)}, f32[1,768]{1,0:T(1,128)}) custom-call(bf16[512,768]{1,0:T(8,128)(2,1)} %collective-permute-done.14.refs_0_.refs_2_, bf16[512,768]{1,0:T(8,128)(2,1)} %copy-done.43, ...), custom_call_target="tpu_custom_call" | custom-call | flops 3623878656 | bytes 10229760 | tf_op jit(solution)/shard_map/hidden/pallas_call | solution.py:284
  141.5 6.8 %hidden_weights.2 = (f32[4,96,768]{2,1,0:T(8,128)}, bf16[4,96,768]{2,1,0:T(8,128)(2,1)}) custom-call(s32[1]{0:T(128)} %bitcast.4.high_ref, bf16[512,768]{1,0:T(8,128)(2,1)} %get-tuple-element.131.refs_0_, bf16[512,768]{1,0:T(8,128)(2,1)} %copy-done.41, bf16[512,768]{1,0:T(8,128)(2,1)} %collective-permute-done.14.refs_0_.refs_2_, ...), custom_call_target="tpu_custom_call" | custom-call | flops 2415919104 | bytes 8060928 | tf_op jit(solution)/shard_map/hidden_weights/pallas_call | solution.py:284
  149.1 6.7 %hidden_weights.3 = (f32[4,96,768]{2,1,0:T(8,128)}, bf16[4,96,768]{2,1,0:T(8,128)(2,1)}) custom-call(s32[1]{0:T(128)} %bitcast.4.high_ref, bf16[512,768]{1,0:T(8,128)(2,1)} %copy-done.2, bf16[512,768]{1,0:T(8,128)(2,1)} %copy-done.39, bf16[512,768]{1,0:T(8,128)(2,1)} %collective-permute-done.6.refs_2_, bf16[512,768]{1,0:T(8,128)(2,1)} %copy-done.42, ...), custom_call_target="tpu_custom_call" | custom-call | flops 2415919104 | bytes 8060928 | tf_op jit(solution)/shard_map/hidden_weights/pallas_call | solution.py:284
  155.9 6.2 %project.1 = (bf16[512,768]{1,0:T(8,128)(2,1)}, bf16[512,768]{1,0:T(8,128)(2,1)}, bf16[512,768]{1,0:T(8,128)(2,1)}, bf16[512,768]{1,0:T(8,128)(2,1)}) custom-call(bf16[2,512,768]{2,1,0:T(8,128)(2,1)} %get-tuple-element.146.refs_4_.refs_0_, bf16[2,512,768]{2,1,0:T(8,128)(2,1)} %get-tuple-element.147.refs_5_.refs_1_, bf16[768,1536]{1,0:T(8,128)(2,1)} %bitcast.89), custom_call_target="tpu_custom_call" | custom-call | flops 2415919104 | bytes 8650752 | tf_op jit(solution)/shard_map/project/pallas_call | solution.py:284
  163.6 4.6 %collective-permute-done.25.far_ref = bf16[512,768]{1,0:T(8,128)(2,1)S(1)} collective-permute-done((bf16[512,768]{1,0:T(8,128)(2,1)S(1)}, bf16[512,768]{1,0:T(8,128)(2,1)S(1)}, u32[]{:S(2)}, u32[]{:S(2)}) %collective-permute-start.25) | collective-permute-done | bytes 786464 | tf_op jit(solution)/shard_map/ppermute | solution.py:35
  169.3 6.0 %middle.1 = (f32[512,768]{1,0:T(8,128)}, bf16[512,768]{1,0:T(8,128)(2,1)}, f32[4,768]{1,0:T(4,128)}, bf16[192,512]{1,0:T(8,128)(2,1)}, bf16[192,512]{1,0:T(8,128...) custom-call(f32[512,768]{1,0:T(8,128)} %get-tuple-element.152.middle_ref, bf16[512,768]{1,0:T(8,128)(2,1)} %copy-done.2, ...), custom_call_target="tpu_custom_call" | custom-call | flops 603979776 | bytes 9059328 | tf_op jit(solution)/shard_map/middle/pallas_call | solution.py:284
  191.5 32.3 %attention_backward.1.part_ref = bf16[2048,576]{1,0:T(8,128)(2,1)} custom-call(s32[4]{0:T(128)} %and_select_fusion.1.start_ref, s32[5]{0:T(128)} %pad_add_fusion.here_ref.order_ref, s32[1,2048]{1,0:T(1,128)} %compare_select_fusion.low_ref, bf16[3,2048,64]{2,1,0:T(8,128)(2,1)} %get-tuple-element.165.q_ref, bf16[3,2048,64]{2,1,0:T(8,128)(2,1)} %get-tuple-element.166.k_ref, ...), custom_call_target="tpu_custom_call" | custom-call | flops 4026531840 | bytes 7110656 | tf_op jit(solution)/shard_map/attention_backward/pallas_call | solution.py:284
  224.8 7.1 %qkv_weights.1 = (f32[4,96,768]{2,1,0:T(8,128)}, bf16[4,96,768]{2,1,0:T(8,128)(2,1)}) custom-call(s32[1]{0:T(128)} %bitcast.4.high_ref, bf16[2048,768]{1,0:T(8,128)(2,1)} %get-tuple-element.186.h1_ref, bf16[2048,576]{1,0:T(8,128)(2,1)} %attention_backward.1.part_ref, bf16[192,768]{1,0:T(8,128)(2,1)} %add_convert_fusion.2.refs_0_), custom_call_target="tpu_custom_call" | custom-call | flops 1811939328 | bytes 7569408 | tf_op jit(solution)/shard_map/qkv_weights/pallas_call | solution.py:284
  231.9 8.5 %first.1 = (bf16[512,768]{1,0:T(8,128)(2,1)}, bf16[512,768]{1,0:T(8,128)(2,1)}, bf16[2,512,768]{2,1,0:T(8,128)(2,1)}, f32[2,768]{1,0:T(2,128)}, f32[1,576]{1,0:T(1,128)}) custom-call(s32[5]{0:T(128)} %pad_add_fusion.here_ref.order_ref, bf16[2048,768]{1,0:T(8,128)(2,1)} %get-tuple-element.150.hat_ref, bf16[768,768]{1,0:T(8,128)(2,1)} %bitcast.82, ...), custom_call_target="tpu_custom_call" | custom-call | flops 1811939328 | bytes 9838848 | tf_op jit(solution)/shard_map/first/pallas_call | solution.py:284
  255.8 4.2 %collective-permute-done.35.got_ref = bf16[2,96,768]{2,1,0:T(8,128)(2,1)S(1)} collective-permute-done((bf16[2,96,768]{2,1,0:T(8,128)(2,1)S(1)}, bf16[2,96,768]{2,1,0:T(8,128)(2,1)S(1)}, u32[]{:S(2)}, u32[]{:S(2)}) %collective-permute-start.35) | collective-permute-done | bytes 294944 | tf_op jit(solution)/shard_map/ppermute | solution.py:35
  262.6 4.3 %collective-permute-done.43 = f32[72,128]{1,0:T(8,128)S(1)} collective-permute-done((f32[72,128]{1,0:T(8,128)S(1)}, f32[72,128]{1,0:T(8,128)S(1)}, u32[]{:S(2)}, u32[]{:S(2)}) %collective-permute-start.43) | collective-permute-done | bytes 36896 | tf_op jit(solution)/shard_map/ppermute | solution.py:35
  279.0 3.1 %collective-permute-done.45 = f32[72,128]{1,0:T(8,128)S(1)} collective-permute-done((f32[72,128]{1,0:T(8,128)S(1)}, f32[72,128]{1,0:T(8,128)S(1)}, u32[]{:S(2)}, u32[]{:S(2)}) %collective-permute-start.45) | collective-permute-done | bytes 36896 | tf_op jit(solution)/shard_map/ppermute | solution.py:35
  289.9 4.7 %token_gradient.1 = bf16[512,768]{1,0:T(8,128)(2,1)} custom-call(bf16[512,768]{1,0:T(8,128)(2,1)} %token_ref.1, f32[1,768]{1,0:T(1,128)} %reshape.518.refs_6_.gain_ref, bf16[512,768]{1,0:T(8,128)(2,1)} %get-tuple-element.189.own_ref, bf16[2,512,768]{2,1,0:T(8,128)(2,1)} %copy-done.1, bf16[512,768]{1,0:T(8,128)(2,1)} %collective-permute-done.38.far_ref, ...), custom_call_target="tpu_custom_call" | custom-call | bytes 6294528 | tf_op jit(solution)/shard_map/token_gradient/pallas_call | solution.py:284
  (278 shorter events, 101.4 us)
Async XLA Ops:
  0.7 51.0 %collective-permute-start = (bf16[512,768]{1,0:T(8,128)(2,1)}, bf16[512,768]{1,0:T(8,128)(2,1)}, u32[]{:S(2)}, u32[]{:S(2)}) collective-permute-start(bf16[512,768]{1,0:T(8,128)(2,1)} %token_ref.1), channel_id=1, source_target_pairs={{0,1},{1,0},{2,3},{3,2},{4,5},{5,4},{6,7},{7,6},{8,9},{9,8},{10,11... | collective-permute-start | bytes 2359304 | tf_op jit(solution)/shard_map/ppermute | solution.py:35
  1.2 30.6 %collective-permute-start.1 = (bf16[512,768]{1,0:T(8,128)(2,1)}, bf16[512,768]{1,0:T(8,128)(2,1)}, u32[]{:S(2)}, u32[]{:S(2)}) collective-permute-start(bf16[512,768]{1,0:T(8,128)(2,1)} %token_ref.1), channel_id=1, source_target_pairs={{0,2},{1,3},{2,0},{3,1},{4,6},{5,7},{6,4},{7,5},{8,10},{9,11},{10,... | collective-permute-start | bytes 2359304 | tf_op jit(solution)/shard_map/ppermute | solution.py:35
  34.2 18.0 %collective-permute-start.2 = (bf16[512,768]{1,0:T(8,128)(2,1)}, bf16[512,768]{1,0:T(8,128)(2,1)}, u32[]{:S(2)}, u32[]{:S(2)}) collective-permute-start(bf16[512,768]{1,0:T(8,128)(2,1)} %collective-permute-done.1.refs_2_), channel_id=1, source_target_pairs={{0,1},{1,0},{2,3},{3,2},{4,5},{5,4},{6,7},{7,6},{8,9},{9,8},{10,11... | collective-permute-start | bytes 2359304 | tf_op jit(solution)/shard_map/ppermute | solution.py:35
  36.6 48.6 %collective-permute-start.6 = (bf16[512,768]{1,0:T(8,128)(2,1)S(1)}, bf16[512,768]{1,0:T(8,128)(2,1)}, u32[]{:S(2)}, u32[]{:S(2)}) collective-permute-start(bf16[512,768]{1,0:T(8,128)(2,1)S(1)} %broadcast_select_fusion.refs_2_.refs_0_.live_grad_ref), channel_id=1, source_target_pairs={{0,2},{1,3},{2,0},{3,1},{4,6},{5,7},{6,4},{7,5},{8,10},{9,11},{10,... | collective-permute-start | bytes 2359304 | tf_op jit(solution)/shard_map/ppermute | solution.py:35
  47.9 37.4 %collective-permute-start.17 = (bf16[2,96,1536]{2,1,0:T(8,128)(2,1)S(1)}, bf16[2,96,1536]{2,1,0:T(8,128)(2,1)S(1)}, u32[]{:S(2)}, u32[]{:S(2)}) collective-permute-start(bf16[2,96,1536]{2,1,0:T(8,128)(2,1)S(1)} %maximum_select_fusion.4), channel_id=1, source_target_pairs={{0,8},{4,12},{8,0},{12,4},{16,24},{20,28},{24,16},{28,20},{1,9},{5... | collective-permute-start | bytes 1769480 | tf_op jit(solution)/shard_map/ppermute | solution.py:35
  51.6 33.6 %collective-permute-start.7 = (bf16[192,768]{1,0:T(8,128)(2,1)}, bf16[192,768]{1,0:T(8,128)(2,1)S(1)}, u32[]{:S(2)}, u32[]{:S(2)}) collective-permute-start(bf16[192,768]{1,0:T(8,128)(2,1)} %turn.1.refs_4_.refs_0_), channel_id=1, source_target_pairs={{0,1},{1,0},{2,3},{3,2},{4,5},{5,4},{6,7},{7,6},{8,9},{9,8},{10,11... | collective-permute-start | bytes 884744 | tf_op jit(solution)/shard_map/ppermute | solution.py:35
  51.6 33.6 %collective-permute-start.8 = (bf16[192,768]{1,0:T(8,128)(2,1)}, bf16[192,768]{1,0:T(8,128)(2,1)S(1)}, u32[]{:S(2)}, u32[]{:S(2)}) collective-permute-start(bf16[192,768]{1,0:T(8,128)(2,1)} %turn.1.refs_4_.refs_0_), channel_id=1, source_target_pairs={{0,2},{1,3},{2,0},{3,1},{4,6},{5,7},{6,4},{7,5},{8,10},{9,11},{10,... | collective-permute-start | bytes 884744 | tf_op jit(solution)/shard_map/ppermute | solution.py:35
  52.1 33.1 %collective-permute-start.9 = (bf16[192,768]{1,0:T(8,128)(2,1)}, bf16[192,768]{1,0:T(8,128)(2,1)S(1)}, u32[]{:S(2)}, u32[]{:S(2)}) collective-permute-start(bf16[192,768]{1,0:T(8,128)(2,1)} %turn.1.refs_4_.refs_0_), channel_id=1, source_target_pairs={{0,3},{1,2},{2,1},{3,0},{4,7},{5,6},{6,5},{7,4},{8,11},{9,10},{10,... | collective-permute-start | bytes 884744 | tf_op jit(solution)/shard_map/ppermute | solution.py:35
  85.4 28.3 %collective-permute-start.18 = (bf16[4,96,1536]{2,1,0:T(8,128)(2,1)S(1)}, bf16[4,96,1536]{2,1,0:T(8,128)(2,1)}, u32[]{:S(2)}, u32[]{:S(2)}) collective-permute-start(bf16[4,96,1536]{2,1,0:T(8,128)(2,1)S(1)} %bitcast.83), channel_id=1, source_target_pairs={{0,4},{4,0},{8,12},{12,8},{16,20},{20,16},{24,28},{28,24},{1,5},{5... | collective-permute-start | bytes 3538952 | tf_op jit(solution)/shard_map/ppermute | solution.py:35
  88.9 28.3 %collective-permute-start.15 = (bf16[512,768]{1,0:T(8,128)(2,1)S(1)}, bf16[512,768]{1,0:T(8,128)(2,1)S(1)}, u32[]{:S(2)}, u32[]{:S(2)}) collective-permute-start(bf16[512,768]{1,0:T(8,128)(2,1)S(1)} %broadcast_select_fusion.refs_2_.refs_0_.live_grad_ref), channel_id=1, source_target_pairs={{0,1},{1,0},{2,3},{3,2},{4,5},{5,4},{6,7},{7,6},{8,9},{9,8},{10,11... | collective-permute-start | bytes 2359304 | tf_op jit(solution)/shard_map/ppermute | solution.py:35
  103.8 24.1 %collective-permute-start.14 = (bf16[512,768]{1,0:T(8,128)(2,1)}, bf16[512,768]{1,0:T(8,128)(2,1)}, u32[]{:S(2)}, u32[]{:S(2)}) collective-permute-start(bf16[512,768]{1,0:T(8,128)(2,1)} %get-tuple-element.131.refs_0_), channel_id=1, source_target_pairs={{0,2},{1,3},{2,0},{3,1},{4,6},{5,7},{6,4},{7,5},{8,10},{9,11},{10,... | collective-permute-start | bytes 2359304 | tf_op jit(solution)/shard_map/ppermute | solution.py:35
  105.7 22.4 %collective-permute-start.20 = (bf16[512,768]{1,0:T(8,128)(2,1)}, bf16[512,768]{1,0:T(8,128)(2,1)S(1)}, u32[]{:S(2)}, u32[]{:S(2)}) collective-permute-start(bf16[512,768]{1,0:T(8,128)(2,1)} %collective-permute-done.6.refs_2_), channel_id=1, source_target_pairs={{0,1},{1,0},{2,3},{3,2},{4,5},{5,4},{6,7},{7,6},{8,9},{9,8},{10,11... | collective-permute-start | bytes 2359304 | tf_op jit(solution)/shard_map/ppermute | solution.py:35
  141.1 27.1 %collective-permute-start.24 = (bf16[512,768]{1,0:T(8,128)(2,1)S(1)}, bf16[512,768]{1,0:T(8,128)(2,1)S(1)}, u32[]{:S(2)}, u32[]{:S(2)}) collective-permute-start(bf16[512,768]{1,0:T(8,128)(2,1)S(1)} %copy-done.40), channel_id=1, source_target_pairs={{0,1},{1,0},{2,3},{3,2},{4,5},{5,4},{6,7},{7,6},{8,9},{9,8},{10,11... | collective-permute-start | bytes 2359304 | tf_op jit(solution)/shard_map/ppermute | solution.py:35
  148.6 19.6 %collective-permute-start.25 = (bf16[512,768]{1,0:T(8,128)(2,1)S(1)}, bf16[512,768]{1,0:T(8,128)(2,1)S(1)}, u32[]{:S(2)}, u32[]{:S(2)}) collective-permute-start(bf16[512,768]{1,0:T(8,128)(2,1)S(1)} %add_convert_fusion.1), channel_id=1, source_target_pairs={{0,2},{1,3},{2,0},{3,1},{4,6},{5,7},{6,4},{7,5},{8,10},{9,11},{10,... | collective-permute-start | bytes 2359304 | tf_op jit(solution)/shard_map/ppermute | solution.py:35
  162.1 18.4 %collective-permute-start.23 = (bf16[4,96,768]{2,1,0:T(8,128)(2,1)}, bf16[4,96,768]{2,1,0:T(8,128)(2,1)S(1)}, u32[]{:S(2)}, u32[]{:S(2)}) collective-permute-start(bf16[4,96,768]{2,1,0:T(8,128)(2,1)} %get-tuple-element.151), channel_id=1, source_target_pairs={{0,4},{4,0},{8,12},{12,8},{16,20},{20,16},{24,28},{28,24},{1,5},{5... | collective-permute-start | bytes 1769480 | tf_op jit(solution)/shard_map/ppermute | solution.py:35
  180.5 44.3 %collective-permute-start.34 = (bf16[512,768]{1,0:T(8,128)(2,1)S(1)}, bf16[512,768]{1,0:T(8,128)(2,1)S(1)}, u32[]{:S(2)}, u32[]{:S(2)}) collective-permute-start(bf16[512,768]{1,0:T(8,128)(2,1)S(1)} %add_convert_fusion), channel_id=1, source_target_pairs={{0,2},{1,3},{2,0},{3,1},{4,6},{5,7},{6,4},{7,5},{8,10},{9,11},{10,... | collective-permute-start | bytes 2359304 | tf_op jit(solution)/shard_map/ppermute | solution.py:35
  183.8 40.9 %collective-permute-start.22 = (bf16[4,96,768]{2,1,0:T(8,128)(2,1)S(1)}, bf16[4,96,768]{2,1,0:T(8,128)(2,1)S(1)}, u32[]{:S(2)}, u32[]{:S(2)}) collective-permute-start(bf16[4,96,768]{2,1,0:T(8,128)(2,1)S(1)} %copy-done.44), channel_id=1, source_target_pairs={{0,4},{4,0},{8,12},{12,8},{16,20},{20,16},{24,28},{28,24},{1,5},{5... | collective-permute-start | bytes 1769480 | tf_op jit(solution)/shard_map/ppermute | solution.py:35
  187.1 36.7 %collective-permute-start.31 = (bf16[192,768]{1,0:T(8,128)(2,1)}, bf16[192,768]{1,0:T(8,128)(2,1)S(1)}, u32[]{:S(2)}, u32[]{:S(2)}) collective-permute-start(bf16[192,768]{1,0:T(8,128)(2,1)} %get-tuple-element.175), channel_id=1, source_target_pairs={{0,2},{1,3},{2,0},{3,1},{4,6},{5,7},{6,4},{7,5},{8,10},{9,11},{10,... | collective-permute-start | bytes 884744 | tf_op jit(solution)/shard_map/ppermute | solution.py:35
  189.6 34.3 %collective-permute-start.32 = (bf16[192,768]{1,0:T(8,128)(2,1)S(1)}, bf16[192,768]{1,0:T(8,128)(2,1)S(1)}, u32[]{:S(2)}, u32[]{:S(2)}) collective-permute-start(bf16[192,768]{1,0:T(8,128)(2,1)S(1)} %copy-done.45), channel_id=1, source_target_pairs={{0,3},{1,2},{2,1},{3,0},{4,7},{5,6},{6,5},{7,4},{8,11},{9,10},{10,... | collective-permute-start | bytes 884744 | tf_op jit(solution)/shard_map/ppermute | solution.py:35
  191.5 33.2 %collective-permute-start.33 = (bf16[2,96,768]{2,1,0:T(8,128)(2,1)}, bf16[2,96,768]{2,1,0:T(8,128)(2,1)S(1)}, u32[]{:S(2)}, u32[]{:S(2)}) collective-permute-start(bf16[2,96,768]{2,1,0:T(8,128)(2,1)} %get-tuple-element.182), channel_id=1, source_target_pairs={{0,8},{4,12},{8,0},{12,4},{16,24},{20,28},{24,16},{28,20},{1,9},{5... | collective-permute-start | bytes 884744 | tf_op jit(solution)/shard_map/ppermute | solution.py:35
  240.7 26.8 %collective-permute-start.37 = (bf16[512,768]{1,0:T(8,128)(2,1)}, bf16[512,768]{1,0:T(8,128)(2,1)}, u32[]{:S(2)}, u32[]{:S(2)}) collective-permute-start(bf16[512,768]{1,0:T(8,128)(2,1)} %get-tuple-element.201), channel_id=1, source_target_pairs={{0,1},{1,0},{2,3},{3,2},{4,5},{5,4},{6,7},{7,6},{8,9},{9,8},{10,11... | collective-permute-start | bytes 2359304 | tf_op jit(solution)/shard_map/ppermute | solution.py:35
  250.8 21.4 %collective-permute-start.39 = (bf16[4,96,768]{2,1,0:T(8,128)(2,1)}, bf16[4,96,768]{2,1,0:T(8,128)(2,1)S(1)}, u32[]{:S(2)}, u32[]{:S(2)}) collective-permute-start(bf16[4,96,768]{2,1,0:T(8,128)(2,1)} %get-tuple-element.202), channel_id=1, source_target_pairs={{0,4},{4,0},{8,12},{12,8},{16,20},{20,16},{24,28},{28,24},{1,5},{5... | collective-permute-start | bytes 1769480 | tf_op jit(solution)/shard_map/ppermute | solution.py:35
  254.9 20.8 %collective-permute-start.47 = (bf16[1,96,768]{2,1,0:T(8,128)(2,1)}, bf16[1,96,768]{2,1,0:T(8,128)(2,1)S(1)}, u32[]{:S(2)}, u32[]{:S(2)}) collective-permute-start(bf16[1,96,768]{2,1,0:T(8,128)(2,1)} %get-tuple-element.216), channel_id=1, source_target_pairs={{0,16},{4,20},{8,24},{12,28},{16,0},{20,4},{24,8},{28,12},{1,17},{... | collective-permute-start | bytes 442376 | tf_op jit(solution)/shard_map/ppermute | solution.py:35
  260.0 30.0 %collective-permute-start.38 = (bf16[512,768]{1,0:T(8,128)(2,1)}, bf16[512,768]{1,0:T(8,128)(2,1)}, u32[]{:S(2)}, u32[]{:S(2)}) collective-permute-start(bf16[512,768]{1,0:T(8,128)(2,1)} %fusion), channel_id=1, source_target_pairs={{0,2},{1,3},{2,0},{3,1},{4,6},{5,7},{6,4},{7,5},{8,10},{9,11},{10,... | collective-permute-start | bytes 2359304 | tf_op jit(solution)/shard_map/ppermute | solution.py:35
  (76 other events, 681.4 us)
